TPU v7x, 32 devices: a whole 2x2x4 slice. The times are simulated.
32 devices in a mesh: row: 2 (over core), col: 4 (over z), depth: 4 (over y, x).
Axes of the slice: x: 2, y: 2, z: 4, core: 2. Of those that a mesh axis runs over, the one named last changes fastest.
Arguments:
- tokens: bfloat16 [768, 4096], P(('col', 'depth'), 'row'), may hold values from -6 to 6
- cotangent: bfloat16 [768, 4096], P(('col', 'depth'), 'row'), may hold values from -6 to 6
- gate_weight: bfloat16 [4096, 14336], P(('row', 'depth'), 'col'), may hold values from -0.09375 to 0.09375
- up_weight: bfloat16 [4096, 14336], P(('row', 'depth'), 'col'), may hold values from -0.09375 to 0.09375
- down_weight: bfloat16 [14336, 4096], P('col', ('row', 'depth')), may hold values from -0.046875 to 0.046875
Outputs:
- output: bfloat16 [768, 4096], P(('col', 'depth'), 'row')
- input_grad: bfloat16 [768, 4096], P(('col', 'depth'), 'row')
- gate_grad: float32 [4096, 14336], P(('row', 'depth'), 'col')
- up_grad: float32 [4096, 14336], P(('row', 'depth'), 'col')
- down_grad: float32 [14336, 4096], P('col', ('row', 'depth'))
All inputs are finite; a program needn't handle non-finite values.
Results may differ from a plain program's by a relative error of at most 0.0049.
Values may be sent and summed in bfloat16 or wider, within the bound.
No kernel may reach another device: no remote copies, remote signals or barrier semaphores. Data moves between devices by JAX's collectives and lax.ppermute only.
A program may use at most 192 MiB of HBM per device.

v0:
```python
import jax
import jax.numpy as jnp
from jax import lax
from jax.sharding import PartitionSpec as P


def dot_tn(left, right):
    return lax.dot_general(
        left, right, (((0,), (0,)), ((), ())), preferred_element_type=jnp.float32
    )


def dot_nt(left, right):
    return lax.dot_general(
        left, right, (((1,), (1,)), ((), ())), preferred_element_type=jnp.float32
    )


def deltas(hidden_grad, gate, up):
    sig = jax.nn.sigmoid(gate)
    gate_delta = (hidden_grad * up * sig * (1.0 + gate * (1.0 - sig))).astype(jnp.bfloat16)
    up_delta = (hidden_grad * gate * sig).astype(jnp.bfloat16)
    return (gate_delta, up_delta)


def activate(gate, up):
    return (gate * jax.nn.sigmoid(gate) * up).astype(jnp.bfloat16)


def on_device(tokens, cotangent, gate_weight, up_weight, down_weight):
    gate_full, up_full = (
        lax.all_gather(gate_weight, "depth", axis=0, tiled=True),
        lax.all_gather(up_weight, "depth", axis=0, tiled=True),
    )
    down_full = lax.all_gather(down_weight, "depth", axis=1, tiled=True)
    tok_rows, cot_rows = (
        lax.all_gather(tokens, "col", axis=0, tiled=True),
        lax.all_gather(cotangent, "col", axis=0, tiled=True),
    )
    gate = lax.psum_scatter(
        jnp.dot(tok_rows, gate_full, preferred_element_type=jnp.float32),
        "row",
        scatter_dimension=0,
        tiled=True,
    )
    up = lax.psum_scatter(
        jnp.dot(tok_rows, up_full, preferred_element_type=jnp.float32),
        "row",
        scatter_dimension=0,
        tiled=True,
    )
    hid_rows = lax.all_gather(activate(gate, up), "row", axis=0, tiled=True)
    hidden_grad = lax.psum_scatter(
        dot_nt(cot_rows, down_full), "row", scatter_dimension=0, tiled=True
    )
    gate_delta, up_delta = deltas(hidden_grad, gate, up)
    gd_rows, ud_rows = (
        lax.all_gather(gate_delta, "row", axis=0, tiled=True),
        lax.all_gather(up_delta, "row", axis=0, tiled=True),
    )
    output = lax.psum_scatter(
        jnp.dot(hid_rows, down_full, preferred_element_type=jnp.float32),
        "col",
        scatter_dimension=0,
        tiled=True,
    ).astype(jnp.bfloat16)
    input_grad = lax.psum_scatter(
        dot_nt(gd_rows, gate_full) + dot_nt(ud_rows, up_full),
        "col",
        scatter_dimension=0,
        tiled=True,
    ).astype(jnp.bfloat16)
    tok_part, cot_part = (
        lax.all_to_all(tok_rows, "depth", split_axis=1, concat_axis=0, tiled=True),
        lax.all_to_all(cot_rows, "depth", split_axis=1, concat_axis=0, tiled=True),
    )
    gd_all, ud_all, hid_all = (
        lax.all_gather(gd_rows, "depth", axis=0, tiled=True),
        lax.all_gather(ud_rows, "depth", axis=0, tiled=True),
        lax.all_gather(hid_rows, "depth", axis=0, tiled=True),
    )
    gate_grad = dot_tn(tok_part, gd_all)
    up_grad = dot_tn(tok_part, ud_all)
    down_grad = dot_tn(hid_all, cot_part)
    return (output, input_grad, gate_grad, up_grad, down_grad)


def solution(mesh):
    return jax.shard_map(
        on_device,
        mesh=mesh,
        in_specs=(
            P(("col", "depth"), "row"),
            P(("col", "depth"), "row"),
            P(("row", "depth"), "col"),
            P(("row", "depth"), "col"),
            P("col", ("row", "depth")),
        ),
        out_specs=(
            P(("col", "depth"), "row"),
            P(("col", "depth"), "row"),
            P(("row", "depth"), "col"),
            P(("row", "depth"), "col"),
            P("col", ("row", "depth")),
        ),
        check_vma=False,
    )
```

profile of v0, /device:TPU:0, one launch (start us, length us, event | category | flops | bytes accessed | tf_op | source)
XLA Modules:
  0.0 807.5 jit_solution(1116714497966719239)
XLA Ops:
  9.6 21.3 %all_gather.33 = bf16[192,2048]{1,0:T(8,128)(2,1)S(1)} all-gather(bf16[48,2048]{1,0:T(8,128)(2,1)S(1)} %copy-done), channel_id=1, replica_groups=mesh['row'=2,'col'=4,'depth'=4] {'col'}, dimensions={0}, use_global_device_ids=true | all-gather | bytes 983040 | tf_op jit(solution)/shard_map/all_gather | solution.py:37
  30.9 121.7 %all-gather.10.cloned.1.call-done = bf16[2048,3584]{1,0:T(8,128)(2,1)} async-done(((bf16[512,3584]{1,0:T(8,128)(2,1)}), bf16[2048,3584]{1,0:T(8,128)(2,1)}) %all-gather.10.cloned.1.call-update) | async-done | bytes 14680080 | tf_op jit(solution)/shard_map/all_gather | solution.py:32
  152.5 9.8 %fusion = f32[192,3584]{1,0:T(8,128)} fusion(bf16[192,2048]{1,0:T(8,128)(2,1)S(1)} %all_gather.33, bf16[2048,3584]{1,0:T(8,128)(2,1)} %all-gather.10.cloned.1.call-done), kind=kOutput, calls=%fused_computation.9 | convolution fusion | flops 2818572288 | bytes 18219008 | tf_op jit(solution)/shard_map/dot_general | solution.py:41
  162.4 132.0 %all-gather.12.cloned.1.call-done = bf16[2048,3584]{1,0:T(8,128)(2,1)} async-done(((bf16[512,3584]{1,0:T(8,128)(2,1)}), bf16[2048,3584]{1,0:T(8,128)(2,1)}) %all-gather.12.cloned.1.call-update) | async-done | bytes 14680080 | tf_op jit(solution)/shard_map/all_gather | solution.py:33
  294.4 9.8 %fusion.1 = f32[192,3584]{1,0:T(8,128)} fusion(bf16[192,2048]{1,0:T(8,128)(2,1)S(1)} %all_gather.33, bf16[2048,3584]{1,0:T(8,128)(2,1)} %all-gather.12.cloned.1.call-done), kind=kOutput, calls=%fused_computation.10 | convolution fusion | flops 2818572288 | bytes 18219008 | tf_op jit(solution)/shard_map/dot_general | solution.py:47
  305.2 19.5 %all_gather.38 = bf16[192,2048]{1,0:T(8,128)(2,1)S(1)} all-gather(bf16[48,2048]{1,0:T(8,128)(2,1)S(1)} %copy-done.1), channel_id=1, replica_groups=mesh['row'=2,'col'=4,'depth'=4] {'col'}, dimensions={0}, use_global_device_ids=true | all-gather | bytes 983040 | tf_op jit(solution)/shard_map/all_gather | solution.py:38
  324.7 111.3 %all-gather.16.cloned.1.call-done = bf16[3584,2048]{1,0:T(8,128)(2,1)} async-done(((bf16[3584,512]{1,0:T(8,128)(2,1)}), bf16[3584,2048]{1,0:T(8,128)(2,1)}) %all-gather.16.cloned.1.call-update) | async-done | bytes 14680080 | tf_op jit(solution)/shard_map/all_gather | solution.py:35
  436.1 11.7 %fusion.3 = f32[192,3584]{1,0:T(8,128)} fusion(bf16[192,2048]{1,0:T(8,128)(2,1)S(1)} %all_gather.38, bf16[3584,2048]{1,0:T(8,128)(2,1)} %all-gather.16.cloned.1.call-done), kind=kOutput, calls=%fused_computation.12 | convolution fusion | flops 2818572288 | bytes 18219008 | tf_op jit(solution)/shard_map/dot_general | solution.py:14
  447.8 1.3 reduce-scatter.6.cloned.1.call-done
  449.1 14.3 %reduce-scatter.8.cloned.1.call-done = f32[96,3584]{1,0:T(8,128)} async-done(((f32[192,3584]{1,0:T(8,128)}), f32[96,3584]{1,0:T(8,128)}) %reduce-scatter.8.cloned.1.call-update) | async-done | bytes 1376272 | tf_op jit(solution)/shard_map/reduce_scatter | solution.py:46
  463.5 14.3 %reduce-scatter.12.cloned.1.call-done = f32[96,3584]{1,0:T(8,128)} async-done(((f32[192,3584]{1,0:T(8,128)}), f32[96,3584]{1,0:T(8,128)}) %reduce-scatter.12.cloned.1.call-update) | async-done | bytes 1376272 | tf_op jit(solution)/shard_map/reduce_scatter | solution.py:53
  477.8 4.2 multiply_convert_fusion
  483.7 9.2 %all-gather.18.cloned.1.call-done = bf16[192,3584]{1,0:T(8,128)(2,1)} async-done(((bf16[96,3584]{1,0:T(8,128)(2,1)}), bf16[192,3584]{1,0:T(8,128)(2,1)}) %all-gather.18.cloned.1.call-update) | async-done | bytes 1376272 | tf_op jit(solution)/shard_map/all_gather | solution.py:58
  492.9 8.5 %fusion.4 = f32[192,2048]{1,0:T(8,128)S(1)} fusion(bf16[192,3584]{1,0:T(8,128)(2,1)} %all-gather.18.cloned.1.call-done, bf16[2048,3584]{1,0:T(8,128)(2,1)} %all-gather.10.cloned.1.call-done), kind=kOutput, calls=%fused_computation.13 | convolution fusion | flops 2818572288 | bytes 17629184 | tf_op jit(solution)/shard_map/dot_general | solution.py:14
  501.4 4.5 all-gather.20.cloned.1.call-done
  505.9 11.6 %convolution_add_fusion = f32[192,2048]{1,0:T(8,128)} fusion(f32[192,2048]{1,0:T(8,128)S(1)} %fusion.4, bf16[192,3584]{1,0:T(8,128)(2,1)} %all-gather.20.cloned.1.call-done, bf16[2048,3584]{1,0:T(8,128)(2,1)} %all-gather.12.cloned.1.call-done), kind=kOutput, calls=%fused_computation.2 | convolution fusion | flops 2818965504 | bytes 19202048 | tf_op jit(solution)/shard_map/dot_general | solution.py:14
  517.6 1.2 all-gather.14.cloned.1.call-done
  518.8 9.8 %fusion.2 = f32[192,2048]{1,0:T(8,128)} fusion(bf16[192,3584]{1,0:T(8,128)(2,1)} %all-gather.14.cloned.1.call-done, bf16[3584,2048]{1,0:T(8,128)(2,1)} %all-gather.16.cloned.1.call-done), kind=kOutput, calls=%fused_computation.11 | convolution fusion | flops 2818572288 | bytes 17629184 | tf_op jit(solution)/shard_map/dot_general | solution.py:62
  531.5 3.9 all-to-all-start
  536.3 21.8 %reduce-scatter.14.cloned.1.call-done = f32[48,2048]{1,0:T(8,128)} async-done(((f32[192,2048]{1,0:T(8,128)}), f32[48,2048]{1,0:T(8,128)}) %reduce-scatter.14.cloned.1.call-update) | async-done | bytes 393232 | tf_op jit(solution)/shard_map/reduce_scatter | solution.py:67
  558.1 1.7 convert_element_type.19
  559.8 35.6 %reduce-scatter.10.cloned.1.call-done = f32[48,2048]{1,0:T(8,128)} async-done(((f32[192,2048]{1,0:T(8,128)}), f32[48,2048]{1,0:T(8,128)}) %reduce-scatter.10.cloned.1.call-update) | async-done | bytes 393232 | tf_op jit(solution)/shard_map/reduce_scatter | solution.py:61
  595.4 1.7 convert_element_type.16
  597.1 3.7 all-to-all-start.1
  600.8 61.3 %all-gather.22.cloned.1.call-done = bf16[768,3584]{1,0:T(8,128)(2,1)} async-done(((bf16[192,3584]{1,0:T(8,128)(2,1)}), bf16[768,3584]{1,0:T(8,128)(2,1)}) %all-gather.22.cloned.1.call-update) | async-done | bytes 5505040 | tf_op jit(solution)/shard_map/all_gather | solution.py:78
  662.1 7.7 convolution_bitcast_fusion.1
  669.8 8.8 %copy.20 = f32[512,3584]{1,0:T(8,128)} copy(f32[512,3584]{0,1:T(8,128)} %convolution_bitcast_fusion.1) | data formatting | bytes 14680064
  678.6 49.2 %all-gather.24.cloned.1.call-done = bf16[768,3584]{1,0:T(8,128)(2,1)} async-done(((bf16[192,3584]{1,0:T(8,128)(2,1)}), bf16[768,3584]{1,0:T(8,128)(2,1)}) %all-gather.24.cloned.1.call-update) | async-done | bytes 5505040 | tf_op jit(solution)/shard_map/all_gather | solution.py:79
  727.8 7.7 convolution_bitcast_fusion
  735.4 8.7 %copy.21 = f32[512,3584]{1,0:T(8,128)} copy(f32[512,3584]{0,1:T(8,128)} %convolution_bitcast_fusion) | data formatting | bytes 14680064
  744.2 49.1 %all-gather.26.cloned.1.call-done = bf16[768,3584]{1,0:T(8,128)(2,1)} async-done(((bf16[192,3584]{1,0:T(8,128)(2,1)}), bf16[768,3584]{1,0:T(8,128)(2,1)}) %all-gather.26.cloned.1.call-update) | async-done | bytes 5505040 | tf_op jit(solution)/shard_map/all_gather | solution.py:80
  793.2 7.7 fusion.5
  (36 shorter events, 9.0 us)
Async XLA Ops:
  7.2 145.4 %all-gather.10.cloned.1.call-start = ((), (), s32[]{:S(2)}) async-start(), calls=%async_computation.7 | async-start | bytes 18350080 | tf_op jit(solution)/shard_map/all_gather | solution.py:32
  7.9 286.5 %all-gather.12.cloned.1.call-start = ((), (), s32[]{:S(2)}) async-start(), calls=%async_computation.9 | async-start | bytes 18350080 | tf_op jit(solution)/shard_map/all_gather | solution.py:33
  8.6 0.9 copy-start
  8.7 427.4 %all-gather.16.cloned.1.call-start = ((), (), s32[]{:S(2)}) async-start(), calls=%async_computation.12 | async-start | bytes 18350080 | tf_op jit(solution)/shard_map/all_gather | solution.py:35
  9.4 439.7 %reduce-scatter.6.cloned.1.call-start = ((), (), s32[]{:S(2)}) async-start(), calls=%async_computation.8 | async-start | bytes 4128768 | tf_op jit(solution)/shard_map/reduce_scatter | solution.py:40
  162.4 301.1 %reduce-scatter.8.cloned.1.call-start = ((), (), s32[]{:S(2)}) async-start(), calls=%async_computation.10 | async-start | bytes 4128768 | tf_op jit(solution)/shard_map/reduce_scatter | solution.py:46
  304.2 1.0 copy-start.1
  304.2 173.5 %reduce-scatter.12.cloned.1.call-start = ((), (), s32[]{:S(2)}) async-start(), calls=%async_computation.14 | async-start | bytes 4128768 | tf_op jit(solution)/shard_map/reduce_scatter | solution.py:53
  447.8 45.2 %all-gather.18.cloned.1.call-start = ((), (), s32[]{:S(2)}) async-start(), calls=%async_computation.15 | async-start | bytes 2064384 | tf_op jit(solution)/shard_map/all_gather | solution.py:58
  482.0 23.9 %all-gather.20.cloned.1.call-start = ((), (), s32[]{:S(2)}) async-start(), calls=%async_computation.16 | async-start | bytes 2064384 | tf_op jit(solution)/shard_map/all_gather | solution.py:59
  482.8 36.1 %all-gather.14.cloned.1.call-start = ((), (), s32[]{:S(2)}) async-start(), calls=%async_computation.11 | async-start | bytes 2064384 | tf_op jit(solution)/shard_map/all_gather | solution.py:52
  483.5 74.6 %reduce-scatter.14.cloned.1.call-start = ((), (), s32[]{:S(2)}) async-start(), calls=%async_computation.17 | async-start | bytes 1966080 | tf_op jit(solution)/shard_map/reduce_scatter | solution.py:67
  517.6 77.9 %reduce-scatter.10.cloned.1.call-start = ((), (), s32[]{:S(2)}) async-start(), calls=%async_computation.13 | async-start | bytes 1966080 | tf_op jit(solution)/shard_map/reduce_scatter | solution.py:61
  528.6 133.5 %all-gather.22.cloned.1.call-start = ((), (), s32[]{:S(2)}) async-start(), calls=%async_computation.18 | async-start | bytes 6881280 | tf_op jit(solution)/shard_map/all_gather | solution.py:78
  529.2 198.6 %all-gather.24.cloned.1.call-start = ((), (), s32[]{:S(2)}) async-start(), calls=%async_computation.19 | async-start | bytes 6881280 | tf_op jit(solution)/shard_map/all_gather | solution.py:79
  529.9 263.3 %all-gather.26.cloned.1.call-start = ((), (), s32[]{:S(2)}) async-start(), calls=%async_computation.20 | async-start | bytes 6881280 | tf_op jit(solution)/shard_map/all_gather | solution.py:80
  531.5 65.6 %all-to-all-start = ((bf16[192,4,512]{2,0,1:T(8,128)(2,1)}), bf16[192,4,512]{2,0,1:T(8,128)(2,1)S(1)}, u32[]{:S(2)}, u32[]{:S(2)}) async-start(bf16[192,4,512]{2,0,1:T(8,128)(2,1)} %bitcast.35), calls=%async_computation.5 | async-start | bytes 1572864 | tf_op jit(solution)/shard_map/all_to_all | solution.py:74
  597.1 147.1 %all-to-all-start.1 = ((bf16[192,4,512]{2,0,1:T(8,128)(2,1)}), bf16[192,4,512]{2,0,1:T(8,128)(2,1)S(1)}, u32[]{:S(2)}, u32[]{:S(2)}) async-start(bf16[192,4,512]{2,0,1:T(8,128)(2,1)} %bitcast.34), calls=%async_computation.6 | async-start | bytes 1572864 | tf_op jit(solution)/shard_map/all_to_all | solution.py:75
Sparse Core Ops, SparseCore 0:
  9.8 142.6 all-gather.9
  154.4 139.9 all-gather.11
  296.2 139.8 all-gather.15
  438.8 10.3 reduce-scatter.5
  451.9 11.5 reduce-scatter.7
  466.1 11.5 reduce-scatter.11
  482.1 10.7 all-gather.17
  495.1 10.7 all-gather.19
  508.1 10.6 all-gather.13
  521.7 36.4 reduce-scatter.13
  561.1 34.2 reduce-scatter.9
  597.3 64.8 all-gather.21
  664.1 63.6 all-gather.23
  729.6 63.6 all-gather.25
where the time goes:
time: 808 us; the launch traced here: 807 us
  waiting for transfers between devices  632 us (78%)
  matrix products  84.2 us (10%)
  blocking collectives  40.8 us (5%)
  local copies, waits for them, and re-layouts  20.5 us (3%)
  between operations  14 us (2%)
  starting transfers between devices  8.36 us (1%)
    all_gather x1, waiting for transfers between devices, on_device(): lax.all_gather(up_weight, 'depth', axis=0, tiled=True)  132 us
    all_gather x1, waiting for transfers between devices, on_device(): lax.all_gather(gate_weight, 'depth', axis=0, tiled=True)  122 us
    all_gather x1, waiting for transfers between devices, on_device(): down_full = lax.all_gather(down_weight, 'depth', axis=1, tiled=True)  111 us
    all_gather x1, waiting for transfers between devices, on_device(): lax.all_gather(gd_rows, 'depth', axis=0, tiled=True)  61.3 us
    all_gather x1, waiting for transfers between devices, on_device(): lax.all_gather(ud_rows, 'depth', axis=0, tiled=True)  49.2 us
    all_gather x1, waiting for transfers between devices, on_device(): lax.all_gather(hid_rows, 'depth', axis=0, tiled=True)  49.1 us
    reduce_scatter x1, waiting for transfers between devices, on_device(): lax.psum_scatter(jnp.dot(hid_rows, down_full, preferred_element_type=jnp....  35.6 us
    dot_general x3, matrix products, dot_nt(): lax.dot_general(left, right, (((1,), (1,)), ((), ())), preferred_element_...  31.8 us
  transfers between devices with their start and end apart: 16, of which 14 were waited for; matrix products, arithmetic and copies ran while one was open for 12% of the time, Pallas kernels for 0%

commit v1 on v0

v1 whole, which is shorter than its diff:
```python
import jax
import jax.numpy as jnp
from jax import lax
from jax.sharding import PartitionSpec as P

F32, BF16 = jnp.float32, jnp.bfloat16


def dot_nn(left, right):
    return jnp.dot(left, right, preferred_element_type=F32)


def dot_tn(left, right):
    return lax.dot_general(left, right, (((0,), (0,)), ((), ())), preferred_element_type=F32)


def dot_nt(left, right):
    return lax.dot_general(left, right, (((1,), (1,)), ((), ())), preferred_element_type=F32)


def deltas(hidden_grad, gate, up):
    sig = jax.nn.sigmoid(gate)
    gate_delta = (hidden_grad * up * sig * (1.0 + gate * (1.0 - sig))).astype(BF16)
    up_delta = (hidden_grad * gate * sig).astype(BF16)
    return gate_delta, up_delta


def activate(gate, up):
    return (gate * jax.nn.sigmoid(gate) * up).astype(BF16)


def make_on_device(mesh):
    n_row, n_col, n_depth = (mesh.shape[a] for a in ("row", "col", "depth"))
    assert n_depth == 4 and n_col % (2 * n_row) == 0

    def swap(x, axis, k):
        n = mesh.shape[axis]
        return lax.ppermute(x, axis, [(i, i ^ k) for i in range(n)])

    def on_device(tokens, cotangent, gate_weight, up_weight, down_weight):
        n, _ = tokens.shape
        feats = gate_weight.shape[0]
        r, d = lax.axis_index("row"), lax.axis_index("depth")
        js = n_col // n_row
        half = js // 2 * n

        gws = [gate_weight] + [swap(gate_weight, "row", i) for i in range(1, n_row)]
        uws = [up_weight] + [swap(up_weight, "row", i) for i in range(1, n_row)]
        dws = [down_weight] + [swap(down_weight, "row", i) for i in range(1, n_row)]

        def gather(x):
            blocks = []
            for k in range(n_depth):
                piece = lax.dynamic_slice(x, (0, (d ^ k) * feats), (n, feats))
                blocks.append(swap(piece, "depth", k) if k else piece)
            own = jnp.stack(blocks)
            cols = jnp.stack([own] + [swap(own, "col", j) for j in range(1, n_col)])
            cols = cols.reshape(n_row, 2, js // 2, n_depth, n, feats)
            cols = cols.transpose(0, 1, 3, 2, 4, 5).reshape(n_row, 2, n_depth, half, feats)
            order = [(0, 0), (1, 0), (0, 2), (1, 1), (0, 1), (0, 3), (1, 2), (1, 3)]
            return jnp.concatenate([cols[:, a, k] for a, k in order], axis=1)

        def spread(x):
            by_dist = [lax.dynamic_index_in_dim(x, r ^ i, 0, keepdims=False) for i in range(n_row)]
            shares = [by_dist[0]] + [swap(by_dist[i], "row", i) for i in range(1, n_row)]
            return shares, jnp.concatenate(by_dist, axis=0)

        tok_shares, tok_all = spread(gather(tokens))
        cot_shares, cot_all = spread(gather(cotangent))
        rows = half * 8

        def reduce_depth(shares, weights, dot):
            def part(lo, hi):
                total = dot(shares[0][lo:hi], weights[0])
                for s, w in zip(shares[1:], weights[1:]):
                    total = total + dot(s[lo:hi], w)
                return total

            sent = part(4 * half, 8 * half).astype(BF16)
            from_x = swap(sent[: 2 * half], "depth", 1)
            from_y = swap(sent[2 * half :], "depth", 2)
            keep = part(0, 4 * half)
            a2 = (keep[2 * half : 3 * half] + from_x[half:].astype(F32)).astype(BF16)
            b1 = (keep[3 * half :] + from_y[half:].astype(F32)).astype(BF16)
            last_y, last_x = swap(a2, "depth", 2), swap(b1, "depth", 1)
            a0 = keep[:half] + from_x[:half].astype(F32) + last_y.astype(F32)
            b0 = keep[half : 2 * half] + from_y[:half].astype(F32) + last_x.astype(F32)
            return jnp.concatenate([a0, b0], axis=0)

        def gather_depth(x):
            a0, b0 = x[:half], x[half:]
            a2, b1 = swap(a0, "depth", 2), swap(b0, "depth", 1)
            a13 = swap(jnp.concatenate([a0, a2]), "depth", 1)
            b23 = swap(jnp.concatenate([b0, b1]), "depth", 2)
            share = jnp.concatenate([x, a2, b1, a13, b23])
            return jnp.concatenate([share] + [swap(share, "row", i) for i in range(1, n_row)])

        def scatter(partial):
            by_dist = partial.reshape(n_row, rows, feats)
            mine = None
            for j in range(n_col):
                h, a, jj = j // js, (j % js) // (js // 2), j % (js // 2)
                share = lax.dynamic_index_in_dim(by_dist, r ^ h, 0, keepdims=False)
                share = share.reshape(8, js // 2, n, feats)[:, jj]
                picks = (0, 4, 2, 5) if a == 0 else (1, 3, 6, 7)
                piece = jnp.stack([share[p] for p in picks])
                piece = swap(piece, "col", j) if j else piece
                mine = piece if mine is None else mine + piece
            mine = mine.astype(BF16)
            out = jnp.zeros((n, feats * n_depth), BF16)
            for k in range(n_depth):
                piece = swap(mine[k], "depth", k) if k else mine[k]
                out = lax.dynamic_update_slice(out, piece, (0, (d ^ k) * feats))
            return out

        gate = reduce_depth(tok_shares, gws, dot_nn)
        up = reduce_depth(tok_shares, uws, dot_nn)
        hid_all = gather_depth(activate(gate, up))
        hidden_grad = reduce_depth(cot_shares, dws, dot_nt)
        gate_delta, up_delta = deltas(hidden_grad, gate, up)
        output = scatter(dot_nn(hid_all, down_weight))
        gd_all, ud_all = gather_depth(gate_delta), gather_depth(up_delta)
        down_grad = dot_tn(hid_all, cot_all)
        gate_grad = dot_tn(tok_all, gd_all)
        input_grad = scatter(dot_nt(gd_all, gate_weight) + dot_nt(ud_all, up_weight))
        up_grad = dot_tn(tok_all, ud_all)
        return output, input_grad, gate_grad, up_grad, down_grad

    return on_device


def solution(mesh):
    act = P(("col", "depth"), "row")
    wide = P(("row", "depth"), "col")
    tall = P("col", ("row", "depth"))
    return jax.shard_map(
        make_on_device(mesh),
        mesh=mesh,
        in_specs=(act, act, wide, wide, tall),
        out_specs=(act, act, wide, wide, tall),
        check_vma=False,
    )
```

time: 808 us -> 308 us (0.38)
  waiting for transfers between devices: 632 us -> 155 us
  starting transfers between devices: 8.36 us -> 86.7 us
  matrix products: 84.2 us -> 37 us
  blocking collectives: 40.8 us -> 0 us
  between operations: 14 us -> 1.5 us
    all_gather x9 -> x0, waiting for transfers between devices: 539 us -> none  [the longest x1 132 us: on_device(): lax.all_gather(up_weight, 'depth', axis=0, tiled=True)]
    ppermute x0 -> x56, waiting for transfers between devices: none -> 155 us  [swap(): return lax.ppermute(x, axis, [(i, i ^ k) for i in range(n)])]
    reduce_scatter x5 -> x0, waiting for transfers between devices: 87.3 us -> none  [the longest x1 35.6 us: on_device(): lax.psum_scatter(jnp.dot(hid_rows, down_full, preferred_element_type=jnp....]
    ppermute x0 -> x56, starting transfers between devices: none -> 86.7 us  [swap(): return lax.ppermute(x, axis, [(i, i ^ k) for i in range(n)])]
    all_gather x2 -> x0, blocking collectives: 40.8 us -> none  [the longest x1 21.3 us: on_device(): lax.all_gather(tokens, 'col', axis=0, tiled=True)]
    dot_general x3 -> x6, matrix products: 31.8 us -> 11.4 us  [dot_nt(): lax.dot_general(left, right, (((1,), (1,)), ((), ())), preferred_element_...]
    dot_general x3 -> x9, matrix products: 29.4 us -> 10.1 us  [dot_nn(): return jnp.dot(left, right, preferred_element_type=F32)]
    unnamed x6 -> x56, local copies, waits for them, and re-layouts: 18.6 us -> 7.52 us
  transfers between devices with their start and end apart: 16 -> 56, of which waited for: 14 -> 24; matrix products, arithmetic and copies ran while one was open for 12% -> 17% of each run, Pallas kernels for 0% -> 0%
where the time goes in v1:
time: 308 us
  waiting for transfers between devices  155 us (50%)
  starting transfers between devices  86.7 us (28%)
  matrix products  37 us (12%)
  local copies, waits for them, and re-layouts  15.4 us (5%)
  other arithmetic  12.3 us (4%)
    ppermute x56, waiting for transfers between devices, swap(): return lax.ppermute(x, axis, [(i, i ^ k) for i in range(n)])  155 us
    ppermute x56, starting transfers between devices, swap(): return lax.ppermute(x, axis, [(i, i ^ k) for i in range(n)])  86.7 us
    dot_general x3, matrix products, dot_tn(): lax.dot_general(left, right, (((0,), (0,)), ((), ())), preferred_element_...  15.5 us
    dot_general x6, matrix products, dot_nt(): lax.dot_general(left, right, (((1,), (1,)), ((), ())), preferred_element_...  11.4 us
    dot_general x9, matrix products, dot_nn(): return jnp.dot(left, right, preferred_element_type=F32)  10.1 us
    unnamed x56, local copies, waits for them, and re-layouts  7.52 us
  transfers between devices with their start and end apart: 56, of which 24 were waited for; matrix products, arithmetic and copies ran while one was open for 17% of the time, Pallas kernels for 0%

profile of v1, /device:TPU:0, one launch (start us, length us, event | category | flops | bytes accessed | tf_op | source)
XLA Modules:
  0.0 307.7 jit_solution(17968586424323349452)
XLA Ops:
  1.6 4.0 %collective-permute-start.2 = (bf16[48,512]{1,0:T(8,128)(2,1)S(1)}, bf16[48,512]{1,0:T(8,128)(2,1)S(1)}, u32[]{:S(2)}, u32[]{:S(2)}) collective-permute-start(bf16[48,512]{1,0:T(8,128)(2,1)S(1)} %get-tuple-element.109), channel_id=1, source_target_pairs={{0,3},{1,2},{2,1},{3,0},{4,7},{5,6},{6,5},{7,4},{8,11},{9,10},{10,... | collective-permute-start | bytes 147464 | tf_op jit(solution)/shard_map/ppermute | solution.py:38
  7.0 2.9 collective-permute-start.30
  10.3 3.7 %collective-permute-start.5 = (bf16[4,48,512]{2,1,0:T(8,128)(2,1)S(1)}, bf16[4,48,512]{2,1,0:T(8,128)(2,1)S(1)}, u32[]{:S(2)}, u32[]{:S(2)}) collective-permute-start(bf16[4,48,512]{2,1,0:T(8,128)(2,1)S(1)} %get-tuple-element.106), channel_id=1, source_target_pairs={{0,12},{4,8},{8,4},{12,0},{1,13},{5,9},{9,5},{13,1},{2,14},{6,10},... | collective-permute-start | bytes 589832 | tf_op jit(solution)/shard_map/ppermute | solution.py:38
  20.3 3.7 %collective-permute-start.33 = (bf16[4,48,512]{2,1,0:T(8,128)(2,1)S(1)}, bf16[4,48,512]{2,1,0:T(8,128)(2,1)S(1)}, u32[]{:S(2)}, u32[]{:S(2)}) collective-permute-start(bf16[4,48,512]{2,1,0:T(8,128)(2,1)S(1)} %get-tuple-element.97), channel_id=1, source_target_pairs={{0,12},{4,8},{8,4},{12,0},{1,13},{5,9},{9,5},{13,1},{2,14},{6,10},... | collective-permute-start | bytes 589832 | tf_op jit(solution)/shard_map/ppermute | solution.py:38
  23.9 10.5 %collective-permute-done.4 = bf16[4,48,512]{2,1,0:T(8,128)(2,1)S(1)} collective-permute-done((bf16[4,48,512]{2,1,0:T(8,128)(2,1)S(1)}, bf16[4,48,512]{2,1,0:T(8,128)(2,1)S(1)}, u32[]{:S(2)}, u32[]{:S(2)}) %collective-permute-start.4) | collective-permute-done | bytes 196640 | tf_op jit(solution)/shard_map/ppermute | solution.py:38
  34.5 6.4 %collective-permute-start.31 = (bf16[4,48,512]{2,1,0:T(8,128)(2,1)S(1)}, bf16[4,48,512]{2,1,0:T(8,128)(2,1)S(1)}, u32[]{:S(2)}, u32[]{:S(2)}) collective-permute-start(bf16[4,48,512]{2,1,0:T(8,128)(2,1)S(1)} %get-tuple-element.97), channel_id=1, source_target_pairs={{0,4},{4,0},{8,12},{12,8},{1,5},{5,1},{9,13},{13,9},{2,6},{6,2},{1... | collective-permute-start | bytes 589832 | tf_op jit(solution)/shard_map/ppermute | solution.py:38
  41.3 4.9 %collective-permute-done.32 = bf16[4,48,512]{2,1,0:T(8,128)(2,1)S(1)} collective-permute-done((bf16[4,48,512]{2,1,0:T(8,128)(2,1)S(1)}, bf16[4,48,512]{2,1,0:T(8,128)(2,1)S(1)}, u32[]{:S(2)}, u32[]{:S(2)}) %collective-permute-start.32) | collective-permute-done | bytes 196640 | tf_op jit(solution)/shard_map/ppermute | solution.py:38
  69.3 6.3 %collective-permute-done.8 = bf16[96,3584]{1,0:T(8,128)(2,1)} collective-permute-done((bf16[96,3584]{1,0:T(8,128)(2,1)}, bf16[96,3584]{1,0:T(8,128)(2,1)}, u32[]{:S(2)}, u32[]{:S(2)}) %collective-permute-start.8) | collective-permute-done | bytes 688160 | tf_op jit(solution)/shard_map/ppermute | solution.py:38
  78.0 12.3 %collective-permute-done.13 = bf16[96,3584]{1,0:T(8,128)(2,1)} collective-permute-done((bf16[96,3584]{1,0:T(8,128)(2,1)}, bf16[96,3584]{1,0:T(8,128)(2,1)}, u32[]{:S(2)}, u32[]{:S(2)}) %collective-permute-start.13) | collective-permute-done | bytes 688160 | tf_op jit(solution)/shard_map/ppermute | solution.py:38
  92.8 11.8 %collective-permute-done.36 = bf16[96,3584]{1,0:T(8,128)(2,1)} collective-permute-done((bf16[96,3584]{1,0:T(8,128)(2,1)}, bf16[96,3584]{1,0:T(8,128)(2,1)}, u32[]{:S(2)}, u32[]{:S(2)}) %collective-permute-start.36) | collective-permute-done | bytes 688160 | tf_op jit(solution)/shard_map/ppermute | solution.py:38
  107.7 5.0 %collective-permute-done.9 = bf16[48,3584]{1,0:T(8,128)(2,1)S(1)} collective-permute-done((bf16[48,3584]{1,0:T(8,128)(2,1)S(1)}, bf16[48,3584]{1,0:T(8,128)(2,1)S(1)}, u32[]{:S(2)}, u32[]{:S(2)}) %collective-permute-start.9) | collective-permute-done | bytes 344096 | tf_op jit(solution)/shard_map/ppermute | solution.py:38
  115.6 4.6 %collective-permute-done.14 = bf16[48,3584]{1,0:T(8,128)(2,1)S(1)} collective-permute-done((bf16[48,3584]{1,0:T(8,128)(2,1)S(1)}, bf16[48,3584]{1,0:T(8,128)(2,1)S(1)}, u32[]{:S(2)}, u32[]{:S(2)}) %collective-permute-start.14) | collective-permute-done | bytes 344096 | tf_op jit(solution)/shard_map/ppermute | solution.py:38
  123.1 3.5 %collective-permute-done.37 = bf16[48,3584]{1,0:T(8,128)(2,1)S(1)} collective-permute-done((bf16[48,3584]{1,0:T(8,128)(2,1)S(1)}, bf16[48,3584]{1,0:T(8,128)(2,1)S(1)}, u32[]{:S(2)}, u32[]{:S(2)}) %collective-permute-start.37) | collective-permute-done | bytes 344096 | tf_op jit(solution)/shard_map/ppermute | solution.py:38
  131.5 5.8 %collective-permute-done.39 = bf16[48,3584]{1,0:T(8,128)(2,1)S(1)} collective-permute-done((bf16[48,3584]{1,0:T(8,128)(2,1)S(1)}, bf16[48,3584]{1,0:T(8,128)(2,1)S(1)}, u32[]{:S(2)}, u32[]{:S(2)}) %collective-permute-start.39) | collective-permute-done | bytes 344096 | tf_op jit(solution)/shard_map/ppermute | solution.py:38
  137.4 2.0 constant_dynamic-update-slice_fusion.31
  145.4 5.3 %collective-permute-done.45 = bf16[48,3584]{1,0:T(8,128)(2,1)S(1)} collective-permute-done((bf16[48,3584]{1,0:T(8,128)(2,1)S(1)}, bf16[48,3584]{1,0:T(8,128)(2,1)S(1)}, u32[]{:S(2)}, u32[]{:S(2)}) %collective-permute-start.45) | collective-permute-done | bytes 344096 | tf_op jit(solution)/shard_map/ppermute | solution.py:38
  153.6 4.5 %collective-permute-done.40 = bf16[48,3584]{1,0:T(8,128)(2,1)S(1)} collective-permute-done((bf16[48,3584]{1,0:T(8,128)(2,1)S(1)}, bf16[48,3584]{1,0:T(8,128)(2,1)S(1)}, u32[]{:S(2)}, u32[]{:S(2)}) %collective-permute-start.40) | collective-permute-done | bytes 344096 | tf_op jit(solution)/shard_map/ppermute | solution.py:38
  161.1 4.3 %collective-permute-done.17 = bf16[48,3584]{1,0:T(8,128)(2,1)S(1)} collective-permute-done((bf16[48,3584]{1,0:T(8,128)(2,1)S(1)}, bf16[48,3584]{1,0:T(8,128)(2,1)S(1)}, u32[]{:S(2)}, u32[]{:S(2)}) %collective-permute-start.17) | collective-permute-done | bytes 344096 | tf_op jit(solution)/shard_map/ppermute | solution.py:38
  170.1 26.3 %collective-permute-done.42 = bf16[96,3584]{1,0:T(8,128)(2,1)S(1)} collective-permute-done((bf16[96,3584]{1,0:T(8,128)(2,1)S(1)}, bf16[96,3584]{1,0:T(8,128)(2,1)S(1)}, u32[]{:S(2)}, u32[]{:S(2)}) %collective-permute-start.42) | collective-permute-done | bytes 688160 | tf_op jit(solution)/shard_map/ppermute | solution.py:38
  199.7 8.7 %collective-permute-done.19 = bf16[96,3584]{1,0:T(8,128)(2,1)S(1)} collective-permute-done((bf16[96,3584]{1,0:T(8,128)(2,1)S(1)}, bf16[96,3584]{1,0:T(8,128)(2,1)S(1)}, u32[]{:S(2)}, u32[]{:S(2)}) %collective-permute-start.19) | collective-permute-done | bytes 688160 | tf_op jit(solution)/shard_map/ppermute | solution.py:38
  208.8 2.3 copy-done.12
  211.3 5.2 %fusion.20 = f32[512,3584]{1,0:T(8,128)} fusion(bf16[768,3584]{1,0:T(8,128)(2,1)S(1)} %constant_dynamic-update-slice_fusion.32, bf16[384,512]{1,0:T(8,128)(2,1)S(1)} %get-tuple-element.62, bf16[384,512]{1,0:T(8,128)(2,1)S(1)} %get-tuple-element.61), kind=kOutput, calls=%fused_computation.55 | convolution fusion | flops 2820145152 | bytes 13631488 | tf_op jit(solution)/shard_map/dot_general | solution.py:14
  216.7 5.2 %fusion.19 = f32[512,3584]{1,0:T(8,128)} fusion(bf16[768,3584]{1,0:T(8,128)(2,1)S(1)} %constant_dynamic-update-slice_fusion.43, bf16[384,512]{1,0:T(8,128)(2,1)S(1)} %get-tuple-element.62, bf16[384,512]{1,0:T(8,128)(2,1)S(1)} %get-tuple-element.61), kind=kOutput, calls=%fused_computation.54 | convolution fusion | flops 2820145152 | bytes 13631488 | tf_op jit(solution)/shard_map/dot_general | solution.py:14
  221.8 3.0 fusion.59
  224.9 3.0 convolution_add_fusion.6
  228.1 3.0 fusion.58
  231.7 3.3 %collective-permute-start.24 = (f32[4,48,512]{2,1,0:T(8,128)S(1)}, f32[4,48,512]{2,1,0:T(8,128)S(1)}, u32[]{:S(2)}, u32[]{:S(2)}) collective-permute-start(f32[4,48,512]{2,1,0:T(8,128)S(1)} %pad_maximum_fusion.16), channel_id=1, source_target_pairs={{0,12},{4,8},{8,4},{12,0},{1,13},{5,9},{9,5},{13,1},{2,14},{6,10},... | collective-permute-start | bytes 1179656 | tf_op jit(solution)/shard_map/ppermute | solution.py:38
  236.3 3.3 %collective-permute-start.52 = (f32[4,48,512]{2,1,0:T(8,128)S(1)}, f32[4,48,512]{2,1,0:T(8,128)S(1)}, u32[]{:S(2)}, u32[]{:S(2)}) collective-permute-start(f32[4,48,512]{2,1,0:T(8,128)S(1)} %pad_maximum_fusion.19), channel_id=1, source_target_pairs={{0,12},{4,8},{8,4},{12,0},{1,13},{5,9},{9,5},{13,1},{2,14},{6,10},... | collective-permute-start | bytes 1179656 | tf_op jit(solution)/shard_map/ppermute | solution.py:38
  239.8 5.2 %fusion.3 = f32[3584,512]{1,0:T(8,128)} fusion(bf16[768,3584]{1,0:T(8,128)(2,1)S(1)} %constant_dynamic-update-slice_fusion.13, bf16[384,512]{1,0:T(8,128)(2,1)S(1)} %copy-done.5, bf16[384,512]{1,0:T(8,128)(2,1)S(1)} %copy-done.3), kind=kOutput, calls=%fused_computation.20 | convolution fusion | flops 2820145152 | bytes 13631488 | tf_op jit(solution)/shard_map/dot_general | solution.py:14
  245.7 17.4 %collective-permute-start.50 = (f32[4,48,512]{2,1,0:T(8,128)S(1)}, f32[4,48,512]{2,1,0:T(8,128)S(1)}, u32[]{:S(2)}, u32[]{:S(2)}) collective-permute-start(f32[4,48,512]{2,1,0:T(8,128)S(1)} %pad_maximum_fusion.17), channel_id=1, source_target_pairs={{0,4},{4,0},{8,12},{12,8},{1,5},{5,1},{9,13},{13,9},{2,6},{6,2},{1... | collective-permute-start | bytes 1179656 | tf_op jit(solution)/shard_map/ppermute | solution.py:38
  263.1 21.9 %collective-permute-done.23 = f32[4,48,512]{2,1,0:T(8,128)S(1)} collective-permute-done((f32[4,48,512]{2,1,0:T(8,128)S(1)}, f32[4,48,512]{2,1,0:T(8,128)S(1)}, u32[]{:S(2)}, u32[]{:S(2)}) %collective-permute-start.23) | collective-permute-done | bytes 393248 | tf_op jit(solution)/shard_map/ppermute | solution.py:38
  288.8 10.9 %collective-permute-done.51 = f32[4,48,512]{2,1,0:T(8,128)S(1)} collective-permute-done((f32[4,48,512]{2,1,0:T(8,128)S(1)}, f32[4,48,512]{2,1,0:T(8,128)S(1)}, u32[]{:S(2)}, u32[]{:S(2)}) %collective-permute-start.51) | collective-permute-done | bytes 393248 | tf_op jit(solution)/shard_map/ppermute | solution.py:38
  (214 shorter events, 86.0 us)
Async XLA Ops:
  13.9 20.5 %collective-permute-start.4 = (bf16[4,48,512]{2,1,0:T(8,128)(2,1)S(1)}, bf16[4,48,512]{2,1,0:T(8,128)(2,1)S(1)}, u32[]{:S(2)}, u32[]{:S(2)}) collective-permute-start(bf16[4,48,512]{2,1,0:T(8,128)(2,1)S(1)} %get-tuple-element.106), channel_id=1, source_target_pairs={{0,8},{4,12},{8,0},{12,4},{1,9},{5,13},{9,1},{13,5},{2,10},{6,14},... | collective-permute-start | bytes 589832 | tf_op jit(solution)/shard_map/ppermute | solution.py:38
  14.0 20.5 %collective-permute-start.3 = (bf16[4,48,512]{2,1,0:T(8,128)(2,1)S(1)}, bf16[4,48,512]{2,1,0:T(8,128)(2,1)S(1)}, u32[]{:S(2)}, u32[]{:S(2)}) collective-permute-start(bf16[4,48,512]{2,1,0:T(8,128)(2,1)S(1)} %get-tuple-element.106), channel_id=1, source_target_pairs={{0,4},{4,0},{8,12},{12,8},{1,5},{5,1},{9,13},{13,9},{2,6},{6,2},{1... | collective-permute-start | bytes 589832 | tf_op jit(solution)/shard_map/ppermute | solution.py:38
  18.8 36.4 %collective-permute-start.7 = (bf16[512,3584]{1,0:T(8,128)(2,1)}, bf16[512,3584]{1,0:T(8,128)(2,1)S(1)}, u32[]{:S(2)}, u32[]{:S(2)}) collective-permute-start(bf16[512,3584]{1,0:T(8,128)(2,1)} %param.7), channel_id=1, source_target_pairs={{0,16},{16,0},{1,17},{17,1},{2,18},{18,2},{3,19},{19,3},{4,20},{20... | collective-permute-start | bytes 11010056 | tf_op jit(solution)/shard_map/ppermute | solution.py:38
  20.2 38.9 %collective-permute-start.12 = (bf16[512,3584]{1,0:T(8,128)(2,1)}, bf16[512,3584]{1,0:T(8,128)(2,1)S(1)}, u32[]{:S(2)}, u32[]{:S(2)}) collective-permute-start(bf16[512,3584]{1,0:T(8,128)(2,1)} %param.8), channel_id=1, source_target_pairs={{0,16},{16,0},{1,17},{17,1},{2,18},{18,2},{3,19},{19,3},{4,20},{20... | collective-permute-start | bytes 11010056 | tf_op jit(solution)/shard_map/ppermute | solution.py:38
  20.3 21.0 %collective-permute-start.33 = (bf16[4,48,512]{2,1,0:T(8,128)(2,1)S(1)}, bf16[4,48,512]{2,1,0:T(8,128)(2,1)S(1)}, u32[]{:S(2)}, u32[]{:S(2)}) collective-permute-start(bf16[4,48,512]{2,1,0:T(8,128)(2,1)S(1)} %get-tuple-element.97), channel_id=1, source_target_pairs={{0,12},{4,8},{8,4},{12,0},{1,13},{5,9},{9,5},{13,1},{2,14},{6,10},... | collective-permute-start | bytes 589832 | tf_op jit(solution)/shard_map/ppermute | solution.py:38
  41.2 21.7 %collective-permute-start.35 = (bf16[3584,512]{1,0:T(8,128)(2,1)S(1)}, bf16[3584,512]{1,0:T(8,128)(2,1)S(1)}, u32[]{:S(2)}, u32[]{:S(2)}) collective-permute-start(bf16[3584,512]{1,0:T(8,128)(2,1)S(1)} %copy-done.2), channel_id=1, source_target_pairs={{0,16},{16,0},{1,17},{17,1},{2,18},{18,2},{3,19},{19,3},{4,20},{20... | collective-permute-start | bytes 11010056 | tf_op jit(solution)/shard_map/ppermute | solution.py:38
  57.0 18.6 %collective-permute-start.8 = (bf16[96,3584]{1,0:T(8,128)(2,1)}, bf16[96,3584]{1,0:T(8,128)(2,1)}, u32[]{:S(2)}, u32[]{:S(2)}) collective-permute-start(bf16[96,3584]{1,0:T(8,128)(2,1)} %get-tuple-element.55), channel_id=1, source_target_pairs={{0,1},{1,0},{2,3},{3,2},{4,5},{5,4},{6,7},{7,6},{8,9},{9,8},{10,11... | collective-permute-start | bytes 2064392 | tf_op jit(solution)/shard_map/ppermute | solution.py:38
  57.6 49.4 %collective-permute-start.10 = (bf16[96,3584]{1,0:T(8,128)(2,1)S(1)}, bf16[96,3584]{1,0:T(8,128)(2,1)}, u32[]{:S(2)}, u32[]{:S(2)}) collective-permute-start(bf16[96,3584]{1,0:T(8,128)(2,1)S(1)} %get-tuple-element.56), channel_id=1, source_target_pairs={{0,2},{1,3},{2,0},{3,1},{4,6},{5,7},{6,4},{7,5},{8,10},{9,11},{10,... | collective-permute-start | bytes 2064392 | tf_op jit(solution)/shard_map/ppermute | solution.py:38
  61.0 29.4 %collective-permute-start.13 = (bf16[96,3584]{1,0:T(8,128)(2,1)}, bf16[96,3584]{1,0:T(8,128)(2,1)}, u32[]{:S(2)}, u32[]{:S(2)}) collective-permute-start(bf16[96,3584]{1,0:T(8,128)(2,1)} %get-tuple-element.57), channel_id=1, source_target_pairs={{0,1},{1,0},{2,3},{3,2},{4,5},{5,4},{6,7},{7,6},{8,9},{9,8},{10,11... | collective-permute-start | bytes 2064392 | tf_op jit(solution)/shard_map/ppermute | solution.py:38
  62.3 53.3 %collective-permute-start.15 = (bf16[96,3584]{1,0:T(8,128)(2,1)S(1)}, bf16[96,3584]{1,0:T(8,128)(2,1)}, u32[]{:S(2)}, u32[]{:S(2)}) collective-permute-start(bf16[96,3584]{1,0:T(8,128)(2,1)S(1)} %get-tuple-element.58), channel_id=1, source_target_pairs={{0,2},{1,3},{2,0},{3,1},{4,6},{5,7},{6,4},{7,5},{8,10},{9,11},{10,... | collective-permute-start | bytes 2064392 | tf_op jit(solution)/shard_map/ppermute | solution.py:38
  65.3 39.2 %collective-permute-start.36 = (bf16[96,3584]{1,0:T(8,128)(2,1)}, bf16[96,3584]{1,0:T(8,128)(2,1)}, u32[]{:S(2)}, u32[]{:S(2)}) collective-permute-start(bf16[96,3584]{1,0:T(8,128)(2,1)} %get-tuple-element.53), channel_id=1, source_target_pairs={{0,1},{1,0},{2,3},{3,2},{4,5},{5,4},{6,7},{7,6},{8,9},{9,8},{10,11... | collective-permute-start | bytes 2064392 | tf_op jit(solution)/shard_map/ppermute | solution.py:38
  75.6 47.5 %collective-permute-start.38 = (bf16[96,3584]{1,0:T(8,128)(2,1)S(1)}, bf16[96,3584]{1,0:T(8,128)(2,1)S(1)}, u32[]{:S(2)}, u32[]{:S(2)}) collective-permute-start(bf16[96,3584]{1,0:T(8,128)(2,1)S(1)} %get-tuple-element.54), channel_id=1, source_target_pairs={{0,2},{1,3},{2,0},{3,1},{4,6},{5,7},{6,4},{7,5},{8,10},{9,11},{10,... | collective-permute-start | bytes 2064392 | tf_op jit(solution)/shard_map/ppermute | solution.py:38
  90.4 22.4 %collective-permute-start.9 = (bf16[48,3584]{1,0:T(8,128)(2,1)S(1)}, bf16[48,3584]{1,0:T(8,128)(2,1)S(1)}, u32[]{:S(2)}, u32[]{:S(2)}) collective-permute-start(bf16[48,3584]{1,0:T(8,128)(2,1)S(1)} %fusion.17), channel_id=1, source_target_pairs={{0,2},{1,3},{2,0},{3,1},{4,6},{5,7},{6,4},{7,5},{8,10},{9,11},{10,... | collective-permute-start | bytes 1032200 | tf_op jit(solution)/shard_map/ppermute | solution.py:38
  107.0 19.6 %collective-permute-start.37 = (bf16[48,3584]{1,0:T(8,128)(2,1)S(1)}, bf16[48,3584]{1,0:T(8,128)(2,1)S(1)}, u32[]{:S(2)}, u32[]{:S(2)}) collective-permute-start(bf16[48,3584]{1,0:T(8,128)(2,1)S(1)} %fusion.9), channel_id=1, source_target_pairs={{0,2},{1,3},{2,0},{3,1},{4,6},{5,7},{6,4},{7,5},{8,10},{9,11},{10,... | collective-permute-start | bytes 1032200 | tf_op jit(solution)/shard_map/ppermute | solution.py:38
  143.2 16.4 %collective-permute-start.41 = (bf16[48,3584]{1,0:T(8,128)(2,1)S(1)}, bf16[48,3584]{1,0:T(8,128)(2,1)S(1)}, u32[]{:S(2)}, u32[]{:S(2)}) collective-permute-start(bf16[48,3584]{1,0:T(8,128)(2,1)S(1)} %get-tuple-element.67), channel_id=1, source_target_pairs={{0,1},{1,0},{2,3},{3,2},{4,5},{5,4},{6,7},{7,6},{8,9},{9,8},{10,11... | collective-permute-start | bytes 1032200 | tf_op jit(solution)/shard_map/ppermute | solution.py:38
  143.8 21.6 %collective-permute-start.17 = (bf16[48,3584]{1,0:T(8,128)(2,1)S(1)}, bf16[48,3584]{1,0:T(8,128)(2,1)S(1)}, u32[]{:S(2)}, u32[]{:S(2)}) collective-permute-start(bf16[48,3584]{1,0:T(8,128)(2,1)S(1)} %get-tuple-element.80), channel_id=1, source_target_pairs={{0,2},{1,3},{2,0},{3,1},{4,6},{5,7},{6,4},{7,5},{8,10},{9,11},{10,... | collective-permute-start | bytes 1032200 | tf_op jit(solution)/shard_map/ppermute | solution.py:38
  150.7 16.3 %collective-permute-start.18 = (bf16[48,3584]{1,0:T(8,128)(2,1)S(1)}, bf16[48,3584]{1,0:T(8,128)(2,1)S(1)}, u32[]{:S(2)}, u32[]{:S(2)}) collective-permute-start(bf16[48,3584]{1,0:T(8,128)(2,1)S(1)} %get-tuple-element.79), channel_id=1, source_target_pairs={{0,1},{1,0},{2,3},{3,2},{4,5},{5,4},{6,7},{7,6},{8,9},{9,8},{10,11... | collective-permute-start | bytes 1032200 | tf_op jit(solution)/shard_map/ppermute | solution.py:38
  152.2 45.0 %collective-permute-start.47 = (bf16[96,3584]{1,0:T(8,128)(2,1)S(1)}, bf16[96,3584]{1,0:T(8,128)(2,1)S(1)}, u32[]{:S(2)}, u32[]{:S(2)}) collective-permute-start(bf16[96,3584]{1,0:T(8,128)(2,1)S(1)} %pad_maximum_fusion.10), channel_id=1, source_target_pairs={{0,1},{1,0},{2,3},{3,2},{4,5},{5,4},{6,7},{7,6},{8,9},{9,8},{10,11... | collective-permute-start | bytes 2064392 | tf_op jit(solution)/shard_map/ppermute | solution.py:38
  158.1 40.1 %collective-permute-start.48 = (bf16[96,3584]{1,0:T(8,128)(2,1)S(1)}, bf16[96,3584]{1,0:T(8,128)(2,1)S(1)}, u32[]{:S(2)}, u32[]{:S(2)}) collective-permute-start(bf16[96,3584]{1,0:T(8,128)(2,1)S(1)} %pad_maximum_fusion.11), channel_id=1, source_target_pairs={{0,2},{1,3},{2,0},{3,1},{4,6},{5,7},{6,4},{7,5},{8,10},{9,11},{10,... | collective-permute-start | bytes 2064392 | tf_op jit(solution)/shard_map/ppermute | solution.py:38
  159.7 36.8 %collective-permute-start.42 = (bf16[96,3584]{1,0:T(8,128)(2,1)S(1)}, bf16[96,3584]{1,0:T(8,128)(2,1)S(1)}, u32[]{:S(2)}, u32[]{:S(2)}) collective-permute-start(bf16[96,3584]{1,0:T(8,128)(2,1)S(1)} %pad_maximum_fusion.8), channel_id=1, source_target_pairs={{0,1},{1,0},{2,3},{3,2},{4,5},{5,4},{6,7},{7,6},{8,9},{9,8},{10,11... | collective-permute-start | bytes 2064392 | tf_op jit(solution)/shard_map/ppermute | solution.py:38
  165.4 31.6 %collective-permute-start.43 = (bf16[96,3584]{1,0:T(8,128)(2,1)S(1)}, bf16[96,3584]{1,0:T(8,128)(2,1)S(1)}, u32[]{:S(2)}, u32[]{:S(2)}) collective-permute-start(bf16[96,3584]{1,0:T(8,128)(2,1)S(1)} %pad_maximum_fusion.9), channel_id=1, source_target_pairs={{0,2},{1,3},{2,0},{3,1},{4,6},{5,7},{6,4},{7,5},{8,10},{9,11},{10,... | collective-permute-start | bytes 2064392 | tf_op jit(solution)/shard_map/ppermute | solution.py:38
  167.0 41.4 %collective-permute-start.19 = (bf16[96,3584]{1,0:T(8,128)(2,1)S(1)}, bf16[96,3584]{1,0:T(8,128)(2,1)S(1)}, u32[]{:S(2)}, u32[]{:S(2)}) collective-permute-start(bf16[96,3584]{1,0:T(8,128)(2,1)S(1)} %pad_maximum_fusion.6), channel_id=1, source_target_pairs={{0,1},{1,0},{2,3},{3,2},{4,5},{5,4},{6,7},{7,6},{8,9},{9,8},{10,11... | collective-permute-start | bytes 2064392 | tf_op jit(solution)/shard_map/ppermute | solution.py:38
  199.2 17.3 %collective-permute-start.49 = (bf16[384,3584]{1,0:T(8,128)(2,1)}, bf16[384,3584]{1,0:T(8,128)(2,1)S(1)}, u32[]{:S(2)}, u32[]{:S(2)}) collective-permute-start(bf16[384,3584]{1,0:T(8,128)(2,1)} %get-tuple-element.69), channel_id=1, source_target_pairs={{0,16},{16,0},{1,17},{17,1},{2,18},{18,2},{3,19},{19,3},{4,20},{20... | collective-permute-start | bytes 8257544 | tf_op jit(solution)/shard_map/ppermute | solution.py:38
  208.7 19.2 %collective-permute-start.21 = (bf16[384,3584]{1,0:T(8,128)(2,1)S(1)}, bf16[384,3584]{1,0:T(8,128)(2,1)S(1)}, u32[]{:S(2)}, u32[]{:S(2)}) collective-permute-start(bf16[384,3584]{1,0:T(8,128)(2,1)S(1)} %get-tuple-element.75), channel_id=1, source_target_pairs={{0,16},{16,0},{1,17},{17,1},{2,18},{18,2},{3,19},{19,3},{4,20},{20... | collective-permute-start | bytes 8257544 | tf_op jit(solution)/shard_map/ppermute | solution.py:38
  235.0 50.0 %collective-permute-start.23 = (f32[4,48,512]{2,1,0:T(8,128)S(1)}, f32[4,48,512]{2,1,0:T(8,128)S(1)}, u32[]{:S(2)}, u32[]{:S(2)}) collective-permute-start(f32[4,48,512]{2,1,0:T(8,128)S(1)} %pad_maximum_fusion.15), channel_id=1, source_target_pairs={{0,8},{4,12},{8,0},{12,4},{1,9},{5,13},{9,1},{13,5},{2,10},{6,14},... | collective-permute-start | bytes 1179656 | tf_op jit(solution)/shard_map/ppermute | solution.py:38
  235.1 49.8 %collective-permute-start.22 = (f32[4,48,512]{2,1,0:T(8,128)S(1)}, f32[4,48,512]{2,1,0:T(8,128)S(1)}, u32[]{:S(2)}, u32[]{:S(2)}) collective-permute-start(f32[4,48,512]{2,1,0:T(8,128)S(1)} %pad_maximum_fusion.14), channel_id=1, source_target_pairs={{0,4},{4,0},{8,12},{12,8},{1,5},{5,1},{9,13},{13,9},{2,6},{6,2},{1... | collective-permute-start | bytes 1179656 | tf_op jit(solution)/shard_map/ppermute | solution.py:38
  236.3 50.9 %collective-permute-start.52 = (f32[4,48,512]{2,1,0:T(8,128)S(1)}, f32[4,48,512]{2,1,0:T(8,128)S(1)}, u32[]{:S(2)}, u32[]{:S(2)}) collective-permute-start(f32[4,48,512]{2,1,0:T(8,128)S(1)} %pad_maximum_fusion.19), channel_id=1, source_target_pairs={{0,12},{4,8},{8,4},{12,0},{1,13},{5,9},{9,5},{13,1},{2,14},{6,10},... | collective-permute-start | bytes 1179656 | tf_op jit(solution)/shard_map/ppermute | solution.py:38
  239.7 60.0 %collective-permute-start.51 = (f32[4,48,512]{2,1,0:T(8,128)S(1)}, f32[4,48,512]{2,1,0:T(8,128)S(1)}, u32[]{:S(2)}, u32[]{:S(2)}) collective-permute-start(f32[4,48,512]{2,1,0:T(8,128)S(1)} %pad_maximum_fusion.18), channel_id=1, source_target_pairs={{0,8},{4,12},{8,0},{12,4},{1,9},{5,13},{9,1},{13,5},{2,10},{6,14},... | collective-permute-start | bytes 1179656 | tf_op jit(solution)/shard_map/ppermute | solution.py:38
  245.7 54.1 %collective-permute-start.50 = (f32[4,48,512]{2,1,0:T(8,128)S(1)}, f32[4,48,512]{2,1,0:T(8,128)S(1)}, u32[]{:S(2)}, u32[]{:S(2)}) collective-permute-start(f32[4,48,512]{2,1,0:T(8,128)S(1)} %pad_maximum_fusion.17), channel_id=1, source_target_pairs={{0,4},{4,0},{8,12},{12,8},{1,5},{5,1},{9,13},{13,9},{2,6},{6,2},{1... | collective-permute-start | bytes 1179656 | tf_op jit(solution)/shard_map/ppermute | solution.py:38
  285.2 16.9 %collective-permute-start.25 = (bf16[48,512]{1,0:T(8,128)(2,1)S(1)}, bf16[48,512]{1,0:T(8,128)(2,1)S(1)}, u32[]{:S(2)}, u32[]{:S(2)}) collective-permute-start(bf16[48,512]{1,0:T(8,128)(2,1)S(1)} %get-tuple-element.104), channel_id=1, source_target_pairs={{0,1},{1,0},{2,3},{3,2},{4,5},{5,4},{6,7},{7,6},{8,9},{9,8},{10,11... | collective-permute-start | bytes 147464 | tf_op jit(solution)/shard_map/ppermute | solution.py:38
  286.6 17.0 %collective-permute-start.26 = (bf16[48,512]{1,0:T(8,128)(2,1)S(1)}, bf16[48,512]{1,0:T(8,128)(2,1)S(1)}, u32[]{:S(2)}, u32[]{:S(2)}) collective-permute-start(bf16[48,512]{1,0:T(8,128)(2,1)S(1)} %get-tuple-element.103), channel_id=1, source_target_pairs={{0,2},{1,3},{2,0},{3,1},{4,6},{5,7},{6,4},{7,5},{8,10},{9,11},{10,... | collective-permute-start | bytes 147464 | tf_op jit(solution)/shard_map/ppermute | solution.py:38
  287.3 16.3 %collective-permute-start.27 = (bf16[48,512]{1,0:T(8,128)(2,1)S(1)}, bf16[48,512]{1,0:T(8,128)(2,1)S(1)}, u32[]{:S(2)}, u32[]{:S(2)}) collective-permute-start(bf16[48,512]{1,0:T(8,128)(2,1)S(1)} %get-tuple-element.102), channel_id=1, source_target_pairs={{0,3},{1,2},{2,1},{3,0},{4,7},{5,6},{6,5},{7,4},{8,11},{9,10},{10,... | collective-permute-start | bytes 147464 | tf_op jit(solution)/shard_map/ppermute | solution.py:38
  (39 other events, 302.6 us)

commit v2 on v1

v2 whole, which is shorter than its diff:
```python
import jax
import jax.numpy as jnp
from jax import lax
from jax.sharding import PartitionSpec as P

F32, BF16 = jnp.float32, jnp.bfloat16


def dot_nn(left, right):
    return jnp.dot(left, right, preferred_element_type=F32)


def dot_tn(left, right):
    return lax.dot_general(left, right, (((0,), (0,)), ((), ())), preferred_element_type=F32)


def dot_nt(left, right):
    return lax.dot_general(left, right, (((1,), (1,)), ((), ())), preferred_element_type=F32)


def deltas(hidden_grad, gate, up):
    sig = jax.nn.sigmoid(gate)
    gate_delta = (hidden_grad * up * sig * (1.0 + gate * (1.0 - sig))).astype(BF16)
    up_delta = (hidden_grad * gate * sig).astype(BF16)
    return gate_delta, up_delta


def activate(gate, up):
    return (gate * jax.nn.sigmoid(gate) * up).astype(BF16)


def make_on_device(mesh):
    n_row, n_col, n_depth = (mesh.shape[a] for a in ("row", "col", "depth"))
    assert n_depth == 4 and n_col == 2 * n_row
    order = [(0, 0), (1, 0), (0, 2), (1, 1), (0, 1), (0, 3), (1, 2), (1, 3)]
    barrier = lax.optimization_barrier

    def swap(x, axis, k):
        n = mesh.shape[axis]
        return lax.ppermute(x, axis, [(i, i ^ k) for i in range(n)])

    def on_device(tokens, cotangent, gate_weight, up_weight, down_weight):
        n, _ = tokens.shape
        feats = gate_weight.shape[0]
        r, d = lax.axis_index("row"), lax.axis_index("depth")

        def by_row(x):
            return [lax.dynamic_index_in_dim(x, r ^ i, 0, keepdims=False) for i in range(n_row)]

        both = jnp.stack([tokens, cotangent])
        own = [lax.dynamic_slice(both, (0, 0, (d ^ k) * feats), (2, n, feats)) for k in range(n_depth)]
        own = jnp.stack([swap(x, "depth", k) if k else x for k, x in enumerate(own)], axis=1)

        def more_cols(cols, k):
            got = swap(jnp.stack(list(cols.values())), "col", k)
            return {**cols, **{j ^ k: got[i] for i, j in enumerate(cols)}}

        def all_cols(cols, k):
            while k:
                cols = more_cols(cols, k)
                k //= 2
            shares = [jnp.concatenate([cols[2 * h + a][k] for a, k in order]) for h in range(n_row)]
            return by_row(jnp.stack(shares))

        def spread(shares):
            return [shares[0]] + [swap(shares[i], "row", i) for i in range(1, n_row)]

        def tiles(w):
            return [w] + [swap(w, "row", i) for i in range(1, n_row)]

        def part(shares, weights, dot, lo, hi):
            total = dot(shares[0][lo:hi], weights[0])
            for s, w in zip(shares[1:], weights[1:]):
                total = total + dot(s[lo:hi], w)
            return total

        def send_first(sent):
            return swap(sent[: 2 * n], "depth", 1), swap(sent[2 * n :], "depth", 2)

        def second(keep, from_x, from_y):
            a2 = (keep[2 * n : 3 * n] + from_x[n:].astype(F32)).astype(BF16)
            b1 = (keep[3 * n :] + from_y[n:].astype(F32)).astype(BF16)
            return a2, b1

        def total(keep, from_x, from_y, last_y, last_x):
            a0 = keep[:n] + from_x[:n].astype(F32) + last_y.astype(F32)
            b0 = keep[n : 2 * n] + from_y[:n].astype(F32) + last_x.astype(F32)
            return a0, b0

        def gather_row(*blocks):
            x = jnp.concatenate(blocks)
            return [x] + [swap(x, "row", i) for i in range(1, n_row)]

        def cross(b_blocks):
            return swap(b_blocks.astype(BF16), "col", 1).astype(F32)

        def finish(x):
            xs, k = dict(enumerate(by_row(x))), 1
            while k < n_row:
                hs = [h for h in xs if h & k]
                got = swap(jnp.stack([xs.pop(h) for h in hs]).astype(BF16), "col", 2 * k).astype(F32)
                for i, h in enumerate(hs):
                    xs[h ^ k] = xs[h ^ k] + got[i]
                k *= 2
            return xs[0].astype(BF16)

        def place(*sums):
            outs = jnp.zeros((len(sums), n, feats * n_depth), BF16)
            for k in range(n_depth):
                piece = jnp.stack([x[k] for x in sums])
                piece = swap(piece, "depth", k) if k else piece
                outs = lax.dynamic_update_slice(outs, piece, (0, 0, (d ^ k) * feats))
            return [outs[i] for i in range(len(sums))]

        gws, uws, dws = tiles(gate_weight), tiles(up_weight), tiles(down_weight)
        tok = all_cols({0: own[0]}, n_col // 2)
        cot_own, tok = barrier((own[1], tok))
        tok_shares = spread(tok)
        tok_all = jnp.concatenate(tok).T

        gate_sent = part(tok_shares, gws, dot_nn, 4 * n, 8 * n).astype(BF16)
        gate_got = send_first(gate_sent)
        cot_cols = more_cols({0: cot_own}, n_col // 2)
        tok_shares, gate_sent = barrier((tok_shares, gate_sent))
        up_sent = part(tok_shares, uws, dot_nn, 4 * n, 8 * n).astype(BF16)
        up_got = send_first(up_sent)
        tok_shares, cot_cols, gate_got, up_sent = barrier((tok_shares, cot_cols, gate_got, up_sent))
        cot = all_cols(cot_cols, n_col // 4)
        gate_keep = part(tok_shares, gws, dot_nn, 0, 4 * n)
        a2, b1 = second(gate_keep, *gate_got)
        gate_last = swap(a2, "depth", 2), swap(b1, "depth", 1)
        tok_shares, cot, a2, b1 = barrier((tok_shares, cot, a2, b1))
        up_keep = part(tok_shares, uws, dot_nn, 0, 4 * n)
        cot_shares = spread(cot)
        back_sent = part(cot_shares, dws, dot_nt, 4 * n, 8 * n).astype(BF16)
        back_got = send_first(back_sent)
        up_got, cot_shares, back_sent = barrier((up_got, cot_shares, back_sent))
        a2, b1 = second(up_keep, *up_got)
        up_last = swap(a2, "depth", 2), swap(b1, "depth", 1)
        cot_shares, a2, b1 = barrier((cot_shares, a2, b1))
        back_keep = part(cot_shares, dws, dot_nt, 0, 4 * n)

        gate = total(gate_keep, *gate_got, *gate_last)
        up = total(up_keep, *up_got, *up_last)
        h_a0, h_b0 = [activate(g, u) for g, u in zip(gate, up)]
        h_a2, h_b1 = swap(h_a0, "depth", 2), swap(h_b0, "depth", 1)
        back_got, h_a0, h_b0 = barrier((back_got, h_a0, h_b0))
        a2, b1 = second(back_keep, *back_got)
        back_last = swap(a2, "depth", 2), swap(b1, "depth", 1)
        h_a2, h_b1, a2, b1 = barrier((h_a2, h_b1, a2, b1))
        h_from_x = swap(jnp.concatenate([h_a0, h_a2]), "depth", 1)
        h_from_y = swap(jnp.concatenate([h_b0, h_b1]), "depth", 2)
        hidden_grad = total(back_keep, *back_got, *back_last)
        d_a0, d_b0 = [jnp.concatenate(deltas(h, g, u)) for h, g, u in zip(hidden_grad, gate, up)]
        d_a2, d_b1 = swap(d_a0, "depth", 2), swap(d_b0, "depth", 1)

        def back(rows):
            blocks = rows[0].shape[0] // (2 * n)
            rows = [x.reshape(blocks, 2, n, -1) for x in rows]
            gd, ud = [[x[:, i].reshape(blocks * n, -1) for x in rows] for i in range(2)]
            sums = [dot_nt(g, gate_weight) + dot_nt(u, up_weight) for g, u in zip(gd, ud)]
            return gd, ud, jnp.stack(sums).reshape(n_row, blocks, n, feats)

        gd_e, ud_e, early = back(gather_row(d_a0, d_b0))
        h_from_x, h_from_y, early = barrier((h_from_x, h_from_y, early))
        hid_rows = gather_row(h_a0, h_b0, h_a2, h_b1, h_from_x, h_from_y)
        out = jnp.stack([dot_nn(x, down_weight) for x in hid_rows]).reshape(n_row, 8, n, feats)
        got = cross(jnp.concatenate([jnp.stack([out[:, i] for i in (1, 3, 6, 7)], axis=1), early[:, 1:]], axis=1))
        hid_rows, cot, out = barrier((hid_rows, cot, out))
        down_grad = dot_tn(jnp.concatenate(hid_rows), jnp.concatenate(cot))

        d_a2, d_b1, down_grad = barrier((d_a2, d_b1, down_grad))
        from_x = swap(jnp.concatenate([d_a0, d_a2]), "depth", 1)
        from_y = swap(jnp.concatenate([d_b0, d_b1]), "depth", 2)
        middle = gather_row(d_a2, d_b1)
        z_out = jnp.stack([out[:, i] for i in (0, 4, 2, 5)], axis=1) + got[:, :4]
        done = finish(jnp.concatenate([z_out, early[:, :1] + got[:, 4:]], axis=1))
        from_x, from_y, middle, done = barrier((from_x, from_y, middle, done))
        late = [jnp.concatenate(x) for x in zip(middle, gather_row(from_x, from_y))]
        gd_l, ud_l, late = back(late)
        tok_all, late = barrier((tok_all, late))
        got_l = cross(jnp.stack([late[:, i] for i in (1, 4, 5)], axis=1))

        def by_share(e, l):
            return jnp.concatenate([x for pair in zip(e, l) for x in pair])

        gate_grad = dot_nn(tok_all, by_share(gd_e, gd_l))
        tok_all, got_l, gate_grad = barrier((tok_all, got_l, gate_grad))
        rest = finish(jnp.stack([late[:, i] for i in (2, 0, 3)], axis=1) + got_l)
        output, input_grad = place(done[:4], [done[4], *rest])
        up_grad = dot_nn(tok_all, by_share(ud_e, ud_l))
        return output, input_grad, gate_grad, up_grad, down_grad

    return on_device


def solution(mesh):
    act = P(("col", "depth"), "row")
    wide = P(("row", "depth"), "col")
    tall = P("col", ("row", "depth"))
    return jax.shard_map(
        make_on_device(mesh),
        mesh=mesh,
        in_specs=(act, act, wide, wide, tall),
        out_specs=(act, act, wide, wide, tall),
        check_vma=False,
    )
```

time: 308 us -> 227 us (0.74)
  waiting for transfers between devices: 155 us -> 117 us
  starting transfers between devices: 86.7 us -> 48.9 us
  local copies, waits for them, and re-layouts: 15.4 us -> 2.57 us
  matrix products: 37 us -> 49.8 us
  other arithmetic: 12.3 us -> 7.59 us
    ppermute x56 -> x43, waiting for transfers between devices: 155 us -> 117 us  [swap(): return lax.ppermute(x, axis, [(i, i ^ k) for i in range(n)])]
    ppermute x56 -> x43, starting transfers between devices: 86.7 us -> 48.9 us  [swap(): return lax.ppermute(x, axis, [(i, i ^ k) for i in range(n)])]
    dot_general x9 -> x12, matrix products: 10.1 us -> 29 us  [dot_nn(): return jnp.dot(left, right, preferred_element_type=F32)]
    dot_general x3 -> x1, matrix products: 15.5 us -> 5.38 us  [dot_tn(): lax.dot_general(left, right, (((0,), (0,)), ((), ())), preferred_element_...]
    unnamed x56 -> x35, local copies, waits for them, and re-layouts: 7.52 us -> 0.35 us
    add x6 -> x3, other arithmetic: 6.12 us -> 0.3 us  [the longest x1 0.16 us: on_device(): z_out = jnp.stack([out[:, i] for i in (0, 4, 2, 5)], axis=1) + got[:, :4]]
    dot_general x6 -> x12, matrix products: 11.4 us -> 15.4 us  [dot_nt(): lax.dot_general(left, right, (((1,), (1,)), ((), ())), preferred_element_...]
  transfers between devices with their start and end apart: 56 -> 43, of which waited for: 24 -> 29; matrix products, arithmetic and copies ran while one was open for 17% -> 24% of each run, Pallas kernels for 0% -> 0%
where the time goes in v2:
time: 227 us
  waiting for transfers between devices  117 us (52%)
  matrix products  49.8 us (22%)
  starting transfers between devices  48.9 us (22%)
  other arithmetic  7.59 us (3%)
  local copies, waits for them, and re-layouts  2.57 us (1%)
    ppermute x43, waiting for transfers between devices, swap(): return lax.ppermute(x, axis, [(i, i ^ k) for i in range(n)])  117 us
    ppermute x43, starting transfers between devices, swap(): return lax.ppermute(x, axis, [(i, i ^ k) for i in range(n)])  48.9 us
    dot_general x12, matrix products, dot_nn(): return jnp.dot(left, right, preferred_element_type=F32)  29 us
    dot_general x12, matrix products, dot_nt(): lax.dot_general(left, right, (((1,), (1,)), ((), ())), preferred_element_...  15.4 us
    dot_general x1, matrix products, dot_tn(): lax.dot_general(left, right, (((0,), (0,)), ((), ())), preferred_element_...  5.38 us
  transfers between devices with their start and end apart: 43, of which 29 were waited for; matrix products, arithmetic and copies ran while one was open for 24% of the time, Pallas kernels for 0%

profile of v2, /device:TPU:0, one launch (start us, length us, event | category | flops | bytes accessed | tf_op | source)
XLA Modules:
  0.0 227.1 jit_solution(11015959284154992504)
XLA Ops:
  1.7 3.0 %collective-permute-start = (bf16[2,48,512]{2,1,0:T(8,128)(2,1)S(1)}, bf16[2,48,512]{2,1,0:T(8,128)(2,1)S(1)}, u32[]{:S(2)}, u32[]{:S(2)}) collective-permute-start(bf16[2,48,512]{2,1,0:T(8,128)(2,1)S(1)} %get-tuple-element.161), channel_id=1, source_target_pairs={{0,1},{1,0},{2,3},{3,2},{4,5},{5,4},{6,7},{7,6},{8,9},{9,8},{10,11... | collective-permute-start | bytes 294920 | tf_op jit(solution)/shard_map/ppermute | solution.py:40
  7.7 2.6 %collective-permute-done.1 = bf16[2,48,512]{2,1,0:T(8,128)(2,1)S(1)} collective-permute-done((bf16[2,48,512]{2,1,0:T(8,128)(2,1)S(1)}, bf16[2,48,512]{2,1,0:T(8,128)(2,1)S(1)}, u32[]{:S(2)}, u32[]{:S(2)}) %collective-permute-start.1) | collective-permute-done | bytes 98336 | tf_op jit(solution)/shard_map/ppermute | solution.py:40
  11.8 2.7 %collective-permute-start.3 = (bf16[1,4,48,512]{3,2,1,0:T(8,128)(2,1)S(1)}, bf16[1,4,48,512]{3,2,1,0:T(8,128)(2,1)S(1)}, u32[]{:S(2)}, u32[]{:S(2)}) collective-permute-start(bf16[1,4,48,512]{3,2,1,0:T(8,128)(2,1)S(1)} %get-tuple-element.158), channel_id=1, source_target_pairs={{0,8},{4,12},{8,0},{12,4},{1,9},{5,13},{9,1},{13,5},{2,10},{6,14},... | collective-permute-start | bytes 589832 | tf_op jit(solution)/shard_map/ppermute | solution.py:40
  14.5 7.6 %collective-permute-done.3 = bf16[1,4,48,512]{3,2,1,0:T(8,128)(2,1)S(1)} collective-permute-done((bf16[1,4,48,512]{3,2,1,0:T(8,128)(2,1)S(1)}, bf16[1,4,48,512]{3,2,1,0:T(8,128)(2,1)S(1)}, u32[]{:S(2)}, u32[]{:S(2)}) %collective-permute-start.3) | collective-permute-done | bytes 196640 | tf_op jit(solution)/shard_map/ppermute | solution.py:40
  22.8 9.3 %collective-permute-done.4 = bf16[2,4,48,512]{3,2,1,0:T(8,128)(2,1)S(1)} collective-permute-done((bf16[2,4,48,512]{3,2,1,0:T(8,128)(2,1)S(1)}, bf16[2,4,48,512]{3,2,1,0:T(8,128)(2,1)S(1)}, u32[]{:S(2)}, u32[]{:S(2)}) %collective-permute-start.4) | collective-permute-done | bytes 393248 | tf_op jit(solution)/shard_map/ppermute | solution.py:40
  33.1 2.7 %collective-permute-start.10 = (bf16[1,4,48,512]{3,2,1,0:T(8,128)(2,1)S(1)}, bf16[1,4,48,512]{3,2,1,0:T(8,128)(2,1)S(1)}, u32[]{:S(2)}, u32[]{:S(2)}) collective-permute-start(bf16[1,4,48,512]{3,2,1,0:T(8,128)(2,1)S(1)} %bitcast.225), channel_id=1, source_target_pairs={{0,8},{4,12},{8,0},{12,4},{1,9},{5,13},{9,1},{13,5},{2,10},{6,14},... | collective-permute-start | bytes 589832 | tf_op jit(solution)/shard_map/ppermute | solution.py:40
  36.7 2.9 %fusion.20 = bf16[192,3584]{1,0:T(8,128)(2,1)S(1)} fusion(f32[192,3584]{1,0:T(8,128)S(1)} %fusion.68, bf16[512,3584]{1,0:T(8,128)(2,1)} %collective-permute-done.6, bf16[384,512]{1,0:T(8,128)(2,1)S(1)} %collective-permute-done.5), kind=kOutput, calls=%fused_computation.26 | convolution fusion | flops 706019328 | bytes 7995392 | tf_op jit(solution)/shard_map/dot_general | solution.py:10
  39.9 2.5 %collective-permute-start.11 = (bf16[96,3584]{1,0:T(8,128)(2,1)S(1)}, bf16[96,3584]{1,0:T(8,128)(2,1)S(1)}, u32[]{:S(2)}, u32[]{:S(2)}) collective-permute-start(bf16[96,3584]{1,0:T(8,128)(2,1)S(1)} %get-tuple-element.128), channel_id=1, source_target_pairs={{0,1},{1,0},{2,3},{3,2},{4,5},{5,4},{6,7},{7,6},{8,9},{9,8},{10,11... | collective-permute-start | bytes 2064392 | tf_op jit(solution)/shard_map/ppermute | solution.py:40
  42.4 2.9 %fusion.65 = f32[192,3584]{1,0:T(8,128)S(1)} fusion(bf16[512,3584]{1,0:T(8,128)(2,1)} %collective-permute-done.7, bf16[384,512]{1,0:T(8,128)(2,1)S(1)} %collective-permute-done.5), kind=kOutput, calls=%fused_computation.144 | convolution fusion | flops 704643072 | bytes 6619136 | tf_op jit(solution)/shard_map/dot_general | solution.py:10
  48.3 9.8 %collective-permute-done.12 = bf16[96,3584]{1,0:T(8,128)(2,1)S(1)} collective-permute-done((bf16[96,3584]{1,0:T(8,128)(2,1)S(1)}, bf16[96,3584]{1,0:T(8,128)(2,1)S(1)}, u32[]{:S(2)}, u32[]{:S(2)}) %collective-permute-start.12) | collective-permute-done | bytes 688160 | tf_op jit(solution)/shard_map/ppermute | solution.py:40
  58.7 1.8 collective-permute-start.13
  60.6 2.9 %fusion.62 = f32[192,3584]{1,0:T(8,128)S(1)} fusion(bf16[512,3584]{1,0:T(8,128)(2,1)} %collective-permute-done.6, bf16[384,512]{1,0:T(8,128)(2,1)S(1)} %collective-permute-done.5), kind=kOutput, calls=%fused_computation.141 | convolution fusion | flops 704643072 | bytes 6619136 | tf_op jit(solution)/shard_map/dot_general | solution.py:10
  64.6 2.1 collective-permute-start.20
  69.0 3.2 %convolution_add_fusion.1 = f32[192,3584]{1,0:T(8,128)S(1)} fusion(f32[192,3584]{1,0:T(8,128)S(1)} %fusion.58, bf16[512,3584]{1,0:T(8,128)(2,1)} %collective-permute-done.7, bf16[384,512]{1,0:T(8,128)(2,1)S(1)} %collective-permute-done.5), kind=kOutput, calls=%fused_computation.21 | convolution fusion | flops 705331200 | bytes 9371648 | tf_op jit(solution)/shard_map/dot_general | solution.py:10
  84.5 3.4 %collective-permute-done.21 = bf16[48,3584]{1,0:T(8,128)(2,1)S(1)} collective-permute-done((bf16[48,3584]{1,0:T(8,128)(2,1)S(1)}, bf16[48,3584]{1,0:T(8,128)(2,1)S(1)}, u32[]{:S(2)}, u32[]{:S(2)}) %collective-permute-start.21) | collective-permute-done | bytes 344096 | tf_op jit(solution)/shard_map/ppermute | solution.py:40
  87.9 3.9 %collective-permute-done.19 = bf16[48,3584]{1,0:T(8,128)(2,1)S(1)} collective-permute-done((bf16[48,3584]{1,0:T(8,128)(2,1)S(1)}, bf16[48,3584]{1,0:T(8,128)(2,1)S(1)}, u32[]{:S(2)}, u32[]{:S(2)}) %collective-permute-start.19) | collective-permute-done | bytes 344096 | tf_op jit(solution)/shard_map/ppermute | solution.py:40
  95.8 10.7 %collective-permute-done.17 = bf16[96,3584]{1,0:T(8,128)(2,1)S(1)} collective-permute-done((bf16[96,3584]{1,0:T(8,128)(2,1)S(1)}, bf16[96,3584]{1,0:T(8,128)(2,1)S(1)}, u32[]{:S(2)}, u32[]{:S(2)}) %collective-permute-start.17) | collective-permute-done | bytes 688160 | tf_op jit(solution)/shard_map/ppermute | solution.py:40
  109.9 4.1 %collective-permute-done.26 = bf16[48,3584]{1,0:T(8,128)(2,1)S(1)} collective-permute-done((bf16[48,3584]{1,0:T(8,128)(2,1)S(1)}, bf16[48,3584]{1,0:T(8,128)(2,1)S(1)}, u32[]{:S(2)}, u32[]{:S(2)}) %collective-permute-start.26) | collective-permute-done | bytes 344096 | tf_op jit(solution)/shard_map/ppermute | solution.py:40
  117.3 4.1 %collective-permute-done.22 = bf16[48,3584]{1,0:T(8,128)(2,1)S(1)} collective-permute-done((bf16[48,3584]{1,0:T(8,128)(2,1)S(1)}, bf16[48,3584]{1,0:T(8,128)(2,1)S(1)}, u32[]{:S(2)}, u32[]{:S(2)}) %collective-permute-start.22) | collective-permute-done | bytes 344096 | tf_op jit(solution)/shard_map/ppermute | solution.py:40
  129.1 6.5 %collective-permute-done.29 = bf16[96,3584]{1,0:T(8,128)(2,1)S(1)} collective-permute-done((bf16[96,3584]{1,0:T(8,128)(2,1)S(1)}, bf16[96,3584]{1,0:T(8,128)(2,1)S(1)}, u32[]{:S(2)}, u32[]{:S(2)}) %collective-permute-start.29) | collective-permute-done | bytes 688160 | tf_op jit(solution)/shard_map/ppermute | solution.py:40
  142.9 5.4 %fusion = f32[3584,512]{1,0:T(8,128)} fusion(bf16[384,3584]{1,0:T(8,128)(2,1)S(1)} %collective-permute-done.31, bf16[384,3584]{1,0:T(8,128)(2,1)S(1)} %constant_dynamic-update-slice_fusion.32, bf16[384,512]{1,0:T(8,128)(2,1)S(1)} %get-tuple-element.85, bf16[384,512]{1,0:T(8,128)(2,1)S(1)} %get-tuple-element.84), kind=kOutput, calls=%fused_computation | convolution fusion | flops 2831155200 | bytes 13631488 | tf_op jit(solution)/shard_map/dot_general | solution.py:14
  148.2 5.6 %collective-permute-done.23 = bf16[96,3584]{1,0:T(8,128)(2,1)S(1)} collective-permute-done((bf16[96,3584]{1,0:T(8,128)(2,1)S(1)}, bf16[96,3584]{1,0:T(8,128)(2,1)S(1)}, u32[]{:S(2)}, u32[]{:S(2)}) %collective-permute-start.23) | collective-permute-done | bytes 688160 | tf_op jit(solution)/shard_map/ppermute | solution.py:40
  160.0 8.2 %collective-permute-done.35 = bf16[2,5,48,512]{3,2,1,0:T(8,128)(2,1)S(1)} collective-permute-done((bf16[2,5,48,512]{3,2,1,0:T(8,128)(2,1)S(1)}, bf16[2,5,48,512]{3,2,1,0:T(8,128)(2,1)S(1)}, u32[]{:S(2)}, u32[]{:S(2)}) %collective-permute-start.35) | collective-permute-done | bytes 491552 | tf_op jit(solution)/shard_map/ppermute | solution.py:40
  169.6 11.4 %collective-permute-done.36 = bf16[1,5,48,512]{3,2,1,0:T(8,128)(2,1)S(1)} collective-permute-done((bf16[1,5,48,512]{3,2,1,0:T(8,128)(2,1)S(1)}, bf16[1,5,48,512]{3,2,1,0:T(8,128)(2,1)S(1)}, u32[]{:S(2)}, u32[]{:S(2)}) %collective-permute-start.36) | collective-permute-done | bytes 245792 | tf_op jit(solution)/shard_map/ppermute | solution.py:40
  181.1 7.6 %collective-permute-done.33 = bf16[192,3584]{1,0:T(8,128)(2,1)S(1)} collective-permute-done((bf16[192,3584]{1,0:T(8,128)(2,1)S(1)}, bf16[192,3584]{1,0:T(8,128)(2,1)S(1)}, u32[]{:S(2)}, u32[]{:S(2)}) %collective-permute-start.33) | collective-permute-done | bytes 1376288 | tf_op jit(solution)/shard_map/ppermute | solution.py:40
  188.7 2.3 %collective-permute-done.32 = bf16[192,3584]{1,0:T(8,128)(2,1)S(1)} collective-permute-done((bf16[192,3584]{1,0:T(8,128)(2,1)S(1)}, bf16[192,3584]{1,0:T(8,128)(2,1)S(1)}, u32[]{:S(2)}, u32[]{:S(2)}) %collective-permute-start.32) | collective-permute-done | bytes 1376288 | tf_op jit(solution)/shard_map/ppermute | solution.py:40
  194.6 1.8 collective-permute-done.37
  200.1 5.2 %fusion.4 = f32[512,3584]{1,0:T(8,128)} fusion(bf16[512,768]{0,1:T(8,128)(2,1)S(1)} %maximum_bitcast_fusion, bf16[288,3584]{1,0:T(8,128)(2,1)S(1)} %bitcast.224, bf16[96,3584]{1,0:T(8,128)(2,1)S(1)} %bitcast.216, bf16[288,3584]{1,0:T(8,128)(2,1)S(1)} %bitcast.222, bf16[96,3584]{1,0:T(8,128)(2,1)S(1)} %bitcast.214), kind=kOutput, calls=%fused_computation.4 | convolution fusion | flops 2840592384 | bytes 13631488 | tf_op jit(solution)/shard_map/dot_general | solution.py:10
  205.3 3.6 %collective-permute-done.38 = bf16[2,3,48,512]{3,2,1,0:T(8,128)(2,1)S(1)} collective-permute-done((bf16[2,3,48,512]{3,2,1,0:T(8,128)(2,1)S(1)}, bf16[2,3,48,512]{3,2,1,0:T(8,128)(2,1)S(1)}, u32[]{:S(2)}, u32[]{:S(2)}) %collective-permute-start.38) | collective-permute-done | bytes 294944 | tf_op jit(solution)/shard_map/ppermute | solution.py:40
  210.2 5.1 %fusion.12 = f32[512,3584]{1,0:T(8,128)} fusion(bf16[512,768]{0,1:T(8,128)(2,1)S(1)} %maximum_bitcast_fusion, bf16[288,3584]{1,0:T(8,128)(2,1)S(1)} %bitcast.220, bf16[96,3584]{1,0:T(8,128)(2,1)S(1)} %bitcast.212, bf16[288,3584]{1,0:T(8,128)(2,1)S(1)} %bitcast.218, bf16[96,3584]{1,0:T(8,128)(2,1)S(1)} %bitcast.210), kind=kOutput, calls=%fused_computation.12 | convolution fusion | flops 2840592384 | bytes 13631488 | tf_op jit(solution)/shard_map/dot_general | solution.py:10
  215.3 2.7 %collective-permute-done.39 = bf16[1,3,48,512]{3,2,1,0:T(8,128)(2,1)S(1)} collective-permute-done((bf16[1,3,48,512]{3,2,1,0:T(8,128)(2,1)S(1)}, bf16[1,3,48,512]{3,2,1,0:T(8,128)(2,1)S(1)}, u32[]{:S(2)}, u32[]{:S(2)}) %collective-permute-start.39) | collective-permute-done | bytes 147488 | tf_op jit(solution)/shard_map/ppermute | solution.py:40
  222.9 2.5 %collective-permute-done.41 = bf16[2,48,512]{2,1,0:T(8,128)(2,1)S(1)} collective-permute-done((bf16[2,48,512]{2,1,0:T(8,128)(2,1)S(1)}, bf16[2,48,512]{2,1,0:T(8,128)(2,1)S(1)}, u32[]{:S(2)}, u32[]{:S(2)}) %collective-permute-start.41) | collective-permute-done | bytes 98336 | tf_op jit(solution)/shard_map/ppermute | solution.py:40
  (184 shorter events, 75.5 us)
Async XLA Ops:
  6.2 30.5 %collective-permute-start.6 = (bf16[512,3584]{1,0:T(8,128)(2,1)}, bf16[512,3584]{1,0:T(8,128)(2,1)}, u32[]{:S(2)}, u32[]{:S(2)}) collective-permute-start(bf16[512,3584]{1,0:T(8,128)(2,1)} %param.7), channel_id=1, source_target_pairs={{0,16},{16,0},{1,17},{17,1},{2,18},{18,2},{3,19},{19,3},{4,20},{20... | collective-permute-start | bytes 11010056 | tf_op jit(solution)/shard_map/ppermute | solution.py:40
  11.8 10.2 %collective-permute-start.3 = (bf16[1,4,48,512]{3,2,1,0:T(8,128)(2,1)S(1)}, bf16[1,4,48,512]{3,2,1,0:T(8,128)(2,1)S(1)}, u32[]{:S(2)}, u32[]{:S(2)}) collective-permute-start(bf16[1,4,48,512]{3,2,1,0:T(8,128)(2,1)S(1)} %get-tuple-element.158), channel_id=1, source_target_pairs={{0,8},{4,12},{8,0},{12,4},{1,9},{5,13},{9,1},{13,5},{2,10},{6,14},... | collective-permute-start | bytes 589832 | tf_op jit(solution)/shard_map/ppermute | solution.py:40
  14.5 27.9 %collective-permute-start.7 = (bf16[512,3584]{1,0:T(8,128)(2,1)}, bf16[512,3584]{1,0:T(8,128)(2,1)}, u32[]{:S(2)}, u32[]{:S(2)}) collective-permute-start(bf16[512,3584]{1,0:T(8,128)(2,1)} %param.8), channel_id=1, source_target_pairs={{0,16},{16,0},{1,17},{17,1},{2,18},{18,2},{3,19},{19,3},{4,20},{20... | collective-permute-start | bytes 11010056 | tf_op jit(solution)/shard_map/ppermute | solution.py:40
  22.1 10.0 %collective-permute-start.4 = (bf16[2,4,48,512]{3,2,1,0:T(8,128)(2,1)S(1)}, bf16[2,4,48,512]{3,2,1,0:T(8,128)(2,1)S(1)}, u32[]{:S(2)}, u32[]{:S(2)}) collective-permute-start(bf16[2,4,48,512]{3,2,1,0:T(8,128)(2,1)S(1)} %pad_maximum_fusion.15), channel_id=1, source_target_pairs={{0,4},{4,0},{8,12},{12,8},{1,5},{5,1},{9,13},{13,9},{2,6},{6,2},{1... | collective-permute-start | bytes 1179656 | tf_op jit(solution)/shard_map/ppermute | solution.py:40
  32.6 40.9 %collective-permute-start.15 = (bf16[3584,512]{1,0:T(8,128)(2,1)}, bf16[3584,512]{1,0:T(8,128)(2,1)S(1)}, u32[]{:S(2)}, u32[]{:S(2)}) collective-permute-start(bf16[3584,512]{1,0:T(8,128)(2,1)} %param.9), channel_id=1, source_target_pairs={{0,16},{16,0},{1,17},{17,1},{2,18},{18,2},{3,19},{19,3},{4,20},{20... | collective-permute-start | bytes 11010056 | tf_op jit(solution)/shard_map/ppermute | solution.py:40
  33.1 15.0 %collective-permute-start.10 = (bf16[1,4,48,512]{3,2,1,0:T(8,128)(2,1)S(1)}, bf16[1,4,48,512]{3,2,1,0:T(8,128)(2,1)S(1)}, u32[]{:S(2)}, u32[]{:S(2)}) collective-permute-start(bf16[1,4,48,512]{3,2,1,0:T(8,128)(2,1)S(1)} %bitcast.225), channel_id=1, source_target_pairs={{0,8},{4,12},{8,0},{12,4},{1,9},{5,13},{9,1},{13,5},{2,10},{6,14},... | collective-permute-start | bytes 589832 | tf_op jit(solution)/shard_map/ppermute | solution.py:40
  39.7 18.4 %collective-permute-start.12 = (bf16[96,3584]{1,0:T(8,128)(2,1)S(1)}, bf16[96,3584]{1,0:T(8,128)(2,1)S(1)}, u32[]{:S(2)}, u32[]{:S(2)}) collective-permute-start(bf16[96,3584]{1,0:T(8,128)(2,1)S(1)} %get-tuple-element.127), channel_id=1, source_target_pairs={{0,2},{1,3},{2,0},{3,1},{4,6},{5,7},{6,4},{7,5},{8,10},{9,11},{10,... | collective-permute-start | bytes 2064392 | tf_op jit(solution)/shard_map/ppermute | solution.py:40
  39.9 18.8 %collective-permute-start.11 = (bf16[96,3584]{1,0:T(8,128)(2,1)S(1)}, bf16[96,3584]{1,0:T(8,128)(2,1)S(1)}, u32[]{:S(2)}, u32[]{:S(2)}) collective-permute-start(bf16[96,3584]{1,0:T(8,128)(2,1)S(1)} %get-tuple-element.128), channel_id=1, source_target_pairs={{0,1},{1,0},{2,3},{3,2},{4,5},{5,4},{6,7},{7,6},{8,9},{9,8},{10,11... | collective-permute-start | bytes 2064392 | tf_op jit(solution)/shard_map/ppermute | solution.py:40
  46.4 30.4 %collective-permute-start.9 = (bf16[96,3584]{1,0:T(8,128)(2,1)S(1)}, bf16[96,3584]{1,0:T(8,128)(2,1)S(1)}, u32[]{:S(2)}, u32[]{:S(2)}) collective-permute-start(bf16[96,3584]{1,0:T(8,128)(2,1)S(1)} %get-tuple-element.129), channel_id=1, source_target_pairs={{0,2},{1,3},{2,0},{3,1},{4,6},{5,7},{6,4},{7,5},{8,10},{9,11},{10,... | collective-permute-start | bytes 2064392 | tf_op jit(solution)/shard_map/ppermute | solution.py:40
  48.1 28.7 %collective-permute-start.8 = (bf16[96,3584]{1,0:T(8,128)(2,1)S(1)}, bf16[96,3584]{1,0:T(8,128)(2,1)S(1)}, u32[]{:S(2)}, u32[]{:S(2)}) collective-permute-start(bf16[96,3584]{1,0:T(8,128)(2,1)S(1)} %get-tuple-element.130), channel_id=1, source_target_pairs={{0,1},{1,0},{2,3},{3,2},{4,5},{5,4},{6,7},{7,6},{8,9},{9,8},{10,11... | collective-permute-start | bytes 2064392 | tf_op jit(solution)/shard_map/ppermute | solution.py:40
  58.7 8.8 %collective-permute-start.13 = (bf16[2,4,48,512]{3,2,1,0:T(8,128)(2,1)S(1)}, bf16[2,4,48,512]{3,2,1,0:T(8,128)(2,1)S(1)}, u32[]{:S(2)}, u32[]{:S(2)}) collective-permute-start(bf16[2,4,48,512]{3,2,1,0:T(8,128)(2,1)S(1)} %pad_maximum_fusion.16), channel_id=1, source_target_pairs={{0,4},{4,0},{8,12},{12,8},{1,5},{5,1},{9,13},{13,9},{2,6},{6,2},{1... | collective-permute-start | bytes 1179656 | tf_op jit(solution)/shard_map/ppermute | solution.py:40
  64.6 18.6 %collective-permute-start.20 = (bf16[48,3584]{1,0:T(8,128)(2,1)S(1)}, bf16[48,3584]{1,0:T(8,128)(2,1)S(1)}, u32[]{:S(2)}, u32[]{:S(2)}) collective-permute-start(bf16[48,3584]{1,0:T(8,128)(2,1)S(1)} %get-tuple-element.115), channel_id=1, source_target_pairs={{0,1},{1,0},{2,3},{3,2},{4,5},{5,4},{6,7},{7,6},{8,9},{9,8},{10,11... | collective-permute-start | bytes 1032200 | tf_op jit(solution)/shard_map/ppermute | solution.py:40
  73.5 10.9 %collective-permute-start.18 = (bf16[48,3584]{1,0:T(8,128)(2,1)S(1)}, bf16[48,3584]{1,0:T(8,128)(2,1)S(1)}, u32[]{:S(2)}, u32[]{:S(2)}) collective-permute-start(bf16[48,3584]{1,0:T(8,128)(2,1)S(1)} %get-tuple-element.116), channel_id=1, source_target_pairs={{0,2},{1,3},{2,0},{3,1},{4,6},{5,7},{6,4},{7,5},{8,10},{9,11},{10,... | collective-permute-start | bytes 1032200 | tf_op jit(solution)/shard_map/ppermute | solution.py:40
  76.9 11.0 %collective-permute-start.21 = (bf16[48,3584]{1,0:T(8,128)(2,1)S(1)}, bf16[48,3584]{1,0:T(8,128)(2,1)S(1)}, u32[]{:S(2)}, u32[]{:S(2)}) collective-permute-start(bf16[48,3584]{1,0:T(8,128)(2,1)S(1)} %get-tuple-element.113), channel_id=1, source_target_pairs={{0,1},{1,0},{2,3},{3,2},{4,5},{5,4},{6,7},{7,6},{8,9},{9,8},{10,11... | collective-permute-start | bytes 1032200 | tf_op jit(solution)/shard_map/ppermute | solution.py:40
  78.4 13.4 %collective-permute-start.19 = (bf16[48,3584]{1,0:T(8,128)(2,1)S(1)}, bf16[48,3584]{1,0:T(8,128)(2,1)S(1)}, u32[]{:S(2)}, u32[]{:S(2)}) collective-permute-start(bf16[48,3584]{1,0:T(8,128)(2,1)S(1)} %get-tuple-element.114), channel_id=1, source_target_pairs={{0,2},{1,3},{2,0},{3,1},{4,6},{5,7},{6,4},{7,5},{8,10},{9,11},{10,... | collective-permute-start | bytes 1032200 | tf_op jit(solution)/shard_map/ppermute | solution.py:40
  79.0 27.6 %collective-permute-start.17 = (bf16[96,3584]{1,0:T(8,128)(2,1)S(1)}, bf16[96,3584]{1,0:T(8,128)(2,1)S(1)}, u32[]{:S(2)}, u32[]{:S(2)}) collective-permute-start(bf16[96,3584]{1,0:T(8,128)(2,1)S(1)} %get-tuple-element.125), channel_id=1, source_target_pairs={{0,2},{1,3},{2,0},{3,1},{4,6},{5,7},{6,4},{7,5},{8,10},{9,11},{10,... | collective-permute-start | bytes 2064392 | tf_op jit(solution)/shard_map/ppermute | solution.py:40
  83.2 23.4 %collective-permute-start.16 = (bf16[96,3584]{1,0:T(8,128)(2,1)S(1)}, bf16[96,3584]{1,0:T(8,128)(2,1)S(1)}, u32[]{:S(2)}, u32[]{:S(2)}) collective-permute-start(bf16[96,3584]{1,0:T(8,128)(2,1)S(1)} %get-tuple-element.126), channel_id=1, source_target_pairs={{0,1},{1,0},{2,3},{3,2},{4,5},{5,4},{6,7},{7,6},{8,9},{9,8},{10,11... | collective-permute-start | bytes 2064392 | tf_op jit(solution)/shard_map/ppermute | solution.py:40
  92.7 17.2 %collective-permute-start.27 = (bf16[48,3584]{1,0:T(8,128)(2,1)S(1)}, bf16[48,3584]{1,0:T(8,128)(2,1)S(1)}, u32[]{:S(2)}, u32[]{:S(2)}) collective-permute-start(bf16[48,3584]{1,0:T(8,128)(2,1)S(1)} %get-tuple-element.77), channel_id=1, source_target_pairs={{0,1},{1,0},{2,3},{3,2},{4,5},{5,4},{6,7},{7,6},{8,9},{9,8},{10,11... | collective-permute-start | bytes 1032200 | tf_op jit(solution)/shard_map/ppermute | solution.py:40
  94.4 19.5 %collective-permute-start.26 = (bf16[48,3584]{1,0:T(8,128)(2,1)S(1)}, bf16[48,3584]{1,0:T(8,128)(2,1)S(1)}, u32[]{:S(2)}, u32[]{:S(2)}) collective-permute-start(bf16[48,3584]{1,0:T(8,128)(2,1)S(1)} %get-tuple-element.76), channel_id=1, source_target_pairs={{0,2},{1,3},{2,0},{3,1},{4,6},{5,7},{6,4},{7,5},{8,10},{9,11},{10,... | collective-permute-start | bytes 1032200 | tf_op jit(solution)/shard_map/ppermute | solution.py:40
  106.7 10.5 %collective-permute-start.24 = (bf16[48,3584]{1,0:T(8,128)(2,1)S(1)}, bf16[48,3584]{1,0:T(8,128)(2,1)S(1)}, u32[]{:S(2)}, u32[]{:S(2)}) collective-permute-start(bf16[48,3584]{1,0:T(8,128)(2,1)S(1)} %get-tuple-element.111), channel_id=1, source_target_pairs={{0,1},{1,0},{2,3},{3,2},{4,5},{5,4},{6,7},{7,6},{8,9},{9,8},{10,11... | collective-permute-start | bytes 1032200 | tf_op jit(solution)/shard_map/ppermute | solution.py:40
  108.4 12.9 %collective-permute-start.22 = (bf16[48,3584]{1,0:T(8,128)(2,1)S(1)}, bf16[48,3584]{1,0:T(8,128)(2,1)S(1)}, u32[]{:S(2)}, u32[]{:S(2)}) collective-permute-start(bf16[48,3584]{1,0:T(8,128)(2,1)S(1)} %get-tuple-element.112), channel_id=1, source_target_pairs={{0,2},{1,3},{2,0},{3,1},{4,6},{5,7},{6,4},{7,5},{8,10},{9,11},{10,... | collective-permute-start | bytes 1032200 | tf_op jit(solution)/shard_map/ppermute | solution.py:40
  114.1 21.6 %collective-permute-start.29 = (bf16[96,3584]{1,0:T(8,128)(2,1)S(1)}, bf16[96,3584]{1,0:T(8,128)(2,1)S(1)}, u32[]{:S(2)}, u32[]{:S(2)}) collective-permute-start(bf16[96,3584]{1,0:T(8,128)(2,1)S(1)} %pad_maximum_fusion.12), channel_id=1, source_target_pairs={{0,2},{1,3},{2,0},{3,1},{4,6},{5,7},{6,4},{7,5},{8,10},{9,11},{10,... | collective-permute-start | bytes 2064392 | tf_op jit(solution)/shard_map/ppermute | solution.py:40
  115.8 19.9 %collective-permute-start.28 = (bf16[96,3584]{1,0:T(8,128)(2,1)S(1)}, bf16[96,3584]{1,0:T(8,128)(2,1)S(1)}, u32[]{:S(2)}, u32[]{:S(2)}) collective-permute-start(bf16[96,3584]{1,0:T(8,128)(2,1)S(1)} %pad_maximum_fusion.11), channel_id=1, source_target_pairs={{0,1},{1,0},{2,3},{3,2},{4,5},{5,4},{6,7},{7,6},{8,9},{9,8},{10,11... | collective-permute-start | bytes 2064392 | tf_op jit(solution)/shard_map/ppermute | solution.py:40
  135.9 17.9 %collective-permute-start.23 = (bf16[96,3584]{1,0:T(8,128)(2,1)S(1)}, bf16[96,3584]{1,0:T(8,128)(2,1)S(1)}, u32[]{:S(2)}, u32[]{:S(2)}) collective-permute-start(bf16[96,3584]{1,0:T(8,128)(2,1)S(1)} %pad_maximum_fusion.9), channel_id=1, source_target_pairs={{0,2},{1,3},{2,0},{3,1},{4,6},{5,7},{6,4},{7,5},{8,10},{9,11},{10,... | collective-permute-start | bytes 2064392 | tf_op jit(solution)/shard_map/ppermute | solution.py:40
  137.7 17.6 %collective-permute-start.25 = (bf16[96,3584]{1,0:T(8,128)(2,1)S(1)}, bf16[96,3584]{1,0:T(8,128)(2,1)S(1)}, u32[]{:S(2)}, u32[]{:S(2)}) collective-permute-start(bf16[96,3584]{1,0:T(8,128)(2,1)S(1)} %pad_maximum_fusion.10), channel_id=1, source_target_pairs={{0,1},{1,0},{2,3},{3,2},{4,5},{5,4},{6,7},{7,6},{8,9},{9,8},{10,11... | collective-permute-start | bytes 2064392 | tf_op jit(solution)/shard_map/ppermute | solution.py:40
  155.5 12.6 %collective-permute-start.35 = (bf16[2,5,48,512]{3,2,1,0:T(8,128)(2,1)S(1)}, bf16[2,5,48,512]{3,2,1,0:T(8,128)(2,1)S(1)}, u32[]{:S(2)}, u32[]{:S(2)}) collective-permute-start(bf16[2,5,48,512]{3,2,1,0:T(8,128)(2,1)S(1)} %pad_maximum_fusion.13), channel_id=1, source_target_pairs={{0,4},{4,0},{8,12},{12,8},{1,5},{5,1},{9,13},{13,9},{2,6},{6,2},{1... | collective-permute-start | bytes 1474568 | tf_op jit(solution)/shard_map/ppermute | solution.py:40
  157.5 31.3 %collective-permute-start.33 = (bf16[192,3584]{1,0:T(8,128)(2,1)S(1)}, bf16[192,3584]{1,0:T(8,128)(2,1)S(1)}, u32[]{:S(2)}, u32[]{:S(2)}) collective-permute-start(bf16[192,3584]{1,0:T(8,128)(2,1)S(1)} %pad_maximum_fusion.7), channel_id=1, source_target_pairs={{0,2},{1,3},{2,0},{3,1},{4,6},{5,7},{6,4},{7,5},{8,10},{9,11},{10,... | collective-permute-start | bytes 4128776 | tf_op jit(solution)/shard_map/ppermute | solution.py:40
  158.5 30.3 %collective-permute-start.34 = (bf16[192,3584]{1,0:T(8,128)(2,1)S(1)}, bf16[192,3584]{1,0:T(8,128)(2,1)S(1)}, u32[]{:S(2)}, u32[]{:S(2)}) collective-permute-start(bf16[192,3584]{1,0:T(8,128)(2,1)S(1)} %constant_dynamic-update-slice_fusion.38), channel_id=1, source_target_pairs={{0,16},{16,0},{1,17},{17,1},{2,18},{18,2},{3,19},{19,3},{4,20},{20... | collective-permute-start | bytes 4128776 | tf_op jit(solution)/shard_map/ppermute | solution.py:40
  158.5 32.6 %collective-permute-start.32 = (bf16[192,3584]{1,0:T(8,128)(2,1)S(1)}, bf16[192,3584]{1,0:T(8,128)(2,1)S(1)}, u32[]{:S(2)}, u32[]{:S(2)}) collective-permute-start(bf16[192,3584]{1,0:T(8,128)(2,1)S(1)} %pad_maximum_fusion.5), channel_id=1, source_target_pairs={{0,1},{1,0},{2,3},{3,2},{4,5},{5,4},{6,7},{7,6},{8,9},{9,8},{10,11... | collective-permute-start | bytes 4128776 | tf_op jit(solution)/shard_map/ppermute | solution.py:40
  168.5 12.6 %collective-permute-start.36 = (bf16[1,5,48,512]{3,2,1,0:T(8,128)(2,1)S(1)}, bf16[1,5,48,512]{3,2,1,0:T(8,128)(2,1)S(1)}, u32[]{:S(2)}, u32[]{:S(2)}) collective-permute-start(bf16[1,5,48,512]{3,2,1,0:T(8,128)(2,1)S(1)} %fusion.39), channel_id=1, source_target_pairs={{0,8},{4,12},{8,0},{12,4},{1,9},{5,13},{9,1},{13,5},{2,10},{6,14},... | collective-permute-start | bytes 737288 | tf_op jit(solution)/shard_map/ppermute | solution.py:40
  199.7 9.1 %collective-permute-start.38 = (bf16[2,3,48,512]{3,2,1,0:T(8,128)(2,1)S(1)}, bf16[2,3,48,512]{3,2,1,0:T(8,128)(2,1)S(1)}, u32[]{:S(2)}, u32[]{:S(2)}) collective-permute-start(bf16[2,3,48,512]{3,2,1,0:T(8,128)(2,1)S(1)} %pad_maximum_fusion.18), channel_id=1, source_target_pairs={{0,4},{4,0},{8,12},{12,8},{1,5},{5,1},{9,13},{13,9},{2,6},{6,2},{1... | collective-permute-start | bytes 884744 | tf_op jit(solution)/shard_map/ppermute | solution.py:40
  209.1 8.9 %collective-permute-start.39 = (bf16[1,3,48,512]{3,2,1,0:T(8,128)(2,1)S(1)}, bf16[1,3,48,512]{3,2,1,0:T(8,128)(2,1)S(1)}, u32[]{:S(2)}, u32[]{:S(2)}) collective-permute-start(bf16[1,3,48,512]{3,2,1,0:T(8,128)(2,1)S(1)} %dynamic-slice_convert_fusion), channel_id=1, source_target_pairs={{0,8},{4,12},{8,0},{12,4},{1,9},{5,13},{9,1},{13,5},{2,10},{6,14},... | collective-permute-start | bytes 442376 | tf_op jit(solution)/shard_map/ppermute | solution.py:40
  (16 other events, 95.5 us)

commit v3 on v2

--- a/solution.py
+++ b/solution.py
@@ -47,9 +47,10 @@
         def by_row(x):
             return [lax.dynamic_index_in_dim(x, r ^ i, 0, keepdims=False) for i in range(n_row)]
 
-        both = jnp.stack([tokens, cotangent])
-        own = [lax.dynamic_slice(both, (0, 0, (d ^ k) * feats), (2, n, feats)) for k in range(n_depth)]
-        own = jnp.stack([swap(x, "depth", k) if k else x for k, x in enumerate(own)], axis=1)
+        def gather_feats(x):
+            pieces = [lax.dynamic_slice(x, (0, 0, (d ^ k) * feats), (2, n, feats)) for k in range(n_depth)]
+            pieces = [swap(x, "depth", k) if k else x for k, x in enumerate(pieces)]
+            return [[x[i] for x in pieces] for i in range(2)]
 
         def more_cols(cols, k):
             got = swap(jnp.stack(list(cols.values())), "col", k)
@@ -59,8 +60,13 @@
             while k:
                 cols = more_cols(cols, k)
                 k //= 2
-            shares = [jnp.concatenate([cols[2 * h + a][k] for a, k in order]) for h in range(n_row)]
-            return by_row(jnp.stack(shares))
+            return cols
+
+        def shares(*parts):
+            by_h = [
+                jnp.concatenate([parts[k // 2][2 * h + a][k % 2] for a, k in order]) for h in range(n_row)
+            ]
+            return by_row(jnp.stack(by_h))
 
         def spread(shares):
             return [shares[0]] + [swap(shares[i], "row", i) for i in range(1, n_row)]
@@ -104,6 +110,11 @@
                 k *= 2
             return xs[0].astype(BF16)
 
+        def direct(a_blocks, b_blocks):
+            xs = [x for pair in zip(by_row(a_blocks), by_row(b_blocks)) for x in pair]
+            got = [swap(x.astype(BF16), "col", j).astype(F32) for j, x in enumerate(xs) if j]
+            return sum(got, xs[0]).astype(BF16)
+
         def place(*sums):
             outs = jnp.zeros((len(sums), n, feats * n_depth), BF16)
             for k in range(n_depth):
@@ -113,19 +124,24 @@
             return [outs[i] for i in range(len(sums))]
 
         gws, uws, dws = tiles(gate_weight), tiles(up_weight), tiles(down_weight)
-        tok = all_cols({0: own[0]}, n_col // 2)
-        cot_own, tok = barrier((own[1], tok))
+        far, near = n_col // 2, n_col // 4
+        tok_own, cot_own = gather_feats(jnp.stack([tokens, cotangent]))
+        tok_1, tok_2 = [more_cols({0: jnp.stack(tok_own[i : i + 2])}, far) for i in (0, 2)]
+        tok = shares(all_cols(tok_1, near), all_cols(tok_2, near))
+        cot_own = jnp.stack(cot_own)
+        cot_own, tok = barrier((cot_own, tok))
         tok_shares = spread(tok)
         tok_all = jnp.concatenate(tok).T
 
         gate_sent = part(tok_shares, gws, dot_nn, 4 * n, 8 * n).astype(BF16)
         gate_got = send_first(gate_sent)
-        cot_cols = more_cols({0: cot_own}, n_col // 2)
+        cot_cols = more_cols({0: cot_own}, far)
         tok_shares, gate_sent = barrier((tok_shares, gate_sent))
         up_sent = part(tok_shares, uws, dot_nn, 4 * n, 8 * n).astype(BF16)
         up_got = send_first(up_sent)
         tok_shares, cot_cols, gate_got, up_sent = barrier((tok_shares, cot_cols, gate_got, up_sent))
-        cot = all_cols(cot_cols, n_col // 4)
+        cot_cols = all_cols(cot_cols, near)
+        cot = shares({j: x[:2] for j, x in cot_cols.items()}, {j: x[2:] for j, x in cot_cols.items()})
         gate_keep = part(tok_shares, gws, dot_nn, 0, 4 * n)
         a2, b1 = second(gate_keep, *gate_got)
         gate_last = swap(a2, "depth", 2), swap(b1, "depth", 1)
@@ -165,16 +181,16 @@
         h_from_x, h_from_y, early = barrier((h_from_x, h_from_y, early))
         hid_rows = gather_row(h_a0, h_b0, h_a2, h_b1, h_from_x, h_from_y)
         out = jnp.stack([dot_nn(x, down_weight) for x in hid_rows]).reshape(n_row, 8, n, feats)
-        got = cross(jnp.concatenate([jnp.stack([out[:, i] for i in (1, 3, 6, 7)], axis=1), early[:, 1:]], axis=1))
-        hid_rows, cot, out = barrier((hid_rows, cot, out))
-        down_grad = dot_tn(jnp.concatenate(hid_rows), jnp.concatenate(cot))
-
-        d_a2, d_b1, down_grad = barrier((d_a2, d_b1, down_grad))
+        d_a2, d_b1, out = barrier((d_a2, d_b1, out))
         from_x = swap(jnp.concatenate([d_a0, d_a2]), "depth", 1)
         from_y = swap(jnp.concatenate([d_b0, d_b1]), "depth", 2)
         middle = gather_row(d_a2, d_b1)
-        z_out = jnp.stack([out[:, i] for i in (0, 4, 2, 5)], axis=1) + got[:, :4]
-        done = finish(jnp.concatenate([z_out, early[:, :1] + got[:, 4:]], axis=1))
+        hid_rows, cot, out, middle = barrier((hid_rows, cot, out, middle))
+        done = direct(
+            jnp.concatenate([jnp.stack([out[:, i] for i in (0, 4, 2, 5)], axis=1), early[:, :1]], axis=1),
+            jnp.concatenate([jnp.stack([out[:, i] for i in (1, 3, 6, 7)], axis=1), early[:, 1:]], axis=1),
+        )
+        down_grad = dot_tn(jnp.concatenate(hid_rows), jnp.concatenate(cot))
         from_x, from_y, middle, done = barrier((from_x, from_y, middle, done))
         late = [jnp.concatenate(x) for x in zip(middle, gather_row(from_x, from_y))]
         gd_l, ud_l, late = back(late)

time: 227 us -> 222 us (0.978)
  waiting for transfers between devices: 117 us -> 112 us
    ppermute x43 -> x46, waiting for transfers between devices: 117 us -> 112 us  [swap(): return lax.ppermute(x, axis, [(i, i ^ k) for i in range(n)])]
    ppermute x43 -> x46, starting transfers between devices: 48.9 us -> 48.5 us  [swap(): return lax.ppermute(x, axis, [(i, i ^ k) for i in range(n)])]
  transfers between devices with their start and end apart: 43 -> 46, of which waited for: 29 -> 31; matrix products, arithmetic and copies ran while one was open for 24% -> 24% of each run, Pallas kernels for 0% -> 0%
where the time goes in v3:
time: 222 us
  waiting for transfers between devices  112 us (50%)
  matrix products  49.6 us (22%)
  starting transfers between devices  48.5 us (22%)
  other arithmetic  7.14 us (3%)
  local copies, waits for them, and re-layouts  2.72 us (1%)
    ppermute x46, waiting for transfers between devices, swap(): return lax.ppermute(x, axis, [(i, i ^ k) for i in range(n)])  112 us
    ppermute x46, starting transfers between devices, swap(): return lax.ppermute(x, axis, [(i, i ^ k) for i in range(n)])  48.5 us
    dot_general x12, matrix products, dot_nn(): return jnp.dot(left, right, preferred_element_type=F32)  29 us
    dot_general x12, matrix products, dot_nt(): lax.dot_general(left, right, (((1,), (1,)), ((), ())), preferred_element_...  15.4 us
    dot_general x1, matrix products, dot_tn(): lax.dot_general(left, right, (((0,), (0,)), ((), ())), preferred_element_...  5.14 us
  transfers between devices with their start and end apart: 46, of which 31 were waited for; matrix products, arithmetic and copies ran while one was open for 24% of the time, Pallas kernels for 0%

profile of v3, /device:TPU:0, one launch (start us, length us, event | category | flops | bytes accessed | tf_op | source)
XLA Modules:
  0.0 222.0 jit_solution(12700373178063352417)
XLA Ops:
  1.7 3.0 %collective-permute-start = (bf16[2,48,512]{2,1,0:T(8,128)(2,1)S(1)}, bf16[2,48,512]{2,1,0:T(8,128)(2,1)S(1)}, u32[]{:S(2)}, u32[]{:S(2)}) collective-permute-start(bf16[2,48,512]{2,1,0:T(8,128)(2,1)S(1)} %get-tuple-element.153), channel_id=1, source_target_pairs={{0,1},{1,0},{2,3},{3,2},{4,5},{5,4},{6,7},{7,6},{8,9},{9,8},{10,11... | collective-permute-start | bytes 294920 | tf_op jit(solution)/shard_map/ppermute | solution.py:40
  7.8 2.7 %collective-permute-start.3 = (bf16[1,2,48,512]{3,2,1,0:T(8,128)(2,1)S(1)}, bf16[1,2,48,512]{3,2,1,0:T(8,128)(2,1)S(1)}, u32[]{:S(2)}, u32[]{:S(2)}) collective-permute-start(bf16[1,2,48,512]{3,2,1,0:T(8,128)(2,1)S(1)} %maximum_bitcast_fusion.1), channel_id=1, source_target_pairs={{0,8},{4,12},{8,0},{12,4},{1,9},{5,13},{9,1},{13,5},{2,10},{6,14},... | collective-permute-start | bytes 294920 | tf_op jit(solution)/shard_map/ppermute | solution.py:40
  11.7 2.7 %collective-permute-start.5 = (bf16[1,2,48,512]{3,2,1,0:T(8,128)(2,1)S(1)}, bf16[1,2,48,512]{3,2,1,0:T(8,128)(2,1)S(1)}, u32[]{:S(2)}, u32[]{:S(2)}) collective-permute-start(bf16[1,2,48,512]{3,2,1,0:T(8,128)(2,1)S(1)} %maximum_bitcast_fusion.2), channel_id=1, source_target_pairs={{0,8},{4,12},{8,0},{12,4},{1,9},{5,13},{9,1},{13,5},{2,10},{6,14},... | collective-permute-start | bytes 294920 | tf_op jit(solution)/shard_map/ppermute | solution.py:40
  14.4 4.8 %collective-permute-done.5 = bf16[1,2,48,512]{3,2,1,0:T(8,128)(2,1)S(1)} collective-permute-done((bf16[1,2,48,512]{3,2,1,0:T(8,128)(2,1)S(1)}, bf16[1,2,48,512]{3,2,1,0:T(8,128)(2,1)S(1)}, u32[]{:S(2)}, u32[]{:S(2)}) %collective-permute-start.5) | collective-permute-done | bytes 98336 | tf_op jit(solution)/shard_map/ppermute | solution.py:40
  21.4 8.5 %collective-permute-done.4 = bf16[2,2,48,512]{3,2,1,0:T(8,128)(2,1)S(1)} collective-permute-done((bf16[2,2,48,512]{3,2,1,0:T(8,128)(2,1)S(1)}, bf16[2,2,48,512]{3,2,1,0:T(8,128)(2,1)S(1)}, u32[]{:S(2)}, u32[]{:S(2)}) %collective-permute-start.4) | collective-permute-done | bytes 196640 | tf_op jit(solution)/shard_map/ppermute | solution.py:40
  30.9 2.4 %collective-permute-start.12 = (bf16[1,4,48,512]{3,2,1,0:T(8,128)(2,1)S(1)}, bf16[1,4,48,512]{3,2,1,0:T(8,128)(2,1)S(1)}, u32[]{:S(2)}, u32[]{:S(2)}) collective-permute-start(bf16[1,4,48,512]{3,2,1,0:T(8,128)(2,1)S(1)} %bitcast.223), channel_id=1, source_target_pairs={{0,8},{4,12},{8,0},{12,4},{1,9},{5,13},{9,1},{13,5},{2,10},{6,14},... | collective-permute-start | bytes 589832 | tf_op jit(solution)/shard_map/ppermute | solution.py:40
  34.2 2.9 %fusion.20 = bf16[192,3584]{1,0:T(8,128)(2,1)S(1)} fusion(f32[192,3584]{1,0:T(8,128)S(1)} %fusion.68, bf16[512,3584]{1,0:T(8,128)(2,1)} %collective-permute-done.8, bf16[384,512]{1,0:T(8,128)(2,1)S(1)} %collective-permute-done.7), kind=kOutput, calls=%fused_computation.26 | convolution fusion | flops 706019328 | bytes 7995392 | tf_op jit(solution)/shard_map/dot_general | solution.py:10
  40.0 2.9 %fusion.65 = f32[192,3584]{1,0:T(8,128)S(1)} fusion(bf16[512,3584]{1,0:T(8,128)(2,1)} %collective-permute-done.9, bf16[384,512]{1,0:T(8,128)(2,1)S(1)} %collective-permute-done.7), kind=kOutput, calls=%fused_computation.146 | convolution fusion | flops 704643072 | bytes 6619136 | tf_op jit(solution)/shard_map/dot_general | solution.py:10
  45.7 10.0 %collective-permute-done.14 = bf16[96,3584]{1,0:T(8,128)(2,1)S(1)} collective-permute-done((bf16[96,3584]{1,0:T(8,128)(2,1)S(1)}, bf16[96,3584]{1,0:T(8,128)(2,1)S(1)}, u32[]{:S(2)}, u32[]{:S(2)}) %collective-permute-start.14) | collective-permute-done | bytes 688160 | tf_op jit(solution)/shard_map/ppermute | solution.py:40
  57.2 1.8 collective-permute-start.15
  59.0 2.9 %fusion.62 = f32[192,3584]{1,0:T(8,128)S(1)} fusion(bf16[512,3584]{1,0:T(8,128)(2,1)} %collective-permute-done.8, bf16[384,512]{1,0:T(8,128)(2,1)S(1)} %collective-permute-done.7), kind=kOutput, calls=%fused_computation.143 | convolution fusion | flops 704643072 | bytes 6619136 | tf_op jit(solution)/shard_map/dot_general | solution.py:10
  66.9 3.2 %convolution_add_fusion.1 = f32[192,3584]{1,0:T(8,128)S(1)} fusion(f32[192,3584]{1,0:T(8,128)S(1)} %fusion.58, bf16[512,3584]{1,0:T(8,128)(2,1)} %collective-permute-done.9, bf16[384,512]{1,0:T(8,128)(2,1)S(1)} %collective-permute-done.7), kind=kOutput, calls=%fused_computation.21 | convolution fusion | flops 705331200 | bytes 9371648 | tf_op jit(solution)/shard_map/dot_general | solution.py:10
  82.3 4.0 %collective-permute-done.23 = bf16[48,3584]{1,0:T(8,128)(2,1)S(1)} collective-permute-done((bf16[48,3584]{1,0:T(8,128)(2,1)S(1)}, bf16[48,3584]{1,0:T(8,128)(2,1)S(1)}, u32[]{:S(2)}, u32[]{:S(2)}) %collective-permute-start.23) | collective-permute-done | bytes 344096 | tf_op jit(solution)/shard_map/ppermute | solution.py:40
  86.3 3.4 %collective-permute-done.21 = bf16[48,3584]{1,0:T(8,128)(2,1)S(1)} collective-permute-done((bf16[48,3584]{1,0:T(8,128)(2,1)S(1)}, bf16[48,3584]{1,0:T(8,128)(2,1)S(1)}, u32[]{:S(2)}, u32[]{:S(2)}) %collective-permute-start.21) | collective-permute-done | bytes 344096 | tf_op jit(solution)/shard_map/ppermute | solution.py:40
  92.4 12.0 %collective-permute-done.19 = bf16[96,3584]{1,0:T(8,128)(2,1)S(1)} collective-permute-done((bf16[96,3584]{1,0:T(8,128)(2,1)S(1)}, bf16[96,3584]{1,0:T(8,128)(2,1)S(1)}, u32[]{:S(2)}, u32[]{:S(2)}) %collective-permute-start.19) | collective-permute-done | bytes 688160 | tf_op jit(solution)/shard_map/ppermute | solution.py:40
  107.9 3.9 %collective-permute-done.28 = bf16[48,3584]{1,0:T(8,128)(2,1)S(1)} collective-permute-done((bf16[48,3584]{1,0:T(8,128)(2,1)S(1)}, bf16[48,3584]{1,0:T(8,128)(2,1)S(1)}, u32[]{:S(2)}, u32[]{:S(2)}) %collective-permute-start.28) | collective-permute-done | bytes 344096 | tf_op jit(solution)/shard_map/ppermute | solution.py:40
  115.0 4.2 %collective-permute-done.24 = bf16[48,3584]{1,0:T(8,128)(2,1)S(1)} collective-permute-done((bf16[48,3584]{1,0:T(8,128)(2,1)S(1)}, bf16[48,3584]{1,0:T(8,128)(2,1)S(1)}, u32[]{:S(2)}, u32[]{:S(2)}) %collective-permute-start.24) | collective-permute-done | bytes 344096 | tf_op jit(solution)/shard_map/ppermute | solution.py:40
  127.0 6.5 %collective-permute-done.31 = bf16[96,3584]{1,0:T(8,128)(2,1)S(1)} collective-permute-done((bf16[96,3584]{1,0:T(8,128)(2,1)S(1)}, bf16[96,3584]{1,0:T(8,128)(2,1)S(1)}, u32[]{:S(2)}, u32[]{:S(2)}) %collective-permute-start.31) | collective-permute-done | bytes 688160 | tf_op jit(solution)/shard_map/ppermute | solution.py:40
  140.6 11.1 %collective-permute-done.25 = bf16[96,3584]{1,0:T(8,128)(2,1)S(1)} collective-permute-done((bf16[96,3584]{1,0:T(8,128)(2,1)S(1)}, bf16[96,3584]{1,0:T(8,128)(2,1)S(1)}, u32[]{:S(2)}, u32[]{:S(2)}) %collective-permute-start.25) | collective-permute-done | bytes 688160 | tf_op jit(solution)/shard_map/ppermute | solution.py:40
  155.6 1.8 collective-permute-start.37
  159.4 5.1 %fusion.16 = f32[3584,512]{1,0:T(8,128)} fusion(bf16[384,3584]{1,0:T(8,128)(2,1)S(1)} %copy-done.6, bf16[384,3584]{1,0:T(8,128)(2,1)S(1)} %copy-done.4, bf16[384,512]{1,0:T(8,128)(2,1)S(1)} %get-tuple-element.104, bf16[384,512]{1,0:T(8,128)(2,1)S(1)} %get-tuple-element.103), kind=kOutput, calls=%fused_computation.16 | convolution fusion | flops 2831155200 | bytes 13631488 | tf_op jit(solution)/shard_map/dot_general | solution.py:14
  164.5 5.8 %collective-permute-done.39 = bf16[5,48,512]{2,1,0:T(8,128)(2,1)S(1)} collective-permute-done((bf16[5,48,512]{2,1,0:T(8,128)(2,1)S(1)}, bf16[5,48,512]{2,1,0:T(8,128)(2,1)S(1)}, u32[]{:S(2)}, u32[]{:S(2)}) %collective-permute-start.39) | collective-permute-done | bytes 245792 | tf_op jit(solution)/shard_map/ppermute | solution.py:40
  170.3 10.4 %collective-permute-done.38 = bf16[5,48,512]{2,1,0:T(8,128)(2,1)S(1)} collective-permute-done((bf16[5,48,512]{2,1,0:T(8,128)(2,1)S(1)}, bf16[5,48,512]{2,1,0:T(8,128)(2,1)S(1)}, u32[]{:S(2)}, u32[]{:S(2)}) %collective-permute-start.38) | collective-permute-done | bytes 245792 | tf_op jit(solution)/shard_map/ppermute | solution.py:40
  180.9 4.2 %collective-permute-done.35 = bf16[192,3584]{1,0:T(8,128)(2,1)S(1)} collective-permute-done((bf16[192,3584]{1,0:T(8,128)(2,1)S(1)}, bf16[192,3584]{1,0:T(8,128)(2,1)S(1)}, u32[]{:S(2)}, u32[]{:S(2)}) %collective-permute-start.35) | collective-permute-done | bytes 1376288 | tf_op jit(solution)/shard_map/ppermute | solution.py:40
  190.0 1.8 collective-permute-done.40
  195.1 1.8 collective-permute-start.41
  196.9 5.2 %fusion = f32[512,3584]{1,0:T(8,128)} fusion(bf16[512,768]{0,1:T(8,128)(2,1)S(1)} %maximum_bitcast_fusion, bf16[288,3584]{1,0:T(8,128)(2,1)S(1)} %bitcast.222, bf16[96,3584]{1,0:T(8,128)(2,1)S(1)} %bitcast.214, bf16[288,3584]{1,0:T(8,128)(2,1)S(1)} %bitcast.220, bf16[96,3584]{1,0:T(8,128)(2,1)S(1)} %bitcast.212), kind=kOutput, calls=%fused_computation | convolution fusion | flops 2840592384 | bytes 13631488 | tf_op jit(solution)/shard_map/dot_general | solution.py:10
  202.1 2.1 collective-permute-done.41
  205.5 5.1 %fusion.8 = f32[512,3584]{1,0:T(8,128)} fusion(bf16[512,768]{0,1:T(8,128)(2,1)S(1)} %maximum_bitcast_fusion, bf16[288,3584]{1,0:T(8,128)(2,1)S(1)} %bitcast.218, bf16[96,3584]{1,0:T(8,128)(2,1)S(1)} %bitcast.210, bf16[288,3584]{1,0:T(8,128)(2,1)S(1)} %bitcast.216, bf16[96,3584]{1,0:T(8,128)(2,1)S(1)} %bitcast.208), kind=kOutput, calls=%fused_computation.8 | convolution fusion | flops 2840592384 | bytes 13631488 | tf_op jit(solution)/shard_map/dot_general | solution.py:10
  210.7 3.0 %collective-permute-done.42 = bf16[1,3,48,512]{3,2,1,0:T(8,128)(2,1)S(1)} collective-permute-done((bf16[1,3,48,512]{3,2,1,0:T(8,128)(2,1)S(1)}, bf16[1,3,48,512]{3,2,1,0:T(8,128)(2,1)S(1)}, u32[]{:S(2)}, u32[]{:S(2)}) %collective-permute-start.42) | collective-permute-done | bytes 147488 | tf_op jit(solution)/shard_map/ppermute | solution.py:40
  215.6 1.8 collective-permute-start.45
  217.4 2.0 collective-permute-done.43
  (202 shorter events, 77.4 us)
Async XLA Ops:
  6.2 28.0 %collective-permute-start.8 = (bf16[512,3584]{1,0:T(8,128)(2,1)}, bf16[512,3584]{1,0:T(8,128)(2,1)}, u32[]{:S(2)}, u32[]{:S(2)}) collective-permute-start(bf16[512,3584]{1,0:T(8,128)(2,1)} %param.7), channel_id=1, source_target_pairs={{0,16},{16,0},{1,17},{17,1},{2,18},{18,2},{3,19},{19,3},{4,20},{20... | collective-permute-start | bytes 11010056 | tf_op jit(solution)/shard_map/ppermute | solution.py:40
  6.2 33.8 %collective-permute-start.9 = (bf16[512,3584]{1,0:T(8,128)(2,1)}, bf16[512,3584]{1,0:T(8,128)(2,1)}, u32[]{:S(2)}, u32[]{:S(2)}) collective-permute-start(bf16[512,3584]{1,0:T(8,128)(2,1)} %param.8), channel_id=1, source_target_pairs={{0,16},{16,0},{1,17},{17,1},{2,18},{18,2},{3,19},{19,3},{4,20},{20... | collective-permute-start | bytes 11010056 | tf_op jit(solution)/shard_map/ppermute | solution.py:40
  7.8 12.3 %collective-permute-start.3 = (bf16[1,2,48,512]{3,2,1,0:T(8,128)(2,1)S(1)}, bf16[1,2,48,512]{3,2,1,0:T(8,128)(2,1)S(1)}, u32[]{:S(2)}, u32[]{:S(2)}) collective-permute-start(bf16[1,2,48,512]{3,2,1,0:T(8,128)(2,1)S(1)} %maximum_bitcast_fusion.1), channel_id=1, source_target_pairs={{0,8},{4,12},{8,0},{12,4},{1,9},{5,13},{9,1},{13,5},{2,10},{6,14},... | collective-permute-start | bytes 294920 | tf_op jit(solution)/shard_map/ppermute | solution.py:40
  19.2 10.7 %collective-permute-start.6 = (bf16[2,2,48,512]{3,2,1,0:T(8,128)(2,1)S(1)}, bf16[2,2,48,512]{3,2,1,0:T(8,128)(2,1)S(1)}, u32[]{:S(2)}, u32[]{:S(2)}) collective-permute-start(bf16[2,2,48,512]{3,2,1,0:T(8,128)(2,1)S(1)} %pad_maximum_fusion.19), channel_id=1, source_target_pairs={{0,4},{4,0},{8,12},{12,8},{1,5},{5,1},{9,13},{13,9},{2,6},{6,2},{1... | collective-permute-start | bytes 589832 | tf_op jit(solution)/shard_map/ppermute | solution.py:40
  20.1 9.8 %collective-permute-start.4 = (bf16[2,2,48,512]{3,2,1,0:T(8,128)(2,1)S(1)}, bf16[2,2,48,512]{3,2,1,0:T(8,128)(2,1)S(1)}, u32[]{:S(2)}, u32[]{:S(2)}) collective-permute-start(bf16[2,2,48,512]{3,2,1,0:T(8,128)(2,1)S(1)} %pad_maximum_fusion.18), channel_id=1, source_target_pairs={{0,4},{4,0},{8,12},{12,8},{1,5},{5,1},{9,13},{13,9},{2,6},{6,2},{1... | collective-permute-start | bytes 589832 | tf_op jit(solution)/shard_map/ppermute | solution.py:40
  30.4 40.9 %collective-permute-start.17 = (bf16[3584,512]{1,0:T(8,128)(2,1)}, bf16[3584,512]{1,0:T(8,128)(2,1)S(1)}, u32[]{:S(2)}, u32[]{:S(2)}) collective-permute-start(bf16[3584,512]{1,0:T(8,128)(2,1)} %param.9), channel_id=1, source_target_pairs={{0,16},{16,0},{1,17},{17,1},{2,18},{18,2},{3,19},{19,3},{4,20},{20... | collective-permute-start | bytes 11010056 | tf_op jit(solution)/shard_map/ppermute | solution.py:40
  30.9 13.6 %collective-permute-start.12 = (bf16[1,4,48,512]{3,2,1,0:T(8,128)(2,1)S(1)}, bf16[1,4,48,512]{3,2,1,0:T(8,128)(2,1)S(1)}, u32[]{:S(2)}, u32[]{:S(2)}) collective-permute-start(bf16[1,4,48,512]{3,2,1,0:T(8,128)(2,1)S(1)} %bitcast.223), channel_id=1, source_target_pairs={{0,8},{4,12},{8,0},{12,4},{1,9},{5,13},{9,1},{13,5},{2,10},{6,14},... | collective-permute-start | bytes 589832 | tf_op jit(solution)/shard_map/ppermute | solution.py:40
  37.2 18.4 %collective-permute-start.14 = (bf16[96,3584]{1,0:T(8,128)(2,1)S(1)}, bf16[96,3584]{1,0:T(8,128)(2,1)S(1)}, u32[]{:S(2)}, u32[]{:S(2)}) collective-permute-start(bf16[96,3584]{1,0:T(8,128)(2,1)S(1)} %get-tuple-element.129), channel_id=1, source_target_pairs={{0,2},{1,3},{2,0},{3,1},{4,6},{5,7},{6,4},{7,5},{8,10},{9,11},{10,... | collective-permute-start | bytes 2064392 | tf_op jit(solution)/shard_map/ppermute | solution.py:40
  38.8 18.4 %collective-permute-start.13 = (bf16[96,3584]{1,0:T(8,128)(2,1)S(1)}, bf16[96,3584]{1,0:T(8,128)(2,1)S(1)}, u32[]{:S(2)}, u32[]{:S(2)}) collective-permute-start(bf16[96,3584]{1,0:T(8,128)(2,1)S(1)} %get-tuple-element.130), channel_id=1, source_target_pairs={{0,1},{1,0},{2,3},{3,2},{4,5},{5,4},{6,7},{7,6},{8,9},{9,8},{10,11... | collective-permute-start | bytes 2064392 | tf_op jit(solution)/shard_map/ppermute | solution.py:40
  44.0 29.6 %collective-permute-start.11 = (bf16[96,3584]{1,0:T(8,128)(2,1)S(1)}, bf16[96,3584]{1,0:T(8,128)(2,1)S(1)}, u32[]{:S(2)}, u32[]{:S(2)}) collective-permute-start(bf16[96,3584]{1,0:T(8,128)(2,1)S(1)} %get-tuple-element.131), channel_id=1, source_target_pairs={{0,2},{1,3},{2,0},{3,1},{4,6},{5,7},{6,4},{7,5},{8,10},{9,11},{10,... | collective-permute-start | bytes 2064392 | tf_op jit(solution)/shard_map/ppermute | solution.py:40
  44.6 29.0 %collective-permute-start.10 = (bf16[96,3584]{1,0:T(8,128)(2,1)S(1)}, bf16[96,3584]{1,0:T(8,128)(2,1)S(1)}, u32[]{:S(2)}, u32[]{:S(2)}) collective-permute-start(bf16[96,3584]{1,0:T(8,128)(2,1)S(1)} %get-tuple-element.132), channel_id=1, source_target_pairs={{0,1},{1,0},{2,3},{3,2},{4,5},{5,4},{6,7},{7,6},{8,9},{9,8},{10,11... | collective-permute-start | bytes 2064392 | tf_op jit(solution)/shard_map/ppermute | solution.py:40
  63.1 16.7 %collective-permute-start.22 = (bf16[48,3584]{1,0:T(8,128)(2,1)S(1)}, bf16[48,3584]{1,0:T(8,128)(2,1)S(1)}, u32[]{:S(2)}, u32[]{:S(2)}) collective-permute-start(bf16[48,3584]{1,0:T(8,128)(2,1)S(1)} %get-tuple-element.119), channel_id=1, source_target_pairs={{0,1},{1,0},{2,3},{3,2},{4,5},{5,4},{6,7},{7,6},{8,9},{9,8},{10,11... | collective-permute-start | bytes 1032200 | tf_op jit(solution)/shard_map/ppermute | solution.py:40
  71.4 10.9 %collective-permute-start.20 = (bf16[48,3584]{1,0:T(8,128)(2,1)S(1)}, bf16[48,3584]{1,0:T(8,128)(2,1)S(1)}, u32[]{:S(2)}, u32[]{:S(2)}) collective-permute-start(bf16[48,3584]{1,0:T(8,128)(2,1)S(1)} %get-tuple-element.120), channel_id=1, source_target_pairs={{0,2},{1,3},{2,0},{3,1},{4,6},{5,7},{6,4},{7,5},{8,10},{9,11},{10,... | collective-permute-start | bytes 1032200 | tf_op jit(solution)/shard_map/ppermute | solution.py:40
  73.8 12.5 %collective-permute-start.23 = (bf16[48,3584]{1,0:T(8,128)(2,1)S(1)}, bf16[48,3584]{1,0:T(8,128)(2,1)S(1)}, u32[]{:S(2)}, u32[]{:S(2)}) collective-permute-start(bf16[48,3584]{1,0:T(8,128)(2,1)S(1)} %get-tuple-element.117), channel_id=1, source_target_pairs={{0,1},{1,0},{2,3},{3,2},{4,5},{5,4},{6,7},{7,6},{8,9},{9,8},{10,11... | collective-permute-start | bytes 1032200 | tf_op jit(solution)/shard_map/ppermute | solution.py:40
  75.0 14.7 %collective-permute-start.21 = (bf16[48,3584]{1,0:T(8,128)(2,1)S(1)}, bf16[48,3584]{1,0:T(8,128)(2,1)S(1)}, u32[]{:S(2)}, u32[]{:S(2)}) collective-permute-start(bf16[48,3584]{1,0:T(8,128)(2,1)S(1)} %get-tuple-element.118), channel_id=1, source_target_pairs={{0,2},{1,3},{2,0},{3,1},{4,6},{5,7},{6,4},{7,5},{8,10},{9,11},{10,... | collective-permute-start | bytes 1032200 | tf_op jit(solution)/shard_map/ppermute | solution.py:40
  76.4 28.0 %collective-permute-start.19 = (bf16[96,3584]{1,0:T(8,128)(2,1)S(1)}, bf16[96,3584]{1,0:T(8,128)(2,1)S(1)}, u32[]{:S(2)}, u32[]{:S(2)}) collective-permute-start(bf16[96,3584]{1,0:T(8,128)(2,1)S(1)} %get-tuple-element.127), channel_id=1, source_target_pairs={{0,2},{1,3},{2,0},{3,1},{4,6},{5,7},{6,4},{7,5},{8,10},{9,11},{10,... | collective-permute-start | bytes 2064392 | tf_op jit(solution)/shard_map/ppermute | solution.py:40
  79.8 24.6 %collective-permute-start.18 = (bf16[96,3584]{1,0:T(8,128)(2,1)S(1)}, bf16[96,3584]{1,0:T(8,128)(2,1)S(1)}, u32[]{:S(2)}, u32[]{:S(2)}) collective-permute-start(bf16[96,3584]{1,0:T(8,128)(2,1)S(1)} %get-tuple-element.128), channel_id=1, source_target_pairs={{0,1},{1,0},{2,3},{3,2},{4,5},{5,4},{6,7},{7,6},{8,9},{9,8},{10,11... | collective-permute-start | bytes 2064392 | tf_op jit(solution)/shard_map/ppermute | solution.py:40
  90.6 17.4 %collective-permute-start.29 = (bf16[48,3584]{1,0:T(8,128)(2,1)S(1)}, bf16[48,3584]{1,0:T(8,128)(2,1)S(1)}, u32[]{:S(2)}, u32[]{:S(2)}) collective-permute-start(bf16[48,3584]{1,0:T(8,128)(2,1)S(1)} %get-tuple-element.79), channel_id=1, source_target_pairs={{0,1},{1,0},{2,3},{3,2},{4,5},{5,4},{6,7},{7,6},{8,9},{9,8},{10,11... | collective-permute-start | bytes 1032200 | tf_op jit(solution)/shard_map/ppermute | solution.py:40
  91.8 20.0 %collective-permute-start.28 = (bf16[48,3584]{1,0:T(8,128)(2,1)S(1)}, bf16[48,3584]{1,0:T(8,128)(2,1)S(1)}, u32[]{:S(2)}, u32[]{:S(2)}) collective-permute-start(bf16[48,3584]{1,0:T(8,128)(2,1)S(1)} %get-tuple-element.78), channel_id=1, source_target_pairs={{0,2},{1,3},{2,0},{3,1},{4,6},{5,7},{6,4},{7,5},{8,10},{9,11},{10,... | collective-permute-start | bytes 1032200 | tf_op jit(solution)/shard_map/ppermute | solution.py:40
  104.6 10.4 %collective-permute-start.26 = (bf16[48,3584]{1,0:T(8,128)(2,1)S(1)}, bf16[48,3584]{1,0:T(8,128)(2,1)S(1)}, u32[]{:S(2)}, u32[]{:S(2)}) collective-permute-start(bf16[48,3584]{1,0:T(8,128)(2,1)S(1)} %get-tuple-element.115), channel_id=1, source_target_pairs={{0,1},{1,0},{2,3},{3,2},{4,5},{5,4},{6,7},{7,6},{8,9},{9,8},{10,11... | collective-permute-start | bytes 1032200 | tf_op jit(solution)/shard_map/ppermute | solution.py:40
  105.8 13.3 %collective-permute-start.24 = (bf16[48,3584]{1,0:T(8,128)(2,1)S(1)}, bf16[48,3584]{1,0:T(8,128)(2,1)S(1)}, u32[]{:S(2)}, u32[]{:S(2)}) collective-permute-start(bf16[48,3584]{1,0:T(8,128)(2,1)S(1)} %get-tuple-element.116), channel_id=1, source_target_pairs={{0,2},{1,3},{2,0},{3,1},{4,6},{5,7},{6,4},{7,5},{8,10},{9,11},{10,... | collective-permute-start | bytes 1032200 | tf_op jit(solution)/shard_map/ppermute | solution.py:40
  112.0 21.6 %collective-permute-start.31 = (bf16[96,3584]{1,0:T(8,128)(2,1)S(1)}, bf16[96,3584]{1,0:T(8,128)(2,1)S(1)}, u32[]{:S(2)}, u32[]{:S(2)}) collective-permute-start(bf16[96,3584]{1,0:T(8,128)(2,1)S(1)} %pad_maximum_fusion.13), channel_id=1, source_target_pairs={{0,2},{1,3},{2,0},{3,1},{4,6},{5,7},{6,4},{7,5},{8,10},{9,11},{10,... | collective-permute-start | bytes 2064392 | tf_op jit(solution)/shard_map/ppermute | solution.py:40
  112.6 20.9 %collective-permute-start.30 = (bf16[96,3584]{1,0:T(8,128)(2,1)S(1)}, bf16[96,3584]{1,0:T(8,128)(2,1)S(1)}, u32[]{:S(2)}, u32[]{:S(2)}) collective-permute-start(bf16[96,3584]{1,0:T(8,128)(2,1)S(1)} %pad_maximum_fusion.12), channel_id=1, source_target_pairs={{0,1},{1,0},{2,3},{3,2},{4,5},{5,4},{6,7},{7,6},{8,9},{9,8},{10,11... | collective-permute-start | bytes 2064392 | tf_op jit(solution)/shard_map/ppermute | solution.py:40
  133.8 17.9 %collective-permute-start.25 = (bf16[96,3584]{1,0:T(8,128)(2,1)S(1)}, bf16[96,3584]{1,0:T(8,128)(2,1)S(1)}, u32[]{:S(2)}, u32[]{:S(2)}) collective-permute-start(bf16[96,3584]{1,0:T(8,128)(2,1)S(1)} %pad_maximum_fusion.10), channel_id=1, source_target_pairs={{0,2},{1,3},{2,0},{3,1},{4,6},{5,7},{6,4},{7,5},{8,10},{9,11},{10,... | collective-permute-start | bytes 2064392 | tf_op jit(solution)/shard_map/ppermute | solution.py:40
  134.5 17.6 %collective-permute-start.27 = (bf16[96,3584]{1,0:T(8,128)(2,1)S(1)}, bf16[96,3584]{1,0:T(8,128)(2,1)S(1)}, u32[]{:S(2)}, u32[]{:S(2)}) collective-permute-start(bf16[96,3584]{1,0:T(8,128)(2,1)S(1)} %pad_maximum_fusion.11), channel_id=1, source_target_pairs={{0,1},{1,0},{2,3},{3,2},{4,5},{5,4},{6,7},{7,6},{8,9},{9,8},{10,11... | collective-permute-start | bytes 2064392 | tf_op jit(solution)/shard_map/ppermute | solution.py:40
  152.5 32.6 %collective-permute-start.35 = (bf16[192,3584]{1,0:T(8,128)(2,1)S(1)}, bf16[192,3584]{1,0:T(8,128)(2,1)S(1)}, u32[]{:S(2)}, u32[]{:S(2)}) collective-permute-start(bf16[192,3584]{1,0:T(8,128)(2,1)S(1)} %pad_maximum_fusion.7), channel_id=1, source_target_pairs={{0,2},{1,3},{2,0},{3,1},{4,6},{5,7},{6,4},{7,5},{8,10},{9,11},{10,... | collective-permute-start | bytes 4128776 | tf_op jit(solution)/shard_map/ppermute | solution.py:40
  154.1 32.4 %collective-permute-start.34 = (bf16[192,3584]{1,0:T(8,128)(2,1)S(1)}, bf16[192,3584]{1,0:T(8,128)(2,1)S(1)}, u32[]{:S(2)}, u32[]{:S(2)}) collective-permute-start(bf16[192,3584]{1,0:T(8,128)(2,1)S(1)} %pad_maximum_fusion.5), channel_id=1, source_target_pairs={{0,1},{1,0},{2,3},{3,2},{4,5},{5,4},{6,7},{7,6},{8,9},{9,8},{10,11... | collective-permute-start | bytes 4128776 | tf_op jit(solution)/shard_map/ppermute | solution.py:40
  155.6 8.9 %collective-permute-start.37 = (bf16[5,48,512]{2,1,0:T(8,128)(2,1)S(1)}, bf16[5,48,512]{2,1,0:T(8,128)(2,1)S(1)}, u32[]{:S(2)}, u32[]{:S(2)}) collective-permute-start(bf16[5,48,512]{2,1,0:T(8,128)(2,1)S(1)} %get-tuple-element.140), channel_id=1, source_target_pairs={{0,4},{4,0},{8,12},{12,8},{1,5},{5,1},{9,13},{13,9},{2,6},{6,2},{1... | collective-permute-start | bytes 737288 | tf_op jit(solution)/shard_map/ppermute | solution.py:40
  157.4 12.9 %collective-permute-start.39 = (bf16[5,48,512]{2,1,0:T(8,128)(2,1)S(1)}, bf16[5,48,512]{2,1,0:T(8,128)(2,1)S(1)}, u32[]{:S(2)}, u32[]{:S(2)}) collective-permute-start(bf16[5,48,512]{2,1,0:T(8,128)(2,1)S(1)} %get-tuple-element.141), channel_id=1, source_target_pairs={{0,12},{4,8},{8,4},{12,0},{1,13},{5,9},{9,5},{13,1},{2,14},{6,10},... | collective-permute-start | bytes 737288 | tf_op jit(solution)/shard_map/ppermute | solution.py:40
  158.3 22.4 %collective-permute-start.38 = (bf16[5,48,512]{2,1,0:T(8,128)(2,1)S(1)}, bf16[5,48,512]{2,1,0:T(8,128)(2,1)S(1)}, u32[]{:S(2)}, u32[]{:S(2)}) collective-permute-start(bf16[5,48,512]{2,1,0:T(8,128)(2,1)S(1)} %fusion.50), channel_id=1, source_target_pairs={{0,8},{4,12},{8,0},{12,4},{1,9},{5,13},{9,1},{13,5},{2,10},{6,14},... | collective-permute-start | bytes 737288 | tf_op jit(solution)/shard_map/ppermute | solution.py:40
  195.1 9.1 %collective-permute-start.41 = (bf16[2,3,48,512]{3,2,1,0:T(8,128)(2,1)S(1)}, bf16[2,3,48,512]{3,2,1,0:T(8,128)(2,1)S(1)}, u32[]{:S(2)}, u32[]{:S(2)}) collective-permute-start(bf16[2,3,48,512]{3,2,1,0:T(8,128)(2,1)S(1)} %pad_maximum_fusion.16), channel_id=1, source_target_pairs={{0,4},{4,0},{8,12},{12,8},{1,5},{5,1},{9,13},{13,9},{2,6},{6,2},{1... | collective-permute-start | bytes 884744 | tf_op jit(solution)/shard_map/ppermute | solution.py:40
  204.5 9.2 %collective-permute-start.42 = (bf16[1,3,48,512]{3,2,1,0:T(8,128)(2,1)S(1)}, bf16[1,3,48,512]{3,2,1,0:T(8,128)(2,1)S(1)}, u32[]{:S(2)}, u32[]{:S(2)}) collective-permute-start(bf16[1,3,48,512]{3,2,1,0:T(8,128)(2,1)S(1)} %dynamic-slice_convert_fusion.3), channel_id=1, source_target_pairs={{0,8},{4,12},{8,0},{12,4},{1,9},{5,13},{9,1},{13,5},{2,10},{6,14},... | collective-permute-start | bytes 442376 | tf_op jit(solution)/shard_map/ppermute | solution.py:40
  (21 other events, 126.0 us)

commit v4 on v3

--- a/solution.py
+++ b/solution.py
@@ -127,9 +127,8 @@
         far, near = n_col // 2, n_col // 4
         tok_own, cot_own = gather_feats(jnp.stack([tokens, cotangent]))
         tok_1, tok_2 = [more_cols({0: jnp.stack(tok_own[i : i + 2])}, far) for i in (0, 2)]
-        tok = shares(all_cols(tok_1, near), all_cols(tok_2, near))
-        cot_own = jnp.stack(cot_own)
-        cot_own, tok = barrier((cot_own, tok))
+        cot_own, tok_1 = barrier((jnp.stack(cot_own), all_cols(tok_1, near)))
+        tok = shares(tok_1, all_cols(tok_2, near))
         tok_shares = spread(tok)
         tok_all = jnp.concatenate(tok).T
 
@@ -178,14 +177,13 @@
             return gd, ud, jnp.stack(sums).reshape(n_row, blocks, n, feats)
 
         gd_e, ud_e, early = back(gather_row(d_a0, d_b0))
-        h_from_x, h_from_y, early = barrier((h_from_x, h_from_y, early))
+        h_from_x, h_from_y, d_a2, d_b1, early = barrier((h_from_x, h_from_y, d_a2, d_b1, early))
+        from_x = swap(jnp.concatenate([d_a0, d_a2]), "depth", 1)
+        from_y = swap(jnp.concatenate([d_b0, d_b1]), "depth", 2)
         hid_rows = gather_row(h_a0, h_b0, h_a2, h_b1, h_from_x, h_from_y)
         out = jnp.stack([dot_nn(x, down_weight) for x in hid_rows]).reshape(n_row, 8, n, feats)
-        d_a2, d_b1, out = barrier((d_a2, d_b1, out))
-        from_x = swap(jnp.concatenate([d_a0, d_a2]), "depth", 1)
-        from_y = swap(jnp.concatenate([d_b0, d_b1]), "depth", 2)
         middle = gather_row(d_a2, d_b1)
-        hid_rows, cot, out, middle = barrier((hid_rows, cot, out, middle))
+        hid_rows, cot, out = barrier((hid_rows, cot, out))
         done = direct(
             jnp.concatenate([jnp.stack([out[:, i] for i in (0, 4, 2, 5)], axis=1), early[:, :1]], axis=1),
             jnp.concatenate([jnp.stack([out[:, i] for i in (1, 3, 6, 7)], axis=1), early[:, 1:]], axis=1),

time: 222 us -> 217 us (0.977)
  waiting for transfers between devices: 112 us -> 105 us
    ppermute x46, waiting for transfers between devices: 112 us -> 105 us  [swap(): return lax.ppermute(x, axis, [(i, i ^ k) for i in range(n)])]
  transfers between devices with their start and end apart: 46 -> 46, of which waited for: 31 -> 31; matrix products, arithmetic and copies ran while one was open for 24% -> 25% of each run, Pallas kernels for 0% -> 0%
where the time goes in v4:
time: 217 us
  waiting for transfers between devices  105 us (48%)
  starting transfers between devices  50.5 us (23%)
  matrix products  49.6 us (23%)
  other arithmetic  6.96 us (3%)
  local copies, waits for them, and re-layouts  2.73 us (1%)
    ppermute x46, waiting for transfers between devices, swap(): return lax.ppermute(x, axis, [(i, i ^ k) for i in range(n)])  105 us
    ppermute x46, starting transfers between devices, swap(): return lax.ppermute(x, axis, [(i, i ^ k) for i in range(n)])  50.5 us
    dot_general x12, matrix products, dot_nn(): return jnp.dot(left, right, preferred_element_type=F32)  29 us
    dot_general x12, matrix products, dot_nt(): lax.dot_general(left, right, (((1,), (1,)), ((), ())), preferred_element_...  15.4 us
    dot_general x1, matrix products, dot_tn(): lax.dot_general(left, right, (((0,), (0,)), ((), ())), preferred_element_...  5.14 us
  transfers between devices with their start and end apart: 46, of which 31 were waited for; matrix products, arithmetic and copies ran while one was open for 25% of the time, Pallas kernels for 0%

profile of v4, /device:TPU:0, one launch (start us, length us, event | category | flops | bytes accessed | tf_op | source)
XLA Modules:
  0.0 216.6 jit_solution(536149072111603204)
XLA Ops:
  1.7 3.0 %collective-permute-start = (bf16[2,48,512]{2,1,0:T(8,128)(2,1)S(1)}, bf16[2,48,512]{2,1,0:T(8,128)(2,1)S(1)}, u32[]{:S(2)}, u32[]{:S(2)}) collective-permute-start(bf16[2,48,512]{2,1,0:T(8,128)(2,1)S(1)} %get-tuple-element.151), channel_id=1, source_target_pairs={{0,1},{1,0},{2,3},{3,2},{4,5},{5,4},{6,7},{7,6},{8,9},{9,8},{10,11... | collective-permute-start | bytes 294920 | tf_op jit(solution)/shard_map/ppermute | solution.py:40
  7.8 2.7 %collective-permute-start.3 = (bf16[1,2,48,512]{3,2,1,0:T(8,128)(2,1)S(1)}, bf16[1,2,48,512]{3,2,1,0:T(8,128)(2,1)S(1)}, u32[]{:S(2)}, u32[]{:S(2)}) collective-permute-start(bf16[1,2,48,512]{3,2,1,0:T(8,128)(2,1)S(1)} %get-tuple-element.172), channel_id=1, source_target_pairs={{0,8},{4,12},{8,0},{12,4},{1,9},{5,13},{9,1},{13,5},{2,10},{6,14},... | collective-permute-start | bytes 294920 | tf_op jit(solution)/shard_map/ppermute | solution.py:40
  11.7 2.7 %collective-permute-start.5 = (bf16[1,2,48,512]{3,2,1,0:T(8,128)(2,1)S(1)}, bf16[1,2,48,512]{3,2,1,0:T(8,128)(2,1)S(1)}, u32[]{:S(2)}, u32[]{:S(2)}) collective-permute-start(bf16[1,2,48,512]{3,2,1,0:T(8,128)(2,1)S(1)} %maximum_bitcast_fusion.1), channel_id=1, source_target_pairs={{0,8},{4,12},{8,0},{12,4},{1,9},{5,13},{9,1},{13,5},{2,10},{6,14},... | collective-permute-start | bytes 294920 | tf_op jit(solution)/shard_map/ppermute | solution.py:40
  14.4 2.2 %collective-permute-done.3 = bf16[1,2,48,512]{3,2,1,0:T(8,128)(2,1)S(1)} collective-permute-done((bf16[1,2,48,512]{3,2,1,0:T(8,128)(2,1)S(1)}, bf16[1,2,48,512]{3,2,1,0:T(8,128)(2,1)S(1)}, u32[]{:S(2)}, u32[]{:S(2)}) %collective-permute-start.3) | collective-permute-done | bytes 98336 | tf_op jit(solution)/shard_map/ppermute | solution.py:40
  17.3 2.0 collective-permute-done.5
  20.0 3.2 %collective-permute-done.4 = bf16[2,2,48,512]{3,2,1,0:T(8,128)(2,1)S(1)} collective-permute-done((bf16[2,2,48,512]{3,2,1,0:T(8,128)(2,1)S(1)}, bf16[2,2,48,512]{3,2,1,0:T(8,128)(2,1)S(1)}, u32[]{:S(2)}, u32[]{:S(2)}) %collective-permute-start.4) | collective-permute-done | bytes 196640 | tf_op jit(solution)/shard_map/ppermute | solution.py:40
  23.4 3.2 %collective-permute-done.6 = bf16[2,2,48,512]{3,2,1,0:T(8,128)(2,1)S(1)} collective-permute-done((bf16[2,2,48,512]{3,2,1,0:T(8,128)(2,1)S(1)}, bf16[2,2,48,512]{3,2,1,0:T(8,128)(2,1)S(1)}, u32[]{:S(2)}, u32[]{:S(2)}) %collective-permute-start.6) | collective-permute-done | bytes 196640 | tf_op jit(solution)/shard_map/ppermute | solution.py:40
  27.5 3.1 %collective-permute-start.12 = (bf16[1,4,48,512]{3,2,1,0:T(8,128)(2,1)S(1)}, bf16[1,4,48,512]{3,2,1,0:T(8,128)(2,1)S(1)}, u32[]{:S(2)}, u32[]{:S(2)}) collective-permute-start(bf16[1,4,48,512]{3,2,1,0:T(8,128)(2,1)S(1)} %bitcast.222), channel_id=1, source_target_pairs={{0,8},{4,12},{8,0},{12,4},{1,9},{5,13},{9,1},{13,5},{2,10},{6,14},... | collective-permute-start | bytes 589832 | tf_op jit(solution)/shard_map/ppermute | solution.py:40
  31.5 2.9 %fusion.20 = bf16[192,3584]{1,0:T(8,128)(2,1)S(1)} fusion(f32[192,3584]{1,0:T(8,128)S(1)} %fusion.53, bf16[512,3584]{1,0:T(8,128)(2,1)} %collective-permute-done.8, bf16[384,512]{1,0:T(8,128)(2,1)S(1)} %collective-permute-done.7), kind=kOutput, calls=%fused_computation.26 | convolution fusion | flops 706019328 | bytes 7995392 | tf_op jit(solution)/shard_map/dot_general | solution.py:10
  37.8 2.9 %fusion.65 = f32[192,3584]{1,0:T(8,128)S(1)} fusion(bf16[512,3584]{1,0:T(8,128)(2,1)} %collective-permute-done.9, bf16[384,512]{1,0:T(8,128)(2,1)S(1)} %collective-permute-done.7), kind=kOutput, calls=%fused_computation.147 | convolution fusion | flops 704643072 | bytes 6619136 | tf_op jit(solution)/shard_map/dot_general | solution.py:10
  42.9 10.0 %collective-permute-done.14 = bf16[96,3584]{1,0:T(8,128)(2,1)S(1)} collective-permute-done((bf16[96,3584]{1,0:T(8,128)(2,1)S(1)}, bf16[96,3584]{1,0:T(8,128)(2,1)S(1)}, u32[]{:S(2)}, u32[]{:S(2)}) %collective-permute-start.14) | collective-permute-done | bytes 688160 | tf_op jit(solution)/shard_map/ppermute | solution.py:40
  54.6 2.1 collective-permute-start.15
  56.7 2.9 %fusion.62 = f32[192,3584]{1,0:T(8,128)S(1)} fusion(bf16[512,3584]{1,0:T(8,128)(2,1)} %collective-permute-done.8, bf16[384,512]{1,0:T(8,128)(2,1)S(1)} %collective-permute-done.7), kind=kOutput, calls=%fused_computation.144 | convolution fusion | flops 704643072 | bytes 6619136 | tf_op jit(solution)/shard_map/dot_general | solution.py:10
  64.4 3.2 %convolution_add_fusion.1 = f32[192,3584]{1,0:T(8,128)S(1)} fusion(f32[192,3584]{1,0:T(8,128)S(1)} %fusion.58, bf16[512,3584]{1,0:T(8,128)(2,1)} %collective-permute-done.9, bf16[384,512]{1,0:T(8,128)(2,1)S(1)} %collective-permute-done.7), kind=kOutput, calls=%fused_computation.21 | convolution fusion | flops 705331200 | bytes 9371648 | tf_op jit(solution)/shard_map/dot_general | solution.py:10
  79.9 3.4 %collective-permute-done.23 = bf16[48,3584]{1,0:T(8,128)(2,1)S(1)} collective-permute-done((bf16[48,3584]{1,0:T(8,128)(2,1)S(1)}, bf16[48,3584]{1,0:T(8,128)(2,1)S(1)}, u32[]{:S(2)}, u32[]{:S(2)}) %collective-permute-start.23) | collective-permute-done | bytes 344096 | tf_op jit(solution)/shard_map/ppermute | solution.py:40
  83.3 3.9 %collective-permute-done.21 = bf16[48,3584]{1,0:T(8,128)(2,1)S(1)} collective-permute-done((bf16[48,3584]{1,0:T(8,128)(2,1)S(1)}, bf16[48,3584]{1,0:T(8,128)(2,1)S(1)}, u32[]{:S(2)}, u32[]{:S(2)}) %collective-permute-start.21) | collective-permute-done | bytes 344096 | tf_op jit(solution)/shard_map/ppermute | solution.py:40
  90.2 11.9 %collective-permute-done.19 = bf16[96,3584]{1,0:T(8,128)(2,1)S(1)} collective-permute-done((bf16[96,3584]{1,0:T(8,128)(2,1)S(1)}, bf16[96,3584]{1,0:T(8,128)(2,1)S(1)}, u32[]{:S(2)}, u32[]{:S(2)}) %collective-permute-start.19) | collective-permute-done | bytes 688160 | tf_op jit(solution)/shard_map/ppermute | solution.py:40
  105.0 4.4 %collective-permute-done.25 = bf16[48,3584]{1,0:T(8,128)(2,1)S(1)} collective-permute-done((bf16[48,3584]{1,0:T(8,128)(2,1)S(1)}, bf16[48,3584]{1,0:T(8,128)(2,1)S(1)}, u32[]{:S(2)}, u32[]{:S(2)}) %collective-permute-start.25) | collective-permute-done | bytes 344096 | tf_op jit(solution)/shard_map/ppermute | solution.py:40
  112.1 4.7 %collective-permute-done.24 = bf16[48,3584]{1,0:T(8,128)(2,1)S(1)} collective-permute-done((bf16[48,3584]{1,0:T(8,128)(2,1)S(1)}, bf16[48,3584]{1,0:T(8,128)(2,1)S(1)}, u32[]{:S(2)}, u32[]{:S(2)}) %collective-permute-start.24) | collective-permute-done | bytes 344096 | tf_op jit(solution)/shard_map/ppermute | solution.py:40
  126.8 4.7 %collective-permute-done.28 = bf16[96,3584]{1,0:T(8,128)(2,1)S(1)} collective-permute-done((bf16[96,3584]{1,0:T(8,128)(2,1)S(1)}, bf16[96,3584]{1,0:T(8,128)(2,1)S(1)}, u32[]{:S(2)}, u32[]{:S(2)}) %collective-permute-start.28) | collective-permute-done | bytes 688160 | tf_op jit(solution)/shard_map/ppermute | solution.py:40
  131.5 14.3 %collective-permute-done.29 = bf16[96,3584]{1,0:T(8,128)(2,1)S(1)} collective-permute-done((bf16[96,3584]{1,0:T(8,128)(2,1)S(1)}, bf16[96,3584]{1,0:T(8,128)(2,1)S(1)}, u32[]{:S(2)}, u32[]{:S(2)}) %collective-permute-start.29) | collective-permute-done | bytes 688160 | tf_op jit(solution)/shard_map/ppermute | solution.py:40
  153.1 1.8 collective-permute-start.37
  155.8 5.7 %collective-permute-done.37 = bf16[5,48,512]{2,1,0:T(8,128)(2,1)S(1)} collective-permute-done((bf16[5,48,512]{2,1,0:T(8,128)(2,1)S(1)}, bf16[5,48,512]{2,1,0:T(8,128)(2,1)S(1)}, u32[]{:S(2)}, u32[]{:S(2)}) %collective-permute-start.37) | collective-permute-done | bytes 245792 | tf_op jit(solution)/shard_map/ppermute | solution.py:40
  163.0 5.1 %fusion.16 = f32[3584,512]{1,0:T(8,128)} fusion(bf16[384,3584]{1,0:T(8,128)(2,1)S(1)} %copy-done.6, bf16[384,3584]{1,0:T(8,128)(2,1)S(1)} %constant_dynamic-update-slice_fusion.34, bf16[384,512]{1,0:T(8,128)(2,1)S(1)} %get-tuple-element.102, bf16[384,512]{1,0:T(8,128)(2,1)S(1)} %get-tuple-element.101), kind=kOutput, calls=%fused_computation.16 | convolution fusion | flops 2831155200 | bytes 13631488 | tf_op jit(solution)/shard_map/dot_general | solution.py:14
  168.2 10.1 %collective-permute-done.38 = bf16[5,48,512]{2,1,0:T(8,128)(2,1)S(1)} collective-permute-done((bf16[5,48,512]{2,1,0:T(8,128)(2,1)S(1)}, bf16[5,48,512]{2,1,0:T(8,128)(2,1)S(1)}, u32[]{:S(2)}, u32[]{:S(2)}) %collective-permute-start.38) | collective-permute-done | bytes 245792 | tf_op jit(solution)/shard_map/ppermute | solution.py:40
  183.3 1.8 collective-permute-done.40
  188.5 1.8 collective-permute-start.41
  190.3 5.2 %fusion = f32[512,3584]{1,0:T(8,128)} fusion(bf16[512,768]{0,1:T(8,128)(2,1)S(1)} %maximum_bitcast_fusion, bf16[288,3584]{1,0:T(8,128)(2,1)S(1)} %bitcast.221, bf16[96,3584]{1,0:T(8,128)(2,1)S(1)} %bitcast.213, bf16[288,3584]{1,0:T(8,128)(2,1)S(1)} %bitcast.219, bf16[96,3584]{1,0:T(8,128)(2,1)S(1)} %bitcast.211), kind=kOutput, calls=%fused_computation | convolution fusion | flops 2840592384 | bytes 13631488 | tf_op jit(solution)/shard_map/dot_general | solution.py:10
  195.5 2.1 collective-permute-done.41
  198.9 5.1 %fusion.8 = f32[512,3584]{1,0:T(8,128)} fusion(bf16[512,768]{0,1:T(8,128)(2,1)S(1)} %maximum_bitcast_fusion, bf16[288,3584]{1,0:T(8,128)(2,1)S(1)} %bitcast.217, bf16[96,3584]{1,0:T(8,128)(2,1)S(1)} %bitcast.209, bf16[288,3584]{1,0:T(8,128)(2,1)S(1)} %bitcast.215, bf16[96,3584]{1,0:T(8,128)(2,1)S(1)} %bitcast.207), kind=kOutput, calls=%fused_computation.8 | convolution fusion | flops 2840592384 | bytes 13631488 | tf_op jit(solution)/shard_map/dot_general | solution.py:10
  204.1 2.9 %collective-permute-done.42 = bf16[1,3,48,512]{3,2,1,0:T(8,128)(2,1)S(1)} collective-permute-done((bf16[1,3,48,512]{3,2,1,0:T(8,128)(2,1)S(1)}, bf16[1,3,48,512]{3,2,1,0:T(8,128)(2,1)S(1)}, u32[]{:S(2)}, u32[]{:S(2)}) %collective-permute-start.42) | collective-permute-done | bytes 147488 | tf_op jit(solution)/shard_map/ppermute | solution.py:40
  210.8 1.7 collective-permute-done.43
  (205 shorter events, 78.0 us)
Async XLA Ops:
  6.2 25.3 %collective-permute-start.8 = (bf16[512,3584]{1,0:T(8,128)(2,1)}, bf16[512,3584]{1,0:T(8,128)(2,1)}, u32[]{:S(2)}, u32[]{:S(2)}) collective-permute-start(bf16[512,3584]{1,0:T(8,128)(2,1)} %param.7), channel_id=1, source_target_pairs={{0,16},{16,0},{1,17},{17,1},{2,18},{18,2},{3,19},{19,3},{4,20},{20... | collective-permute-start | bytes 11010056 | tf_op jit(solution)/shard_map/ppermute | solution.py:40
  6.2 31.6 %collective-permute-start.9 = (bf16[512,3584]{1,0:T(8,128)(2,1)}, bf16[512,3584]{1,0:T(8,128)(2,1)}, u32[]{:S(2)}, u32[]{:S(2)}) collective-permute-start(bf16[512,3584]{1,0:T(8,128)(2,1)} %param.8), channel_id=1, source_target_pairs={{0,16},{16,0},{1,17},{17,1},{2,18},{18,2},{3,19},{19,3},{4,20},{20... | collective-permute-start | bytes 11010056 | tf_op jit(solution)/shard_map/ppermute | solution.py:40
  7.8 8.8 %collective-permute-start.3 = (bf16[1,2,48,512]{3,2,1,0:T(8,128)(2,1)S(1)}, bf16[1,2,48,512]{3,2,1,0:T(8,128)(2,1)S(1)}, u32[]{:S(2)}, u32[]{:S(2)}) collective-permute-start(bf16[1,2,48,512]{3,2,1,0:T(8,128)(2,1)S(1)} %get-tuple-element.172), channel_id=1, source_target_pairs={{0,8},{4,12},{8,0},{12,4},{1,9},{5,13},{9,1},{13,5},{2,10},{6,14},... | collective-permute-start | bytes 294920 | tf_op jit(solution)/shard_map/ppermute | solution.py:40
  27.0 42.0 %collective-permute-start.17 = (bf16[3584,512]{1,0:T(8,128)(2,1)}, bf16[3584,512]{1,0:T(8,128)(2,1)S(1)}, u32[]{:S(2)}, u32[]{:S(2)}) collective-permute-start(bf16[3584,512]{1,0:T(8,128)(2,1)} %param.9), channel_id=1, source_target_pairs={{0,16},{16,0},{1,17},{17,1},{2,18},{18,2},{3,19},{19,3},{4,20},{20... | collective-permute-start | bytes 11010056 | tf_op jit(solution)/shard_map/ppermute | solution.py:40
  27.5 14.9 %collective-permute-start.12 = (bf16[1,4,48,512]{3,2,1,0:T(8,128)(2,1)S(1)}, bf16[1,4,48,512]{3,2,1,0:T(8,128)(2,1)S(1)}, u32[]{:S(2)}, u32[]{:S(2)}) collective-permute-start(bf16[1,4,48,512]{3,2,1,0:T(8,128)(2,1)S(1)} %bitcast.222), channel_id=1, source_target_pairs={{0,8},{4,12},{8,0},{12,4},{1,9},{5,13},{9,1},{13,5},{2,10},{6,14},... | collective-permute-start | bytes 589832 | tf_op jit(solution)/shard_map/ppermute | solution.py:40
  34.6 18.4 %collective-permute-start.14 = (bf16[96,3584]{1,0:T(8,128)(2,1)S(1)}, bf16[96,3584]{1,0:T(8,128)(2,1)S(1)}, u32[]{:S(2)}, u32[]{:S(2)}) collective-permute-start(bf16[96,3584]{1,0:T(8,128)(2,1)S(1)} %get-tuple-element.129), channel_id=1, source_target_pairs={{0,2},{1,3},{2,0},{3,1},{4,6},{5,7},{6,4},{7,5},{8,10},{9,11},{10,... | collective-permute-start | bytes 2064392 | tf_op jit(solution)/shard_map/ppermute | solution.py:40
  36.2 18.4 %collective-permute-start.13 = (bf16[96,3584]{1,0:T(8,128)(2,1)S(1)}, bf16[96,3584]{1,0:T(8,128)(2,1)S(1)}, u32[]{:S(2)}, u32[]{:S(2)}) collective-permute-start(bf16[96,3584]{1,0:T(8,128)(2,1)S(1)} %get-tuple-element.130), channel_id=1, source_target_pairs={{0,1},{1,0},{2,3},{3,2},{4,5},{5,4},{6,7},{7,6},{8,9},{9,8},{10,11... | collective-permute-start | bytes 2064392 | tf_op jit(solution)/shard_map/ppermute | solution.py:40
  41.8 29.4 %collective-permute-start.11 = (bf16[96,3584]{1,0:T(8,128)(2,1)S(1)}, bf16[96,3584]{1,0:T(8,128)(2,1)S(1)}, u32[]{:S(2)}, u32[]{:S(2)}) collective-permute-start(bf16[96,3584]{1,0:T(8,128)(2,1)S(1)} %get-tuple-element.127), channel_id=1, source_target_pairs={{0,2},{1,3},{2,0},{3,1},{4,6},{5,7},{6,4},{7,5},{8,10},{9,11},{10,... | collective-permute-start | bytes 2064392 | tf_op jit(solution)/shard_map/ppermute | solution.py:40
  42.4 28.8 %collective-permute-start.10 = (bf16[96,3584]{1,0:T(8,128)(2,1)S(1)}, bf16[96,3584]{1,0:T(8,128)(2,1)S(1)}, u32[]{:S(2)}, u32[]{:S(2)}) collective-permute-start(bf16[96,3584]{1,0:T(8,128)(2,1)S(1)} %get-tuple-element.128), channel_id=1, source_target_pairs={{0,1},{1,0},{2,3},{3,2},{4,5},{5,4},{6,7},{7,6},{8,9},{9,8},{10,11... | collective-permute-start | bytes 2064392 | tf_op jit(solution)/shard_map/ppermute | solution.py:40
  54.6 8.5 %collective-permute-start.15 = (bf16[2,4,48,512]{3,2,1,0:T(8,128)(2,1)S(1)}, bf16[2,4,48,512]{3,2,1,0:T(8,128)(2,1)S(1)}, u32[]{:S(2)}, u32[]{:S(2)}) collective-permute-start(bf16[2,4,48,512]{3,2,1,0:T(8,128)(2,1)S(1)} %pad_maximum_fusion.14), channel_id=1, source_target_pairs={{0,4},{4,0},{8,12},{12,8},{1,5},{5,1},{9,13},{13,9},{2,6},{6,2},{1... | collective-permute-start | bytes 1179656 | tf_op jit(solution)/shard_map/ppermute | solution.py:40
  60.7 17.0 %collective-permute-start.22 = (bf16[48,3584]{1,0:T(8,128)(2,1)S(1)}, bf16[48,3584]{1,0:T(8,128)(2,1)S(1)}, u32[]{:S(2)}, u32[]{:S(2)}) collective-permute-start(bf16[48,3584]{1,0:T(8,128)(2,1)S(1)} %get-tuple-element.117), channel_id=1, source_target_pairs={{0,1},{1,0},{2,3},{3,2},{4,5},{5,4},{6,7},{7,6},{8,9},{9,8},{10,11... | collective-permute-start | bytes 1032200 | tf_op jit(solution)/shard_map/ppermute | solution.py:40
  69.0 10.9 %collective-permute-start.20 = (bf16[48,3584]{1,0:T(8,128)(2,1)S(1)}, bf16[48,3584]{1,0:T(8,128)(2,1)S(1)}, u32[]{:S(2)}, u32[]{:S(2)}) collective-permute-start(bf16[48,3584]{1,0:T(8,128)(2,1)S(1)} %get-tuple-element.118), channel_id=1, source_target_pairs={{0,2},{1,3},{2,0},{3,1},{4,6},{5,7},{6,4},{7,5},{8,10},{9,11},{10,... | collective-permute-start | bytes 1032200 | tf_op jit(solution)/shard_map/ppermute | solution.py:40
  71.3 12.0 %collective-permute-start.23 = (bf16[48,3584]{1,0:T(8,128)(2,1)S(1)}, bf16[48,3584]{1,0:T(8,128)(2,1)S(1)}, u32[]{:S(2)}, u32[]{:S(2)}) collective-permute-start(bf16[48,3584]{1,0:T(8,128)(2,1)S(1)} %get-tuple-element.115), channel_id=1, source_target_pairs={{0,1},{1,0},{2,3},{3,2},{4,5},{5,4},{6,7},{7,6},{8,9},{9,8},{10,11... | collective-permute-start | bytes 1032200 | tf_op jit(solution)/shard_map/ppermute | solution.py:40
  72.9 14.3 %collective-permute-start.21 = (bf16[48,3584]{1,0:T(8,128)(2,1)S(1)}, bf16[48,3584]{1,0:T(8,128)(2,1)S(1)}, u32[]{:S(2)}, u32[]{:S(2)}) collective-permute-start(bf16[48,3584]{1,0:T(8,128)(2,1)S(1)} %get-tuple-element.116), channel_id=1, source_target_pairs={{0,2},{1,3},{2,0},{3,1},{4,6},{5,7},{6,4},{7,5},{8,10},{9,11},{10,... | collective-permute-start | bytes 1032200 | tf_op jit(solution)/shard_map/ppermute | solution.py:40
  74.3 27.7 %collective-permute-start.19 = (bf16[96,3584]{1,0:T(8,128)(2,1)S(1)}, bf16[96,3584]{1,0:T(8,128)(2,1)S(1)}, u32[]{:S(2)}, u32[]{:S(2)}) collective-permute-start(bf16[96,3584]{1,0:T(8,128)(2,1)S(1)} %get-tuple-element.125), channel_id=1, source_target_pairs={{0,2},{1,3},{2,0},{3,1},{4,6},{5,7},{6,4},{7,5},{8,10},{9,11},{10,... | collective-permute-start | bytes 2064392 | tf_op jit(solution)/shard_map/ppermute | solution.py:40
  77.7 24.3 %collective-permute-start.18 = (bf16[96,3584]{1,0:T(8,128)(2,1)S(1)}, bf16[96,3584]{1,0:T(8,128)(2,1)S(1)}, u32[]{:S(2)}, u32[]{:S(2)}) collective-permute-start(bf16[96,3584]{1,0:T(8,128)(2,1)S(1)} %get-tuple-element.126), channel_id=1, source_target_pairs={{0,1},{1,0},{2,3},{3,2},{4,5},{5,4},{6,7},{7,6},{8,9},{9,8},{10,11... | collective-permute-start | bytes 2064392 | tf_op jit(solution)/shard_map/ppermute | solution.py:40
  88.0 17.0 %collective-permute-start.26 = (bf16[48,3584]{1,0:T(8,128)(2,1)S(1)}, bf16[48,3584]{1,0:T(8,128)(2,1)S(1)}, u32[]{:S(2)}, u32[]{:S(2)}) collective-permute-start(bf16[48,3584]{1,0:T(8,128)(2,1)S(1)} %get-tuple-element.81), channel_id=1, source_target_pairs={{0,1},{1,0},{2,3},{3,2},{4,5},{5,4},{6,7},{7,6},{8,9},{9,8},{10,11... | collective-permute-start | bytes 1032200 | tf_op jit(solution)/shard_map/ppermute | solution.py:40
  89.6 19.8 %collective-permute-start.25 = (bf16[48,3584]{1,0:T(8,128)(2,1)S(1)}, bf16[48,3584]{1,0:T(8,128)(2,1)S(1)}, u32[]{:S(2)}, u32[]{:S(2)}) collective-permute-start(bf16[48,3584]{1,0:T(8,128)(2,1)S(1)} %get-tuple-element.78), channel_id=1, source_target_pairs={{0,2},{1,3},{2,0},{3,1},{4,6},{5,7},{6,4},{7,5},{8,10},{9,11},{10,... | collective-permute-start | bytes 1032200 | tf_op jit(solution)/shard_map/ppermute | solution.py:40
  102.2 9.9 %collective-permute-start.30 = (bf16[48,3584]{1,0:T(8,128)(2,1)S(1)}, bf16[48,3584]{1,0:T(8,128)(2,1)S(1)}, u32[]{:S(2)}, u32[]{:S(2)}) collective-permute-start(bf16[48,3584]{1,0:T(8,128)(2,1)S(1)} %get-tuple-element.113), channel_id=1, source_target_pairs={{0,1},{1,0},{2,3},{3,2},{4,5},{5,4},{6,7},{7,6},{8,9},{9,8},{10,11... | collective-permute-start | bytes 1032200 | tf_op jit(solution)/shard_map/ppermute | solution.py:40
  103.8 13.0 %collective-permute-start.24 = (bf16[48,3584]{1,0:T(8,128)(2,1)S(1)}, bf16[48,3584]{1,0:T(8,128)(2,1)S(1)}, u32[]{:S(2)}, u32[]{:S(2)}) collective-permute-start(bf16[48,3584]{1,0:T(8,128)(2,1)S(1)} %get-tuple-element.114), channel_id=1, source_target_pairs={{0,2},{1,3},{2,0},{3,1},{4,6},{5,7},{6,4},{7,5},{8,10},{9,11},{10,... | collective-permute-start | bytes 1032200 | tf_op jit(solution)/shard_map/ppermute | solution.py:40
  109.6 21.9 %collective-permute-start.28 = (bf16[96,3584]{1,0:T(8,128)(2,1)S(1)}, bf16[96,3584]{1,0:T(8,128)(2,1)S(1)}, u32[]{:S(2)}, u32[]{:S(2)}) collective-permute-start(bf16[96,3584]{1,0:T(8,128)(2,1)S(1)} %pad_maximum_fusion.11), channel_id=1, source_target_pairs={{0,2},{1,3},{2,0},{3,1},{4,6},{5,7},{6,4},{7,5},{8,10},{9,11},{10,... | collective-permute-start | bytes 2064392 | tf_op jit(solution)/shard_map/ppermute | solution.py:40
  110.2 21.3 %collective-permute-start.27 = (bf16[96,3584]{1,0:T(8,128)(2,1)S(1)}, bf16[96,3584]{1,0:T(8,128)(2,1)S(1)}, u32[]{:S(2)}, u32[]{:S(2)}) collective-permute-start(bf16[96,3584]{1,0:T(8,128)(2,1)S(1)} %pad_maximum_fusion.10), channel_id=1, source_target_pairs={{0,1},{1,0},{2,3},{3,2},{4,5},{5,4},{6,7},{7,6},{8,9},{9,8},{10,11... | collective-permute-start | bytes 2064392 | tf_op jit(solution)/shard_map/ppermute | solution.py:40
  118.9 27.0 %collective-permute-start.29 = (bf16[96,3584]{1,0:T(8,128)(2,1)S(1)}, bf16[96,3584]{1,0:T(8,128)(2,1)S(1)}, u32[]{:S(2)}, u32[]{:S(2)}) collective-permute-start(bf16[96,3584]{1,0:T(8,128)(2,1)S(1)} %pad_maximum_fusion.12), channel_id=1, source_target_pairs={{0,2},{1,3},{2,0},{3,1},{4,6},{5,7},{6,4},{7,5},{8,10},{9,11},{10,... | collective-permute-start | bytes 2064392 | tf_op jit(solution)/shard_map/ppermute | solution.py:40
  119.6 26.3 %collective-permute-start.31 = (bf16[96,3584]{1,0:T(8,128)(2,1)S(1)}, bf16[96,3584]{1,0:T(8,128)(2,1)S(1)}, u32[]{:S(2)}, u32[]{:S(2)}) collective-permute-start(bf16[96,3584]{1,0:T(8,128)(2,1)S(1)} %pad_maximum_fusion.13), channel_id=1, source_target_pairs={{0,1},{1,0},{2,3},{3,2},{4,5},{5,4},{6,7},{7,6},{8,9},{9,8},{10,11... | collective-permute-start | bytes 2064392 | tf_op jit(solution)/shard_map/ppermute | solution.py:40
  146.2 32.6 %collective-permute-start.34 = (bf16[192,3584]{1,0:T(8,128)(2,1)S(1)}, bf16[192,3584]{1,0:T(8,128)(2,1)S(1)}, u32[]{:S(2)}, u32[]{:S(2)}) collective-permute-start(bf16[192,3584]{1,0:T(8,128)(2,1)S(1)} %pad_maximum_fusion.7), channel_id=1, source_target_pairs={{0,2},{1,3},{2,0},{3,1},{4,6},{5,7},{6,4},{7,5},{8,10},{9,11},{10,... | collective-permute-start | bytes 4128776 | tf_op jit(solution)/shard_map/ppermute | solution.py:40
  147.0 31.9 %collective-permute-start.35 = (bf16[192,3584]{1,0:T(8,128)(2,1)S(1)}, bf16[192,3584]{1,0:T(8,128)(2,1)S(1)}, u32[]{:S(2)}, u32[]{:S(2)}) collective-permute-start(bf16[192,3584]{1,0:T(8,128)(2,1)S(1)} %constant_dynamic-update-slice_fusion.32), channel_id=1, source_target_pairs={{0,16},{16,0},{1,17},{17,1},{2,18},{18,2},{3,19},{19,3},{4,20},{20... | collective-permute-start | bytes 4128776 | tf_op jit(solution)/shard_map/ppermute | solution.py:40
  147.4 32.5 %collective-permute-start.33 = (bf16[192,3584]{1,0:T(8,128)(2,1)S(1)}, bf16[192,3584]{1,0:T(8,128)(2,1)S(1)}, u32[]{:S(2)}, u32[]{:S(2)}) collective-permute-start(bf16[192,3584]{1,0:T(8,128)(2,1)S(1)} %pad_maximum_fusion.5), channel_id=1, source_target_pairs={{0,1},{1,0},{2,3},{3,2},{4,5},{5,4},{6,7},{7,6},{8,9},{9,8},{10,11... | collective-permute-start | bytes 4128776 | tf_op jit(solution)/shard_map/ppermute | solution.py:40
  153.1 8.4 %collective-permute-start.37 = (bf16[5,48,512]{2,1,0:T(8,128)(2,1)S(1)}, bf16[5,48,512]{2,1,0:T(8,128)(2,1)S(1)}, u32[]{:S(2)}, u32[]{:S(2)}) collective-permute-start(bf16[5,48,512]{2,1,0:T(8,128)(2,1)S(1)} %get-tuple-element.138), channel_id=1, source_target_pairs={{0,4},{4,0},{8,12},{12,8},{1,5},{5,1},{9,13},{13,9},{2,6},{6,2},{1... | collective-permute-start | bytes 737288 | tf_op jit(solution)/shard_map/ppermute | solution.py:40
  154.9 13.2 %collective-permute-start.39 = (bf16[5,48,512]{2,1,0:T(8,128)(2,1)S(1)}, bf16[5,48,512]{2,1,0:T(8,128)(2,1)S(1)}, u32[]{:S(2)}, u32[]{:S(2)}) collective-permute-start(bf16[5,48,512]{2,1,0:T(8,128)(2,1)S(1)} %get-tuple-element.139), channel_id=1, source_target_pairs={{0,12},{4,8},{8,4},{12,0},{1,13},{5,9},{9,5},{13,1},{2,14},{6,10},... | collective-permute-start | bytes 737288 | tf_op jit(solution)/shard_map/ppermute | solution.py:40
  161.5 16.7 %collective-permute-start.38 = (bf16[5,48,512]{2,1,0:T(8,128)(2,1)S(1)}, bf16[5,48,512]{2,1,0:T(8,128)(2,1)S(1)}, u32[]{:S(2)}, u32[]{:S(2)}) collective-permute-start(bf16[5,48,512]{2,1,0:T(8,128)(2,1)S(1)} %fusion.49), channel_id=1, source_target_pairs={{0,8},{4,12},{8,0},{12,4},{1,9},{5,13},{9,1},{13,5},{2,10},{6,14},... | collective-permute-start | bytes 737288 | tf_op jit(solution)/shard_map/ppermute | solution.py:40
  188.5 9.1 %collective-permute-start.41 = (bf16[2,3,48,512]{3,2,1,0:T(8,128)(2,1)S(1)}, bf16[2,3,48,512]{3,2,1,0:T(8,128)(2,1)S(1)}, u32[]{:S(2)}, u32[]{:S(2)}) collective-permute-start(bf16[2,3,48,512]{3,2,1,0:T(8,128)(2,1)S(1)} %pad_maximum_fusion.16), channel_id=1, source_target_pairs={{0,4},{4,0},{8,12},{12,8},{1,5},{5,1},{9,13},{13,9},{2,6},{6,2},{1... | collective-permute-start | bytes 884744 | tf_op jit(solution)/shard_map/ppermute | solution.py:40
  197.8 9.2 %collective-permute-start.42 = (bf16[1,3,48,512]{3,2,1,0:T(8,128)(2,1)S(1)}, bf16[1,3,48,512]{3,2,1,0:T(8,128)(2,1)S(1)}, u32[]{:S(2)}, u32[]{:S(2)}) collective-permute-start(bf16[1,3,48,512]{3,2,1,0:T(8,128)(2,1)S(1)} %dynamic-slice_convert_fusion.3), channel_id=1, source_target_pairs={{0,8},{4,12},{8,0},{12,4},{1,9},{5,13},{9,1},{13,5},{2,10},{6,14},... | collective-permute-start | bytes 442376 | tf_op jit(solution)/shard_map/ppermute | solution.py:40
  (21 other events, 148.5 us)

commit v5 on v4

--- a/solution.py
+++ b/solution.py
@@ -183,7 +183,7 @@
         hid_rows = gather_row(h_a0, h_b0, h_a2, h_b1, h_from_x, h_from_y)
         out = jnp.stack([dot_nn(x, down_weight) for x in hid_rows]).reshape(n_row, 8, n, feats)
         middle = gather_row(d_a2, d_b1)
-        hid_rows, cot, out = barrier((hid_rows, cot, out))
+        hid_rows, cot, out, middle = barrier((hid_rows, cot, out, middle))
         done = direct(
             jnp.concatenate([jnp.stack([out[:, i] for i in (0, 4, 2, 5)], axis=1), early[:, :1]], axis=1),
             jnp.concatenate([jnp.stack([out[:, i] for i in (1, 3, 6, 7)], axis=1), early[:, 1:]], axis=1),

time: 217 us -> 217 us (level)
  transfers between devices with their start and end apart: 46 -> 46, of which waited for: 31 -> 32; matrix products, arithmetic and copies ran while one was open for 25% -> 25% of each run, Pallas kernels for 0% -> 0%
where the time goes in v5:
time: 217 us; the launch traced here: 216 us
  waiting for transfers between devices  105 us (48%)
  starting transfers between devices  50.2 us (23%)
  matrix products  49.6 us (23%)
  other arithmetic  6.96 us (3%)
  local copies, waits for them, and re-layouts  2.73 us (1%)
    ppermute x46, waiting for transfers between devices, swap(): return lax.ppermute(x, axis, [(i, i ^ k) for i in range(n)])  105 us
    ppermute x46, starting transfers between devices, swap(): return lax.ppermute(x, axis, [(i, i ^ k) for i in range(n)])  50.2 us
    dot_general x12, matrix products, dot_nn(): return jnp.dot(left, right, preferred_element_type=F32)  29 us
    dot_general x12, matrix products, dot_nt(): lax.dot_general(left, right, (((1,), (1,)), ((), ())), preferred_element_...  15.4 us
    dot_general x1, matrix products, dot_tn(): lax.dot_general(left, right, (((0,), (0,)), ((), ())), preferred_element_...  5.14 us
  transfers between devices with their start and end apart: 46, of which 32 were waited for; matrix products, arithmetic and copies ran while one was open for 25% of the time, Pallas kernels for 0%

profile of v5, /device:TPU:0, one launch (start us, length us, event | category | flops | bytes accessed | tf_op | source)
XLA Modules:
  0.0 216.2 jit_solution(6829036072998132024)
XLA Ops:
  1.7 3.0 %collective-permute-start = (bf16[2,48,512]{2,1,0:T(8,128)(2,1)S(1)}, bf16[2,48,512]{2,1,0:T(8,128)(2,1)S(1)}, u32[]{:S(2)}, u32[]{:S(2)}) collective-permute-start(bf16[2,48,512]{2,1,0:T(8,128)(2,1)S(1)} %get-tuple-element.155), channel_id=1, source_target_pairs={{0,1},{1,0},{2,3},{3,2},{4,5},{5,4},{6,7},{7,6},{8,9},{9,8},{10,11... | collective-permute-start | bytes 294920 | tf_op jit(solution)/shard_map/ppermute | solution.py:40
  7.8 2.7 %collective-permute-start.3 = (bf16[1,2,48,512]{3,2,1,0:T(8,128)(2,1)S(1)}, bf16[1,2,48,512]{3,2,1,0:T(8,128)(2,1)S(1)}, u32[]{:S(2)}, u32[]{:S(2)}) collective-permute-start(bf16[1,2,48,512]{3,2,1,0:T(8,128)(2,1)S(1)} %get-tuple-element.176), channel_id=1, source_target_pairs={{0,8},{4,12},{8,0},{12,4},{1,9},{5,13},{9,1},{13,5},{2,10},{6,14},... | collective-permute-start | bytes 294920 | tf_op jit(solution)/shard_map/ppermute | solution.py:40
  11.7 2.7 %collective-permute-start.5 = (bf16[1,2,48,512]{3,2,1,0:T(8,128)(2,1)S(1)}, bf16[1,2,48,512]{3,2,1,0:T(8,128)(2,1)S(1)}, u32[]{:S(2)}, u32[]{:S(2)}) collective-permute-start(bf16[1,2,48,512]{3,2,1,0:T(8,128)(2,1)S(1)} %maximum_bitcast_fusion.1), channel_id=1, source_target_pairs={{0,8},{4,12},{8,0},{12,4},{1,9},{5,13},{9,1},{13,5},{2,10},{6,14},... | collective-permute-start | bytes 294920 | tf_op jit(solution)/shard_map/ppermute | solution.py:40
  14.4 2.2 %collective-permute-done.3 = bf16[1,2,48,512]{3,2,1,0:T(8,128)(2,1)S(1)} collective-permute-done((bf16[1,2,48,512]{3,2,1,0:T(8,128)(2,1)S(1)}, bf16[1,2,48,512]{3,2,1,0:T(8,128)(2,1)S(1)}, u32[]{:S(2)}, u32[]{:S(2)}) %collective-permute-start.3) | collective-permute-done | bytes 98336 | tf_op jit(solution)/shard_map/ppermute | solution.py:40
  17.3 2.0 collective-permute-done.5
  20.0 3.2 %collective-permute-done.4 = bf16[2,2,48,512]{3,2,1,0:T(8,128)(2,1)S(1)} collective-permute-done((bf16[2,2,48,512]{3,2,1,0:T(8,128)(2,1)S(1)}, bf16[2,2,48,512]{3,2,1,0:T(8,128)(2,1)S(1)}, u32[]{:S(2)}, u32[]{:S(2)}) %collective-permute-start.4) | collective-permute-done | bytes 196640 | tf_op jit(solution)/shard_map/ppermute | solution.py:40
  23.4 3.2 %collective-permute-done.6 = bf16[2,2,48,512]{3,2,1,0:T(8,128)(2,1)S(1)} collective-permute-done((bf16[2,2,48,512]{3,2,1,0:T(8,128)(2,1)S(1)}, bf16[2,2,48,512]{3,2,1,0:T(8,128)(2,1)S(1)}, u32[]{:S(2)}, u32[]{:S(2)}) %collective-permute-start.6) | collective-permute-done | bytes 196640 | tf_op jit(solution)/shard_map/ppermute | solution.py:40
  27.5 3.1 %collective-permute-start.12 = (bf16[1,4,48,512]{3,2,1,0:T(8,128)(2,1)S(1)}, bf16[1,4,48,512]{3,2,1,0:T(8,128)(2,1)S(1)}, u32[]{:S(2)}, u32[]{:S(2)}) collective-permute-start(bf16[1,4,48,512]{3,2,1,0:T(8,128)(2,1)S(1)} %bitcast.222), channel_id=1, source_target_pairs={{0,8},{4,12},{8,0},{12,4},{1,9},{5,13},{9,1},{13,5},{2,10},{6,14},... | collective-permute-start | bytes 589832 | tf_op jit(solution)/shard_map/ppermute | solution.py:40
  31.5 2.9 %fusion.20 = bf16[192,3584]{1,0:T(8,128)(2,1)S(1)} fusion(f32[192,3584]{1,0:T(8,128)S(1)} %fusion.53, bf16[512,3584]{1,0:T(8,128)(2,1)} %collective-permute-done.8, bf16[384,512]{1,0:T(8,128)(2,1)S(1)} %collective-permute-done.7), kind=kOutput, calls=%fused_computation.26 | convolution fusion | flops 706019328 | bytes 7995392 | tf_op jit(solution)/shard_map/dot_general | solution.py:10
  37.8 2.9 %fusion.65 = f32[192,3584]{1,0:T(8,128)S(1)} fusion(bf16[512,3584]{1,0:T(8,128)(2,1)} %collective-permute-done.9, bf16[384,512]{1,0:T(8,128)(2,1)S(1)} %collective-permute-done.7), kind=kOutput, calls=%fused_computation.147 | convolution fusion | flops 704643072 | bytes 6619136 | tf_op jit(solution)/shard_map/dot_general | solution.py:10
  42.9 10.0 %collective-permute-done.14 = bf16[96,3584]{1,0:T(8,128)(2,1)S(1)} collective-permute-done((bf16[96,3584]{1,0:T(8,128)(2,1)S(1)}, bf16[96,3584]{1,0:T(8,128)(2,1)S(1)}, u32[]{:S(2)}, u32[]{:S(2)}) %collective-permute-start.14) | collective-permute-done | bytes 688160 | tf_op jit(solution)/shard_map/ppermute | solution.py:40
  54.6 2.1 collective-permute-start.15
  56.7 2.9 %fusion.62 = f32[192,3584]{1,0:T(8,128)S(1)} fusion(bf16[512,3584]{1,0:T(8,128)(2,1)} %collective-permute-done.8, bf16[384,512]{1,0:T(8,128)(2,1)S(1)} %collective-permute-done.7), kind=kOutput, calls=%fused_computation.144 | convolution fusion | flops 704643072 | bytes 6619136 | tf_op jit(solution)/shard_map/dot_general | solution.py:10
  64.4 3.2 %convolution_add_fusion.1 = f32[192,3584]{1,0:T(8,128)S(1)} fusion(f32[192,3584]{1,0:T(8,128)S(1)} %fusion.58, bf16[512,3584]{1,0:T(8,128)(2,1)} %collective-permute-done.9, bf16[384,512]{1,0:T(8,128)(2,1)S(1)} %collective-permute-done.7), kind=kOutput, calls=%fused_computation.21 | convolution fusion | flops 705331200 | bytes 9371648 | tf_op jit(solution)/shard_map/dot_general | solution.py:10
  79.9 3.4 %collective-permute-done.23 = bf16[48,3584]{1,0:T(8,128)(2,1)S(1)} collective-permute-done((bf16[48,3584]{1,0:T(8,128)(2,1)S(1)}, bf16[48,3584]{1,0:T(8,128)(2,1)S(1)}, u32[]{:S(2)}, u32[]{:S(2)}) %collective-permute-start.23) | collective-permute-done | bytes 344096 | tf_op jit(solution)/shard_map/ppermute | solution.py:40
  83.3 3.9 %collective-permute-done.21 = bf16[48,3584]{1,0:T(8,128)(2,1)S(1)} collective-permute-done((bf16[48,3584]{1,0:T(8,128)(2,1)S(1)}, bf16[48,3584]{1,0:T(8,128)(2,1)S(1)}, u32[]{:S(2)}, u32[]{:S(2)}) %collective-permute-start.21) | collective-permute-done | bytes 344096 | tf_op jit(solution)/shard_map/ppermute | solution.py:40
  90.2 11.9 %collective-permute-done.19 = bf16[96,3584]{1,0:T(8,128)(2,1)S(1)} collective-permute-done((bf16[96,3584]{1,0:T(8,128)(2,1)S(1)}, bf16[96,3584]{1,0:T(8,128)(2,1)S(1)}, u32[]{:S(2)}, u32[]{:S(2)}) %collective-permute-start.19) | collective-permute-done | bytes 688160 | tf_op jit(solution)/shard_map/ppermute | solution.py:40
  105.0 4.4 %collective-permute-done.25 = bf16[48,3584]{1,0:T(8,128)(2,1)S(1)} collective-permute-done((bf16[48,3584]{1,0:T(8,128)(2,1)S(1)}, bf16[48,3584]{1,0:T(8,128)(2,1)S(1)}, u32[]{:S(2)}, u32[]{:S(2)}) %collective-permute-start.25) | collective-permute-done | bytes 344096 | tf_op jit(solution)/shard_map/ppermute | solution.py:40
  112.1 4.7 %collective-permute-done.24 = bf16[48,3584]{1,0:T(8,128)(2,1)S(1)} collective-permute-done((bf16[48,3584]{1,0:T(8,128)(2,1)S(1)}, bf16[48,3584]{1,0:T(8,128)(2,1)S(1)}, u32[]{:S(2)}, u32[]{:S(2)}) %collective-permute-start.24) | collective-permute-done | bytes 344096 | tf_op jit(solution)/shard_map/ppermute | solution.py:40
  126.8 4.7 %collective-permute-done.28 = bf16[96,3584]{1,0:T(8,128)(2,1)S(1)} collective-permute-done((bf16[96,3584]{1,0:T(8,128)(2,1)S(1)}, bf16[96,3584]{1,0:T(8,128)(2,1)S(1)}, u32[]{:S(2)}, u32[]{:S(2)}) %collective-permute-start.28) | collective-permute-done | bytes 688160 | tf_op jit(solution)/shard_map/ppermute | solution.py:40
  131.5 14.3 %collective-permute-done.29 = bf16[96,3584]{1,0:T(8,128)(2,1)S(1)} collective-permute-done((bf16[96,3584]{1,0:T(8,128)(2,1)S(1)}, bf16[96,3584]{1,0:T(8,128)(2,1)S(1)}, u32[]{:S(2)}, u32[]{:S(2)}) %collective-permute-start.29) | collective-permute-done | bytes 688160 | tf_op jit(solution)/shard_map/ppermute | solution.py:40
  153.3 1.8 collective-permute-start.37
  157.1 5.1 %fusion.16 = f32[3584,512]{1,0:T(8,128)} fusion(bf16[384,3584]{1,0:T(8,128)(2,1)S(1)} %copy-done.6, bf16[384,3584]{1,0:T(8,128)(2,1)S(1)} %constant_dynamic-update-slice_fusion.32, bf16[384,512]{1,0:T(8,128)(2,1)S(1)} %get-tuple-element.106, bf16[384,512]{1,0:T(8,128)(2,1)S(1)} %get-tuple-element.105), kind=kOutput, calls=%fused_computation.16 | convolution fusion | flops 2831155200 | bytes 13631488 | tf_op jit(solution)/shard_map/dot_general | solution.py:14
  162.2 5.8 %collective-permute-done.39 = bf16[5,48,512]{2,1,0:T(8,128)(2,1)S(1)} collective-permute-done((bf16[5,48,512]{2,1,0:T(8,128)(2,1)S(1)}, bf16[5,48,512]{2,1,0:T(8,128)(2,1)S(1)}, u32[]{:S(2)}, u32[]{:S(2)}) %collective-permute-start.39) | collective-permute-done | bytes 245792 | tf_op jit(solution)/shard_map/ppermute | solution.py:40
  168.0 10.4 %collective-permute-done.38 = bf16[5,48,512]{2,1,0:T(8,128)(2,1)S(1)} collective-permute-done((bf16[5,48,512]{2,1,0:T(8,128)(2,1)S(1)}, bf16[5,48,512]{2,1,0:T(8,128)(2,1)S(1)}, u32[]{:S(2)}, u32[]{:S(2)}) %collective-permute-start.38) | collective-permute-done | bytes 245792 | tf_op jit(solution)/shard_map/ppermute | solution.py:40
  183.0 1.8 collective-permute-done.40
  188.2 1.8 collective-permute-start.41
  190.0 5.2 %fusion = f32[512,3584]{1,0:T(8,128)} fusion(bf16[512,768]{0,1:T(8,128)(2,1)S(1)} %maximum_bitcast_fusion, bf16[288,3584]{1,0:T(8,128)(2,1)S(1)} %bitcast.221, bf16[96,3584]{1,0:T(8,128)(2,1)S(1)} %bitcast.213, bf16[288,3584]{1,0:T(8,128)(2,1)S(1)} %bitcast.219, bf16[96,3584]{1,0:T(8,128)(2,1)S(1)} %bitcast.211), kind=kOutput, calls=%fused_computation | convolution fusion | flops 2840592384 | bytes 13631488 | tf_op jit(solution)/shard_map/dot_general | solution.py:10
  195.2 2.1 collective-permute-done.41
  198.6 5.1 %fusion.8 = f32[512,3584]{1,0:T(8,128)} fusion(bf16[512,768]{0,1:T(8,128)(2,1)S(1)} %maximum_bitcast_fusion, bf16[288,3584]{1,0:T(8,128)(2,1)S(1)} %bitcast.217, bf16[96,3584]{1,0:T(8,128)(2,1)S(1)} %bitcast.209, bf16[288,3584]{1,0:T(8,128)(2,1)S(1)} %bitcast.215, bf16[96,3584]{1,0:T(8,128)(2,1)S(1)} %bitcast.207), kind=kOutput, calls=%fused_computation.8 | convolution fusion | flops 2840592384 | bytes 13631488 | tf_op jit(solution)/shard_map/dot_general | solution.py:10
  203.7 2.9 %collective-permute-done.42 = bf16[1,3,48,512]{3,2,1,0:T(8,128)(2,1)S(1)} collective-permute-done((bf16[1,3,48,512]{3,2,1,0:T(8,128)(2,1)S(1)}, bf16[1,3,48,512]{3,2,1,0:T(8,128)(2,1)S(1)}, u32[]{:S(2)}, u32[]{:S(2)}) %collective-permute-start.42) | collective-permute-done | bytes 147488 | tf_op jit(solution)/shard_map/ppermute | solution.py:40
  210.5 1.7 collective-permute-done.43
  (205 shorter events, 77.2 us)
Async XLA Ops:
  6.2 25.3 %collective-permute-start.8 = (bf16[512,3584]{1,0:T(8,128)(2,1)}, bf16[512,3584]{1,0:T(8,128)(2,1)}, u32[]{:S(2)}, u32[]{:S(2)}) collective-permute-start(bf16[512,3584]{1,0:T(8,128)(2,1)} %param.7), channel_id=1, source_target_pairs={{0,16},{16,0},{1,17},{17,1},{2,18},{18,2},{3,19},{19,3},{4,20},{20... | collective-permute-start | bytes 11010056 | tf_op jit(solution)/shard_map/ppermute | solution.py:40
  6.2 31.6 %collective-permute-start.9 = (bf16[512,3584]{1,0:T(8,128)(2,1)}, bf16[512,3584]{1,0:T(8,128)(2,1)}, u32[]{:S(2)}, u32[]{:S(2)}) collective-permute-start(bf16[512,3584]{1,0:T(8,128)(2,1)} %param.8), channel_id=1, source_target_pairs={{0,16},{16,0},{1,17},{17,1},{2,18},{18,2},{3,19},{19,3},{4,20},{20... | collective-permute-start | bytes 11010056 | tf_op jit(solution)/shard_map/ppermute | solution.py:40
  7.8 8.8 %collective-permute-start.3 = (bf16[1,2,48,512]{3,2,1,0:T(8,128)(2,1)S(1)}, bf16[1,2,48,512]{3,2,1,0:T(8,128)(2,1)S(1)}, u32[]{:S(2)}, u32[]{:S(2)}) collective-permute-start(bf16[1,2,48,512]{3,2,1,0:T(8,128)(2,1)S(1)} %get-tuple-element.176), channel_id=1, source_target_pairs={{0,8},{4,12},{8,0},{12,4},{1,9},{5,13},{9,1},{13,5},{2,10},{6,14},... | collective-permute-start | bytes 294920 | tf_op jit(solution)/shard_map/ppermute | solution.py:40
  11.7 7.6 %collective-permute-start.5 = (bf16[1,2,48,512]{3,2,1,0:T(8,128)(2,1)S(1)}, bf16[1,2,48,512]{3,2,1,0:T(8,128)(2,1)S(1)}, u32[]{:S(2)}, u32[]{:S(2)}) collective-permute-start(bf16[1,2,48,512]{3,2,1,0:T(8,128)(2,1)S(1)} %maximum_bitcast_fusion.1), channel_id=1, source_target_pairs={{0,8},{4,12},{8,0},{12,4},{1,9},{5,13},{9,1},{13,5},{2,10},{6,14},... | collective-permute-start | bytes 294920 | tf_op jit(solution)/shard_map/ppermute | solution.py:40
  27.0 42.0 %collective-permute-start.17 = (bf16[3584,512]{1,0:T(8,128)(2,1)}, bf16[3584,512]{1,0:T(8,128)(2,1)S(1)}, u32[]{:S(2)}, u32[]{:S(2)}) collective-permute-start(bf16[3584,512]{1,0:T(8,128)(2,1)} %param.9), channel_id=1, source_target_pairs={{0,16},{16,0},{1,17},{17,1},{2,18},{18,2},{3,19},{19,3},{4,20},{20... | collective-permute-start | bytes 11010056 | tf_op jit(solution)/shard_map/ppermute | solution.py:40
  27.5 14.9 %collective-permute-start.12 = (bf16[1,4,48,512]{3,2,1,0:T(8,128)(2,1)S(1)}, bf16[1,4,48,512]{3,2,1,0:T(8,128)(2,1)S(1)}, u32[]{:S(2)}, u32[]{:S(2)}) collective-permute-start(bf16[1,4,48,512]{3,2,1,0:T(8,128)(2,1)S(1)} %bitcast.222), channel_id=1, source_target_pairs={{0,8},{4,12},{8,0},{12,4},{1,9},{5,13},{9,1},{13,5},{2,10},{6,14},... | collective-permute-start | bytes 589832 | tf_op jit(solution)/shard_map/ppermute | solution.py:40
  34.6 18.4 %collective-permute-start.14 = (bf16[96,3584]{1,0:T(8,128)(2,1)S(1)}, bf16[96,3584]{1,0:T(8,128)(2,1)S(1)}, u32[]{:S(2)}, u32[]{:S(2)}) collective-permute-start(bf16[96,3584]{1,0:T(8,128)(2,1)S(1)} %get-tuple-element.133), channel_id=1, source_target_pairs={{0,2},{1,3},{2,0},{3,1},{4,6},{5,7},{6,4},{7,5},{8,10},{9,11},{10,... | collective-permute-start | bytes 2064392 | tf_op jit(solution)/shard_map/ppermute | solution.py:40
  36.2 18.4 %collective-permute-start.13 = (bf16[96,3584]{1,0:T(8,128)(2,1)S(1)}, bf16[96,3584]{1,0:T(8,128)(2,1)S(1)}, u32[]{:S(2)}, u32[]{:S(2)}) collective-permute-start(bf16[96,3584]{1,0:T(8,128)(2,1)S(1)} %get-tuple-element.134), channel_id=1, source_target_pairs={{0,1},{1,0},{2,3},{3,2},{4,5},{5,4},{6,7},{7,6},{8,9},{9,8},{10,11... | collective-permute-start | bytes 2064392 | tf_op jit(solution)/shard_map/ppermute | solution.py:40
  41.8 29.4 %collective-permute-start.11 = (bf16[96,3584]{1,0:T(8,128)(2,1)S(1)}, bf16[96,3584]{1,0:T(8,128)(2,1)S(1)}, u32[]{:S(2)}, u32[]{:S(2)}) collective-permute-start(bf16[96,3584]{1,0:T(8,128)(2,1)S(1)} %get-tuple-element.131), channel_id=1, source_target_pairs={{0,2},{1,3},{2,0},{3,1},{4,6},{5,7},{6,4},{7,5},{8,10},{9,11},{10,... | collective-permute-start | bytes 2064392 | tf_op jit(solution)/shard_map/ppermute | solution.py:40
  42.4 28.8 %collective-permute-start.10 = (bf16[96,3584]{1,0:T(8,128)(2,1)S(1)}, bf16[96,3584]{1,0:T(8,128)(2,1)S(1)}, u32[]{:S(2)}, u32[]{:S(2)}) collective-permute-start(bf16[96,3584]{1,0:T(8,128)(2,1)S(1)} %get-tuple-element.132), channel_id=1, source_target_pairs={{0,1},{1,0},{2,3},{3,2},{4,5},{5,4},{6,7},{7,6},{8,9},{9,8},{10,11... | collective-permute-start | bytes 2064392 | tf_op jit(solution)/shard_map/ppermute | solution.py:40
  54.6 8.5 %collective-permute-start.15 = (bf16[2,4,48,512]{3,2,1,0:T(8,128)(2,1)S(1)}, bf16[2,4,48,512]{3,2,1,0:T(8,128)(2,1)S(1)}, u32[]{:S(2)}, u32[]{:S(2)}) collective-permute-start(bf16[2,4,48,512]{3,2,1,0:T(8,128)(2,1)S(1)} %pad_maximum_fusion.14), channel_id=1, source_target_pairs={{0,4},{4,0},{8,12},{12,8},{1,5},{5,1},{9,13},{13,9},{2,6},{6,2},{1... | collective-permute-start | bytes 1179656 | tf_op jit(solution)/shard_map/ppermute | solution.py:40
  60.7 17.0 %collective-permute-start.22 = (bf16[48,3584]{1,0:T(8,128)(2,1)S(1)}, bf16[48,3584]{1,0:T(8,128)(2,1)S(1)}, u32[]{:S(2)}, u32[]{:S(2)}) collective-permute-start(bf16[48,3584]{1,0:T(8,128)(2,1)S(1)} %get-tuple-element.121), channel_id=1, source_target_pairs={{0,1},{1,0},{2,3},{3,2},{4,5},{5,4},{6,7},{7,6},{8,9},{9,8},{10,11... | collective-permute-start | bytes 1032200 | tf_op jit(solution)/shard_map/ppermute | solution.py:40
  69.0 10.9 %collective-permute-start.20 = (bf16[48,3584]{1,0:T(8,128)(2,1)S(1)}, bf16[48,3584]{1,0:T(8,128)(2,1)S(1)}, u32[]{:S(2)}, u32[]{:S(2)}) collective-permute-start(bf16[48,3584]{1,0:T(8,128)(2,1)S(1)} %get-tuple-element.122), channel_id=1, source_target_pairs={{0,2},{1,3},{2,0},{3,1},{4,6},{5,7},{6,4},{7,5},{8,10},{9,11},{10,... | collective-permute-start | bytes 1032200 | tf_op jit(solution)/shard_map/ppermute | solution.py:40
  71.3 12.0 %collective-permute-start.23 = (bf16[48,3584]{1,0:T(8,128)(2,1)S(1)}, bf16[48,3584]{1,0:T(8,128)(2,1)S(1)}, u32[]{:S(2)}, u32[]{:S(2)}) collective-permute-start(bf16[48,3584]{1,0:T(8,128)(2,1)S(1)} %get-tuple-element.119), channel_id=1, source_target_pairs={{0,1},{1,0},{2,3},{3,2},{4,5},{5,4},{6,7},{7,6},{8,9},{9,8},{10,11... | collective-permute-start | bytes 1032200 | tf_op jit(solution)/shard_map/ppermute | solution.py:40
  72.9 14.3 %collective-permute-start.21 = (bf16[48,3584]{1,0:T(8,128)(2,1)S(1)}, bf16[48,3584]{1,0:T(8,128)(2,1)S(1)}, u32[]{:S(2)}, u32[]{:S(2)}) collective-permute-start(bf16[48,3584]{1,0:T(8,128)(2,1)S(1)} %get-tuple-element.120), channel_id=1, source_target_pairs={{0,2},{1,3},{2,0},{3,1},{4,6},{5,7},{6,4},{7,5},{8,10},{9,11},{10,... | collective-permute-start | bytes 1032200 | tf_op jit(solution)/shard_map/ppermute | solution.py:40
  74.3 27.7 %collective-permute-start.19 = (bf16[96,3584]{1,0:T(8,128)(2,1)S(1)}, bf16[96,3584]{1,0:T(8,128)(2,1)S(1)}, u32[]{:S(2)}, u32[]{:S(2)}) collective-permute-start(bf16[96,3584]{1,0:T(8,128)(2,1)S(1)} %get-tuple-element.129), channel_id=1, source_target_pairs={{0,2},{1,3},{2,0},{3,1},{4,6},{5,7},{6,4},{7,5},{8,10},{9,11},{10,... | collective-permute-start | bytes 2064392 | tf_op jit(solution)/shard_map/ppermute | solution.py:40
  77.7 24.3 %collective-permute-start.18 = (bf16[96,3584]{1,0:T(8,128)(2,1)S(1)}, bf16[96,3584]{1,0:T(8,128)(2,1)S(1)}, u32[]{:S(2)}, u32[]{:S(2)}) collective-permute-start(bf16[96,3584]{1,0:T(8,128)(2,1)S(1)} %get-tuple-element.130), channel_id=1, source_target_pairs={{0,1},{1,0},{2,3},{3,2},{4,5},{5,4},{6,7},{7,6},{8,9},{9,8},{10,11... | collective-permute-start | bytes 2064392 | tf_op jit(solution)/shard_map/ppermute | solution.py:40
  88.0 17.0 %collective-permute-start.26 = (bf16[48,3584]{1,0:T(8,128)(2,1)S(1)}, bf16[48,3584]{1,0:T(8,128)(2,1)S(1)}, u32[]{:S(2)}, u32[]{:S(2)}) collective-permute-start(bf16[48,3584]{1,0:T(8,128)(2,1)S(1)} %get-tuple-element.83), channel_id=1, source_target_pairs={{0,1},{1,0},{2,3},{3,2},{4,5},{5,4},{6,7},{7,6},{8,9},{9,8},{10,11... | collective-permute-start | bytes 1032200 | tf_op jit(solution)/shard_map/ppermute | solution.py:40
  89.6 19.8 %collective-permute-start.25 = (bf16[48,3584]{1,0:T(8,128)(2,1)S(1)}, bf16[48,3584]{1,0:T(8,128)(2,1)S(1)}, u32[]{:S(2)}, u32[]{:S(2)}) collective-permute-start(bf16[48,3584]{1,0:T(8,128)(2,1)S(1)} %get-tuple-element.80), channel_id=1, source_target_pairs={{0,2},{1,3},{2,0},{3,1},{4,6},{5,7},{6,4},{7,5},{8,10},{9,11},{10,... | collective-permute-start | bytes 1032200 | tf_op jit(solution)/shard_map/ppermute | solution.py:40
  102.2 9.9 %collective-permute-start.30 = (bf16[48,3584]{1,0:T(8,128)(2,1)S(1)}, bf16[48,3584]{1,0:T(8,128)(2,1)S(1)}, u32[]{:S(2)}, u32[]{:S(2)}) collective-permute-start(bf16[48,3584]{1,0:T(8,128)(2,1)S(1)} %get-tuple-element.117), channel_id=1, source_target_pairs={{0,1},{1,0},{2,3},{3,2},{4,5},{5,4},{6,7},{7,6},{8,9},{9,8},{10,11... | collective-permute-start | bytes 1032200 | tf_op jit(solution)/shard_map/ppermute | solution.py:40
  103.8 13.0 %collective-permute-start.24 = (bf16[48,3584]{1,0:T(8,128)(2,1)S(1)}, bf16[48,3584]{1,0:T(8,128)(2,1)S(1)}, u32[]{:S(2)}, u32[]{:S(2)}) collective-permute-start(bf16[48,3584]{1,0:T(8,128)(2,1)S(1)} %get-tuple-element.118), channel_id=1, source_target_pairs={{0,2},{1,3},{2,0},{3,1},{4,6},{5,7},{6,4},{7,5},{8,10},{9,11},{10,... | collective-permute-start | bytes 1032200 | tf_op jit(solution)/shard_map/ppermute | solution.py:40
  109.6 21.9 %collective-permute-start.28 = (bf16[96,3584]{1,0:T(8,128)(2,1)S(1)}, bf16[96,3584]{1,0:T(8,128)(2,1)S(1)}, u32[]{:S(2)}, u32[]{:S(2)}) collective-permute-start(bf16[96,3584]{1,0:T(8,128)(2,1)S(1)} %pad_maximum_fusion.11), channel_id=1, source_target_pairs={{0,2},{1,3},{2,0},{3,1},{4,6},{5,7},{6,4},{7,5},{8,10},{9,11},{10,... | collective-permute-start | bytes 2064392 | tf_op jit(solution)/shard_map/ppermute | solution.py:40
  110.2 21.3 %collective-permute-start.27 = (bf16[96,3584]{1,0:T(8,128)(2,1)S(1)}, bf16[96,3584]{1,0:T(8,128)(2,1)S(1)}, u32[]{:S(2)}, u32[]{:S(2)}) collective-permute-start(bf16[96,3584]{1,0:T(8,128)(2,1)S(1)} %pad_maximum_fusion.10), channel_id=1, source_target_pairs={{0,1},{1,0},{2,3},{3,2},{4,5},{5,4},{6,7},{7,6},{8,9},{9,8},{10,11... | collective-permute-start | bytes 2064392 | tf_op jit(solution)/shard_map/ppermute | solution.py:40
  118.9 27.0 %collective-permute-start.29 = (bf16[96,3584]{1,0:T(8,128)(2,1)S(1)}, bf16[96,3584]{1,0:T(8,128)(2,1)S(1)}, u32[]{:S(2)}, u32[]{:S(2)}) collective-permute-start(bf16[96,3584]{1,0:T(8,128)(2,1)S(1)} %pad_maximum_fusion.12), channel_id=1, source_target_pairs={{0,2},{1,3},{2,0},{3,1},{4,6},{5,7},{6,4},{7,5},{8,10},{9,11},{10,... | collective-permute-start | bytes 2064392 | tf_op jit(solution)/shard_map/ppermute | solution.py:40
  119.6 26.3 %collective-permute-start.31 = (bf16[96,3584]{1,0:T(8,128)(2,1)S(1)}, bf16[96,3584]{1,0:T(8,128)(2,1)S(1)}, u32[]{:S(2)}, u32[]{:S(2)}) collective-permute-start(bf16[96,3584]{1,0:T(8,128)(2,1)S(1)} %pad_maximum_fusion.13), channel_id=1, source_target_pairs={{0,1},{1,0},{2,3},{3,2},{4,5},{5,4},{6,7},{7,6},{8,9},{9,8},{10,11... | collective-permute-start | bytes 2064392 | tf_op jit(solution)/shard_map/ppermute | solution.py:40
  147.0 32.2 %collective-permute-start.34 = (bf16[192,3584]{1,0:T(8,128)(2,1)S(1)}, bf16[192,3584]{1,0:T(8,128)(2,1)S(1)}, u32[]{:S(2)}, u32[]{:S(2)}) collective-permute-start(bf16[192,3584]{1,0:T(8,128)(2,1)S(1)} %pad_maximum_fusion.7), channel_id=1, source_target_pairs={{0,2},{1,3},{2,0},{3,1},{4,6},{5,7},{6,4},{7,5},{8,10},{9,11},{10,... | collective-permute-start | bytes 4128776 | tf_op jit(solution)/shard_map/ppermute | solution.py:40
  147.7 31.8 %collective-permute-start.33 = (bf16[192,3584]{1,0:T(8,128)(2,1)S(1)}, bf16[192,3584]{1,0:T(8,128)(2,1)S(1)}, u32[]{:S(2)}, u32[]{:S(2)}) collective-permute-start(bf16[192,3584]{1,0:T(8,128)(2,1)S(1)} %pad_maximum_fusion.5), channel_id=1, source_target_pairs={{0,1},{1,0},{2,3},{3,2},{4,5},{5,4},{6,7},{7,6},{8,9},{9,8},{10,11... | collective-permute-start | bytes 4128776 | tf_op jit(solution)/shard_map/ppermute | solution.py:40
  153.3 8.9 %collective-permute-start.37 = (bf16[5,48,512]{2,1,0:T(8,128)(2,1)S(1)}, bf16[5,48,512]{2,1,0:T(8,128)(2,1)S(1)}, u32[]{:S(2)}, u32[]{:S(2)}) collective-permute-start(bf16[5,48,512]{2,1,0:T(8,128)(2,1)S(1)} %get-tuple-element.142), channel_id=1, source_target_pairs={{0,4},{4,0},{8,12},{12,8},{1,5},{5,1},{9,13},{13,9},{2,6},{6,2},{1... | collective-permute-start | bytes 737288 | tf_op jit(solution)/shard_map/ppermute | solution.py:40
  155.1 12.9 %collective-permute-start.39 = (bf16[5,48,512]{2,1,0:T(8,128)(2,1)S(1)}, bf16[5,48,512]{2,1,0:T(8,128)(2,1)S(1)}, u32[]{:S(2)}, u32[]{:S(2)}) collective-permute-start(bf16[5,48,512]{2,1,0:T(8,128)(2,1)S(1)} %get-tuple-element.143), channel_id=1, source_target_pairs={{0,12},{4,8},{8,4},{12,0},{1,13},{5,9},{9,5},{13,1},{2,14},{6,10},... | collective-permute-start | bytes 737288 | tf_op jit(solution)/shard_map/ppermute | solution.py:40
  156.0 22.4 %collective-permute-start.38 = (bf16[5,48,512]{2,1,0:T(8,128)(2,1)S(1)}, bf16[5,48,512]{2,1,0:T(8,128)(2,1)S(1)}, u32[]{:S(2)}, u32[]{:S(2)}) collective-permute-start(bf16[5,48,512]{2,1,0:T(8,128)(2,1)S(1)} %fusion.49), channel_id=1, source_target_pairs={{0,8},{4,12},{8,0},{12,4},{1,9},{5,13},{9,1},{13,5},{2,10},{6,14},... | collective-permute-start | bytes 737288 | tf_op jit(solution)/shard_map/ppermute | solution.py:40
  188.2 9.1 %collective-permute-start.41 = (bf16[2,3,48,512]{3,2,1,0:T(8,128)(2,1)S(1)}, bf16[2,3,48,512]{3,2,1,0:T(8,128)(2,1)S(1)}, u32[]{:S(2)}, u32[]{:S(2)}) collective-permute-start(bf16[2,3,48,512]{3,2,1,0:T(8,128)(2,1)S(1)} %pad_maximum_fusion.16), channel_id=1, source_target_pairs={{0,4},{4,0},{8,12},{12,8},{1,5},{5,1},{9,13},{13,9},{2,6},{6,2},{1... | collective-permute-start | bytes 884744 | tf_op jit(solution)/shard_map/ppermute | solution.py:40
  197.5 9.2 %collective-permute-start.42 = (bf16[1,3,48,512]{3,2,1,0:T(8,128)(2,1)S(1)}, bf16[1,3,48,512]{3,2,1,0:T(8,128)(2,1)S(1)}, u32[]{:S(2)}, u32[]{:S(2)}) collective-permute-start(bf16[1,3,48,512]{3,2,1,0:T(8,128)(2,1)S(1)} %dynamic-slice_convert_fusion.3), channel_id=1, source_target_pairs={{0,8},{4,12},{8,0},{12,4},{1,9},{5,13},{9,1},{13,5},{2,10},{6,14},... | collective-permute-start | bytes 442376 | tf_op jit(solution)/shard_map/ppermute | solution.py:40
  (21 other events, 141.9 us)
